TPU v7x, 256 devices: a whole 4x4x8 slice. The times are simulated.
256 devices in a mesh: aa: 8 (over x, core), ba: 32 (over z, y).
Axes of the slice: x: 4, y: 4, z: 8, core: 2. Of those that a mesh axis runs over, the one named last changes fastest.
Arguments:
- spec_in: bfloat16 [640, 2, 3, 32, 1288], P('aa', None, None, 'ba'), may hold values from -0.23925781 to 0.23925781
- legendre: bfloat16 [640, 32, 1288], P('aa'), may hold values from -0.15625 to 0.15625
- pair_wave: int32 [640], replicated, may hold values from 0 to 639, each once
- quad_weight: float32 [32], replicated, may hold values from 1 to 3
- forcing: bfloat16 [64, 3, 32, 5248], P('aa', None, None, 'ba'), may hold values from -6 to 6
Outputs:
- grid: bfloat16 [64, 3, 32, 5248], P('aa', None, None, 'ba')
- spec_out: bfloat16 [640, 2, 3, 32, 1288], P('aa', None, None, 'ba')
Inputs may be any that keep to these rules, and one draw needn't show every extreme that they name: Each value appears once; pair p holds the zonal wavenumbers pair_wave[p] and 1279 - pair_wave[p].
All inputs are finite; a program needn't handle non-finite values.
Results may differ from a plain program's by a relative error of at most 0.012.
Values may be sent and summed in bfloat16 or wider, within the bound.
No kernel may reach another device: no remote copies, remote signals or barrier semaphores. Data moves between devices by JAX's collectives and lax.ppermute only.
A program may use at most 128 MiB of HBM per device.

v0:
```python
import math

import jax
import jax.numpy as jnp
from jax import lax
from jax.sharding import PartitionSpec as P

TRUNCATION = 1279
FIELDS = 3


def slot_masks(first_waves, slot_count):
    slots = jnp.arange(slot_count, dtype=jnp.int32)[None, :]
    limit = TRUNCATION - first_waves[:, None]
    own_first = (slots <= limit).astype(jnp.float32)
    own_second = ((slots > limit) & (slots <= TRUNCATION + 1)).astype(jnp.float32)
    sign_first = (1 - 2 * (slots % 2)).astype(jnp.float32)
    sign_second = (1 - 2 * ((slots - 1 - limit) % 2)).astype(jnp.float32)
    north = jnp.stack([own_first, own_second], axis=1)
    south = jnp.stack([own_first * sign_first, own_second * sign_second], axis=1)
    return jnp.stack([north, south], axis=1)


def phase_tables(lengths, wavenumbers, blocks):
    inner_index = jnp.arange(128, dtype=jnp.int32)
    block_starts = jnp.arange(blocks, dtype=jnp.int32) * 128
    modulus = lengths[:, None, None]
    inner_turn = wavenumbers[None, :, None] * inner_index[None, None, :] % modulus
    outer_turn = block_starts[None, :, None] * wavenumbers[None, None, :] % modulus
    angle_scale = 2.0 * math.pi / lengths.astype(jnp.float32)
    inner_angle = inner_turn.astype(jnp.float32) * angle_scale[:, None, None]
    outer_angle = outer_turn.astype(jnp.float32) * angle_scale[:, None, None]
    return (jnp.cos(inner_angle), jnp.sin(inner_angle), jnp.cos(outer_angle), jnp.sin(outer_angle))


def split_table(table):
    table_high = table.astype(jnp.bfloat16)
    table_low = (table - table_high.astype(jnp.float32)).astype(jnp.bfloat16)
    return (table_high, table_low)


def table_product(samples, table):
    table_high, table_low = split_table(table)
    first = jnp.einsum("thcjb,tkb->thcjk", samples, table_high, preferred_element_type=jnp.float32)
    second = jnp.einsum("thcjb,tkb->thcjk", samples, table_low, preferred_element_type=jnp.float32)
    return first + second


def inverse_rows(fourier, lengths, wavenumbers, lon_pad):
    lat_rows = fourier.shape[0]
    column_count = fourier.shape[3]
    blocks = lon_pad // 128
    inner_cos, inner_sin, outer_cos, outer_sin = phase_tables(lengths, wavenumbers, blocks)
    doubling = jnp.where(wavenumbers == 0, 1.0, 2.0).astype(jnp.float32)
    values = fourier.astype(jnp.float32).reshape(lat_rows, 2, 2, column_count, -1) * doubling
    real_part = values[:, :, 0][:, :, :, None, :]
    imag_part = values[:, :, 1][:, :, :, None, :]
    turn_cos = outer_cos[:, None, None]
    turn_sin = outer_sin[:, None, None]
    turned_real = real_part * turn_cos - imag_part * turn_sin
    turned_imag = real_part * turn_sin + imag_part * turn_cos
    careful = lax.Precision.HIGH
    grid_rows = jnp.einsum(
        "thcjk,tkb->thcjb", turned_real, inner_cos, precision=careful
    ) - jnp.einsum("thcjk,tkb->thcjb", turned_imag, inner_sin, precision=careful)
    grid_rows = grid_rows.reshape(lat_rows, 2, column_count, lon_pad)
    inside = jnp.arange(lon_pad, dtype=jnp.int32)[None, :] < lengths[:, None]
    return jnp.where(inside[:, None, None, :], grid_rows, 0.0).astype(jnp.bfloat16)


def direct_rows(tendency, lengths, weights_here, wavenumbers):
    lat_rows = tendency.shape[0]
    column_count = tendency.shape[2]
    lon_pad = tendency.shape[3]
    blocks = lon_pad // 128
    inner_cos, inner_sin, outer_cos, outer_sin = phase_tables(lengths, wavenumbers, blocks)
    inside = jnp.arange(lon_pad, dtype=jnp.int32)[None, :] < lengths[:, None]
    samples = jnp.where(inside[:, None, None, :], tendency, jnp.zeros((), jnp.bfloat16))
    samples = samples.reshape(lat_rows, 2, column_count, blocks, 128)
    part_cos = table_product(samples, inner_cos)
    part_sin = table_product(samples, inner_sin)
    turn_cos = outer_cos[:, None, None]
    turn_sin = outer_sin[:, None, None]
    real_sum = jnp.sum(part_cos * turn_cos - part_sin * turn_sin, axis=3)
    imag_sum = -jnp.sum(part_sin * turn_cos + part_cos * turn_sin, axis=3)
    factor = weights_here / jnp.sqrt(lengths.astype(jnp.float32))
    stacked = jnp.stack([real_sum, imag_sum], axis=2) * factor[:, None, None, None, None]
    return stacked.reshape(lat_rows, 2, 2, column_count, -1, 2).astype(jnp.bfloat16)


def per_device(spec_in, legendre, pair_wave, quad_weight, forcing):
    pairs_here = legendre.shape[0]
    kept_total = legendre.shape[1]
    slot_count = legendre.shape[2]
    level_group = spec_in.shape[3]
    lat_group = kept_total // lax.axis_size("aa")
    lon_pad = forcing.shape[3] * lax.axis_size("ba")
    column_total = FIELDS * level_group
    group = lax.axis_index("aa")
    first_waves = lax.dynamic_slice_in_dim(pair_wave, group * pairs_here, pairs_here)
    masking = slot_masks(first_waves, slot_count)
    spec_flat = spec_in.reshape(pairs_here, 2 * column_total, slot_count)
    masked = masking.astype(jnp.bfloat16)[:, :, :, None, :] * spec_flat[:, None, None, :, :]
    fourier = jnp.einsum("pts,phwcs->thcpw", legendre, masked, preferred_element_type=jnp.float32)
    fourier = fourier.reshape(kept_total, 2, 2, column_total, pairs_here, 2).astype(jnp.bfloat16)
    wavenumbers = jnp.stack([pair_wave, TRUNCATION - pair_wave], axis=1).reshape(-1)
    north_index = (
        TRUNCATION + 1 - kept_total + group * lat_group + jnp.arange(lat_group, dtype=jnp.int32)
    )
    lengths = 20 + 4 * north_index
    grid_parts = inverse_rows(
        lax.all_to_all(fourier, "aa", split_axis=0, concat_axis=4, tiled=True),
        lengths,
        wavenumbers,
        lon_pad,
    )
    grid_lat = grid_parts.reshape(2 * lat_group, FIELDS, level_group, lon_pad)
    grid = lax.all_to_all(grid_lat, "ba", split_axis=3, concat_axis=2, tiled=True)
    grid_wide = grid.astype(jnp.float32)
    tend_columns = (
        grid_wide * jnp.roll(grid_wide, -1, axis=1) + forcing.astype(jnp.float32)
    ).astype(jnp.bfloat16)
    tend_lat = lax.all_to_all(tend_columns, "ba", split_axis=2, concat_axis=3, tiled=True)
    tend_rows = tend_lat.reshape(lat_group, 2, column_total, lon_pad)
    weights_here = lax.dynamic_slice_in_dim(quad_weight, group * lat_group, lat_group)
    direct = direct_rows(tend_rows, lengths, weights_here, wavenumbers)
    partial_value = jnp.einsum(
        "pts,thrcpw->phwrcs",
        legendre,
        lax.all_to_all(direct, "aa", split_axis=4, concat_axis=0, tiled=True),
        preferred_element_type=jnp.float32,
    )
    spec_parts = jnp.sum(masking[:, :, :, None, None, :] * partial_value, axis=(1, 2)).astype(
        jnp.bfloat16
    )
    spec_out = spec_parts.reshape(pairs_here, 2, FIELDS, level_group, slot_count)
    return (grid, spec_out)


def solution(mesh):
    placed = (
        P("aa", None, None, "ba", None),
        P("aa", None, None),
        P(),
        P(),
        P("aa", None, None, "ba"),
    )
    return jax.shard_map(
        per_device,
        mesh=mesh,
        in_specs=placed,
        out_specs=(P("aa", None, None, "ba"), P("aa", None, None, "ba", None)),
        check_vma=False,
    )
```

profile of v0, /device:TPU:1, one launch (start us, length us, event | category | flops | bytes accessed | tf_op | source)
XLA Modules:
  0.0 434.6 jit_solution(5047695889281591804)
XLA Ops:
  11.0 8.2 %fusion.63 = bf16[32,2,6,80,2]{0,2,4,1,3:T(8,128)(2,1)} fusion(bf16[80,32,1288]{2,1,0:T(8,128)(2,1)} %param.10, bf16[80,6,1288]{2,1,0:T(8,128)(2,1)} %copy.53, bf16[80,2,2,1288]{3,2,1,0:T(2,128)(2,1)S(1)} %fusion.108), kind=kOutput, calls=%fused_computation.78 | convolution fusion | flops 160803840 | bytes 8778240 | tf_op jit(solution)/shard_map/pts,phwcs->thcpw/dot_general | solution.py:104
  21.6 7.0 %all-to-all-start = ((bf16[32,2,2,3,80,2]{4,5,3,2,1,0:T(2,128)(2,1)}), bf16[32,2,2,3,80,2]{4,5,3,2,1,0:T(2,128)(2,1)S(1)}, u32[]{:S(2)}, u32[]{:S(2)}) async-start(bf16[32,2,2,3,80,2]{4,5,3,2,1,0:T(2,128)(2,1)} %copy.55), calls=%async_computation | async-start | bytes 393216 | tf_op jit(solution)/shard_map/all_to_all | solution.py:112
  29.6 14.1 %fusion.76 = (f32[4,41,1280]{2,1,0:T(8,128)}, f32[4,41,1280]{2,1,0:T(8,128)}) fusion(s32[4]{0:T(128)S(1)} %fusion.99, s32[41,1280]{1,0:T(8,128)S(1)} %multiply_bitcast_fusion.1, f32[4]{0:T(128)S(1)} %get-tuple-element.21, pred[4]{0:T(512)(128)(4,1)S(1)} %compare_bitcast_fusion), kind=kLoop, calls=%fused_computation.83 | loop fusion | flops 1889280 | bytes 1889316 | tf_op jit(solution)/shard_map/cos | solution.py:33
  44.0 7.1 %copy.57 = f32[4,2,2,3,8,80,2]{0,6,5,4,3,2,1:T(2,128)} copy(f32[4,2,2,3,8,80,2]{5,0,4,6,3,2,1:T(4,128)S(1)} %convert_bitcast_fusion.1) | data formatting | bytes 491520 | tf_op jit(solution)/shard_map/convert_element_type | solution.py:55
  66.5 38.5 %fusion.4 = f32[4,2,3,41,128]{4,3,2,1,0:T(8,128)S(1)} fusion(f32[4,41,1280]{2,1,0:T(8,128)} %get-tuple-element.15, f32[4,2,3,1280]{3,2,1,0:T(4,128)} %copy.60, f32[4,41,1280]{2,1,0:T(8,128)S(1)} %copy-done.1, f32[4,2,3,1280]{3,2,1,0:T(4,128)} %copy.59, s32[4]{0:T(128)S(1)} %fusion.99, s32[1280,128]{1,0:T(8,128)S(1)} %multiply_bitcast_fusion, ...), kind=kOutput, calls=%fused_computation.11 | convolution fusion | flops 976988160 | bytes 3084324 | tf_op jit(solution)/shard_map/thcjk,tkb->thcjb/dot_general | solution.py:65
  105.0 37.7 %fusion.68 = bf16[4,2,3,41,128]{4,3,2,1,0:T(8,128)(2,1)} fusion(f32[4,2,3,41,128]{4,3,2,1,0:T(8,128)S(1)} %fusion.4, s32[4]{0:T(128)S(1)} %fusion.99, s32[1280,128]{1,0:T(8,128)S(1)} %multiply_bitcast_fusion, f32[4]{0:T(128)S(1)} %get-tuple-element.21, f32[4,41,1280]{2,1,0:T(8,128)S(1)} %copy-done.3, f32[4,2,3,1280]{3,2,1,0:T(4,128)S(1)} %copy-done.6, ...), kind=kOutput, calls=%fused_computation.79 | convolution fusion | flops 977240064 | bytes 3336228 | tf_op jit(solution)/shard_map/thcjk,tkb->thcjb/dot_general | solution.py:63
  143.9 5.7 %copy.62 = bf16[8,3,1,5248]{0,1,2,3:T(4,128)(2,1)} copy(bf16[8,3,1,5248]{3,0,1,2:T(8,128)(2,1)S(1)} %fusion.82) | data formatting | bytes 503808 | tf_op jit(solution)/shard_map/convert_element_type | solution.py:68
  149.6 6.8 %reshape.530 = bf16[32,2,1968]{2,1,0:T(2,128)(2,1)S(1)} reshape(bf16[5248,1,3,8]{3,2,1,0:T(4,128)(2,1)} %bitcast.96) | data formatting | bytes 503808
  156.4 22.3 %all_to_all.48 = bf16[32,2,1968]{2,1,0:T(2,128)(2,1)S(1)} all-to-all(bf16[32,2,1968]{2,1,0:T(2,128)(2,1)S(1)} %reshape.530), channel_id=1, replica_groups=mesh['aa'=8,'ba'=32] {'ba'}, dimensions={0} | all-to-all | bytes 503808 | tf_op jit(solution)/shard_map/all_to_all | solution.py:118
  178.7 6.1 %reshape.531 = bf16[5248,1,3,8]{3,2,1,0:T(4,128)(2,1)} reshape(bf16[32,2,1968]{2,1,0:T(2,128)(2,1)S(1)} %all_to_all.48) | data formatting | bytes 503808
  184.8 7.6 %copy.87 = bf16[8,3,32,164]{3,2,0,1:T(8,128)(2,1)S(1)} copy(bf16[8,3,32,164]{0,1,3,2:T(4,128)(2,1)} %bitcast.93) | data formatting | bytes 503808 | tf_op jit(solution)/shard_map/all_to_all | solution.py:118
  197.9 12.7 %all-to-all-done.2 = bf16[8,3,32,164]{3,0,1,2:T(8,128)(2,1)S(1)} async-done(((bf16[8,3,32,164]{3,0,1,2:T(8,128)(2,1)}), bf16[8,3,32,164]{3,0,1,2:T(8,128)(2,1)S(1)}, u32[]{:S(2)}, u32[]{:S(2)}) %all-to-all-start.2) | async-done | bytes 251936 | tf_op jit(solution)/shard_map/all_to_all | solution.py:123
  211.5 34.4 %fusion.49 = f32[4,2,3,41,1280]{4,3,2,1,0:T(8,128)S(1)} fusion(bf16[4,2,3,41,128]{4,3,2,1,0:T(8,128)(2,1)S(1)} %reshape.517, pred[4,41,128]{2,1,0:T(8,128)(4,1)S(1)} %broadcast_compare_fusion, s32[4]{0:T(128)S(1)} %fusion.99, s32[1280,128]{1,0:T(8,128)S(1)} %multiply_bitcast_fusion, f32[4]{0:T(128)S(1)} %get-tuple-element.21, ...), kind=kOutput, calls=%fused_computation.64 | convolution fusion | flops 329116672 | bytes 5966372 | tf_op jit(solution)/shard_map/thcjb,tkb->thcjk/dot_general | solution.py:44
  246.0 34.2 %fusion.47 = f32[4,2,3,41,1280]{4,3,2,1,0:T(8,128)S(1)} fusion(bf16[4,2,3,41,128]{4,3,2,1,0:T(8,128)(2,1)S(1)} %reshape.517, pred[4,41,128]{2,1,0:T(8,128)(4,1)S(1)} %broadcast_compare_fusion, s32[4]{0:T(128)S(1)} %fusion.99, s32[1280,128]{1,0:T(8,128)S(1)} %multiply_bitcast_fusion, f32[4]{0:T(128)S(1)} %get-tuple-element.21, ...), kind=kOutput, calls=%fused_computation.62 | convolution fusion | flops 329116672 | bytes 5966372 | tf_op jit(solution)/shard_map/thcjb,tkb->thcjk/dot_general | solution.py:44
  280.3 34.7 %convolution_add_fusion.1 = f32[4,2,3,41,1280]{4,3,2,1,0:T(8,128)S(1)} fusion(f32[4,2,3,41,1280]{4,3,2,1,0:T(8,128)S(1)} %fusion.49, s32[4]{0:T(128)S(1)} %fusion.99, s32[1280,128]{1,0:T(8,128)S(1)} %multiply_bitcast_fusion, f32[4]{0:T(128)S(1)} %get-tuple-element.21, bf16[4,2,3,41,128]{4,3,2,1,0:T(8,128)(2,1)S(1)} %reshape.517, ...), kind=kOutput, calls=%fused_computation.20 | convolution fusion | flops 332342272 | bytes 11004452 | tf_op jit(solution)/shard_map/thcjb,tkb->thcjk/dot_general | solution.py:45
  314.9 37.6 %subtract_reduce_fusion = (f32[4,2,3,1280]{3,2,1,0:T(4,128)S(1)}, f32[4,2,3,1280]{3,2,1,0:T(4,128)S(1)}) fusion(f32[4,2,3,41,1280]{4,3,2,1,0:T(8,128)S(1)} %convolution_add_fusion.1, f32[4,41,1280]{2,1,0:T(8,128)S(1)} %copy-done.4, f32[4,41,1280]{2,1,0:T(8,128)S(1)} %copy-done.2, f32[4,2,3,41,1280]{4,3,2,1,0:T(8,128)S(1)} %fusion.47, s32[4]{0:T(128)S(1)} %fusion.99, ...), kind=kOutput, calls=%fused_computation.10 | convolution fusion | flops 342356992 | bytes 12929572 | tf_op jit(solution)/shard_map/thcjb,tkb->thcjk/dot_general | solution.py:45
  355.2 4.3 copy.71
  366.5 6.4 %copy.72 = bf16[4,2,2,3,640,2]{0,5,3,1,2,4:T(2,128)(2,1)} copy(bf16[4,2,2,3,640,2]{4,0,5,3,2,1:T(4,128)(2,1)S(1)} %fusion.88) | data formatting | bytes 245760 | tf_op jit(solution)/shard_map/convert_element_type | solution.py:88
  373.0 11.7 %reshape.532 = bf16[8,2,3840]{2,1,0:T(2,128)(2,1)} reshape(bf16[640,2,2,3,2,4]{5,4,3,2,1,0:T(2,128)(2,1)} %bitcast.99) | data formatting | bytes 245760
  384.6 8.2 %all-to-all-start.3 = ((bf16[8,2,3840]{2,1,0:T(2,128)(2,1)}), bf16[8,2,3840]{2,1,0:T(2,128)(2,1)S(1)}, u32[]{:S(2)}, u32[]{:S(2)}) async-start(bf16[8,2,3840]{2,1,0:T(2,128)(2,1)} %reshape.532), calls=%async_computation.3 | async-start | bytes 245760 | tf_op jit(solution)/shard_map/all_to_all | solution.py:130
  395.0 8.1 %copy.76 = bf16[8,3,32,164]{3,2,1,0:T(8,128)(2,1)} copy(bf16[8,3,32,164]{0,1,3,2:T(4,128)(2,1)} %bitcast.94) | data formatting | bytes 503808
  403.2 9.6 %reshape.533 = bf16[640,2,2,3,2,4]{5,4,3,2,1,0:T(2,128)(2,1)} reshape(bf16[8,2,3840]{2,1,0:T(2,128)(2,1)S(1)} %all-to-all-done.3) | data formatting | bytes 245760
  412.7 8.0 %copy.89 = bf16[4,2,2,3,8,80,2]{5,4,6,3,2,1,0:T(8,128)(2,1)S(1)} copy(bf16[4,2,2,3,8,80,2]{0,6,3,1,2,5,4:T(2,128)(2,1)} %bitcast.100) | data formatting | bytes 245760 | tf_op jit(solution)/shard_map/all_to_all | solution.py:130
  421.9 10.0 %multiply_reduce_fusion = bf16[80,2,3,1288]{3,2,1,0:T(4,128)(2,1)S(1)} fusion(bf16[32,2,2,3,80,2]{0,3,5,2,1,4:T(4,128)(2,1)S(1)} %copy.75, bf16[80,32,1288]{2,1,0:T(8,128)(2,1)} %param.10, f32[80,2,2,1288]{3,2,1,0:T(2,128)S(1)} %copy-done), kind=kOutput, calls=%fused_computation | convolution fusion | flops 162597120 | bytes 9602560 | tf_op jit(solution)/shard_map/pts,thrcpw->phwrcs/dot_general | solution.py:127
  (77 shorter events, 52.0 us)
Async XLA Ops:
  0.7 3.0 copy-start.8
  19.1 10.4 %copy-start.9 = (f32[32]{0:T(128)S(1)}, f32[32]{0:T(128)}, u32[]{:S(2)}) copy-start(f32[32]{0:T(128)} %param.12) | copy-start | bytes 388
  21.6 22.4 %all-to-all-start = ((bf16[32,2,2,3,80,2]{4,5,3,2,1,0:T(2,128)(2,1)}), bf16[32,2,2,3,80,2]{4,5,3,2,1,0:T(2,128)(2,1)S(1)}, u32[]{:S(2)}, u32[]{:S(2)}) async-start(bf16[32,2,2,3,80,2]{4,5,3,2,1,0:T(2,128)(2,1)} %copy.55), calls=%async_computation | async-start | bytes 393216 | tf_op jit(solution)/shard_map/all_to_all | solution.py:112
  62.5 4.0 copy-start.1
  66.5 38.5 %copy-start.3 = (f32[4,41,1280]{2,1,0:T(8,128)S(1)}, f32[4,41,1280]{2,1,0:T(8,128)}, u32[]{:S(2)}) copy-start(f32[4,41,1280]{2,1,0:T(8,128)} %get-tuple-element.15) | copy-start | bytes 2519044
  66.5 38.5 %copy-start.6 = (f32[4,2,3,1280]{3,2,1,0:T(4,128)S(1)}, f32[4,2,3,1280]{3,2,1,0:T(4,128)}, u32[]{:S(2)}) copy-start(f32[4,2,3,1280]{3,2,1,0:T(4,128)} %copy.60) | copy-start | bytes 368644
  66.5 38.5 %copy-start.7 = (f32[4,2,3,1280]{3,2,1,0:T(4,128)S(1)}, f32[4,2,3,1280]{3,2,1,0:T(4,128)}, u32[]{:S(2)}) copy-start(f32[4,2,3,1280]{3,2,1,0:T(4,128)} %copy.59) | copy-start | bytes 368644
  184.8 7.6 %copy-start.5 = (bf16[8,3,32,164]{3,2,1,0:T(8,128)(2,1)S(1)}, bf16[8,3,32,164]{3,2,1,0:T(8,128)(2,1)}, u32[]{:S(2)}) copy-start(bf16[8,3,32,164]{3,2,1,0:T(8,128)(2,1)} %param.13) | copy-start | bytes 755716
  193.6 17.0 %all-to-all-start.2 = ((bf16[8,3,32,164]{3,0,1,2:T(8,128)(2,1)}), bf16[8,3,32,164]{3,0,1,2:T(8,128)(2,1)S(1)}, u32[]{:S(2)}, u32[]{:S(2)}) async-start(bf16[8,3,32,164]{3,0,1,2:T(8,128)(2,1)} %copy.65), calls=%async_computation.2 | async-start | bytes 786432 | tf_op jit(solution)/shard_map/all_to_all | solution.py:123
  280.2 34.7 %copy-start.2 = (f32[4,41,1280]{2,1,0:T(8,128)S(1)}, f32[4,41,1280]{2,1,0:T(8,128)}, u32[]{:S(2)}) copy-start(f32[4,41,1280]{2,1,0:T(8,128)} %get-tuple-element.14) | copy-start | bytes 2519044
  280.2 34.7 %copy-start.4 = (f32[4,41,1280]{2,1,0:T(8,128)S(1)}, f32[4,41,1280]{2,1,0:T(8,128)}, u32[]{:S(2)}) copy-start(f32[4,41,1280]{2,1,0:T(8,128)} %get-tuple-element.15) | copy-start | bytes 2519044
  384.6 18.5 %all-to-all-start.3 = ((bf16[8,2,3840]{2,1,0:T(2,128)(2,1)}), bf16[8,2,3840]{2,1,0:T(2,128)(2,1)S(1)}, u32[]{:S(2)}, u32[]{:S(2)}) async-start(bf16[8,2,3840]{2,1,0:T(2,128)(2,1)} %reshape.532), calls=%async_computation.3 | async-start | bytes 245760 | tf_op jit(solution)/shard_map/all_to_all | solution.py:130
  412.7 9.1 %copy-start = (f32[80,2,2,1288]{3,2,1,0:T(2,128)S(1)}, f32[80,2,2,1288]{3,2,1,0:T(2,128)}, u32[]{:S(2)}) copy-start(f32[80,2,2,1288]{3,2,1,0:T(2,128)} %pad_maximum_fusion) | copy-start | bytes 4945924
where the time goes:
time: 443 us; the launch traced here: 435 us
  matrix products  235 us (53%)
  local copies, waits for them, and re-layouts  115 us (26%)
  other arithmetic  28.6 us (6%)
  blocking collectives  22.3 us (5%)
  starting transfers between devices  19.4 us (4%)
  waiting for transfers between devices  12.7 us (3%)
    dot_general x2, matrix products, table_product(): jnp.einsum('thcjb,tkb->thcjk', samples, table_low, preferred_element_type...  72.3 us
    dot_general x2, matrix products, table_product(): jnp.einsum('thcjb,tkb->thcjk', samples, table_high, preferred_element_typ...  68.7 us
    unnamed x27, local copies, waits for them, and re-layouts  46 us
    dot_general x1, matrix products, inverse_rows(): jnp.einsum('thcjk,tkb->thcjb', turned_imag, inner_sin, precision=careful)  38.5 us
    dot_general x1, matrix products, inverse_rows(): jnp.einsum('thcjk,tkb->thcjb', turned_real, inner_cos, precision=careful)  37.7 us
    all_to_all x1, blocking collectives, per_device(): lax.all_to_all(grid_lat, 'ba', split_axis=3, concat_axis=2, tiled=True)  22.3 us
    cos x1, other arithmetic, phase_tables(): jnp.cos(outer_angle)  14.1 us
    all_to_all x1, waiting for transfers between devices, per_device(): lax.all_to_all(tend_columns, 'ba', split_axis=2, concat_axis=3, tiled=True)  12.7 us
  transfers between devices with their start and end apart: 3, of which 1 were waited for; matrix products, arithmetic and copies ran while one was open for 6% of the time, Pallas kernels for 0%

commit v1 on v0

v1 whole, which is shorter than its diff:
```python
import functools
import math

import jax
import jax.numpy as jnp
from jax import lax
from jax.experimental import pallas as pl
from jax.experimental.pallas import tpu as pltpu
from jax.sharding import PartitionSpec as P

TRUNCATION = 1279
FIELDS = 3
PAIRS = 80
WAVES = 1280
COLS = 164
OWNERS = 32
BROWS = 176
PAIR_BLOCK = 8
F32 = jnp.float32
BF16 = jnp.bfloat16
NT = (((1,), (1,)), ((), ()))
NN = (((1,), (0,)), ((), ()))


def vmem_params(mib):
    return pltpu.CompilerParams(vmem_limit_bytes=mib << 20)


def swap_kernel(x_ref, o_ref, left, right):
    major, minor = x_ref.shape[0], x_ref.shape[1]
    x = x_ref[...].astype(F32)
    left[...] = x[:, :, :128].reshape(major * minor, 128)
    right[:, 0:36] = x[:, :, 128:164].reshape(major * minor, 36)
    for k in range(minor):
        o_ref[k, :, 0:128] = left[pl.ds(k, major, stride=minor), :].astype(BF16)
        o_ref[k, :, 128:164] = right[pl.ds(k, major, stride=minor), :][:, 0:36].astype(BF16)


def swap_leading(x):
    major, minor, cols = x.shape
    return pl.pallas_call(
        swap_kernel,
        out_shape=jax.ShapeDtypeStruct((minor, major, cols), BF16),
        scratch_shapes=[pltpu.VMEM((major * minor, 128), F32), pltpu.VMEM((major * minor, 128), F32)],
        compiler_params=vmem_params(16),
        cost_estimate=pl.CostEstimate(flops=0, bytes_accessed=4 * major * minor * 256, transcendentals=0),
        name="swap_leading",
    )(x)


def legendre_inverse_kernel(pw_ref, me_ref, leg_ref, spec_ref, out_ref, by_pair, by_lat):
    step = pl.program_id(0)
    slots = leg_ref.shape[2]
    slot = lax.broadcasted_iota(jnp.int32, (8, slots), 1)
    alternate = jnp.where(slot % 2 == 0, 1.0, -1.0).astype(F32)
    valid = slot <= TRUNCATION + 1
    row = lax.broadcasted_iota(jnp.int32, (32, 32), 0)
    for k in range(PAIR_BLOCK):
        pair = step * PAIR_BLOCK + k
        wave = pw_ref[me_ref[0] * PAIRS + pair]
        first = slot <= TRUNCATION - wave
        a = jnp.where(valid, spec_ref[k].astype(F32), 0.0)
        b = a * alternate
        lhs = jnp.concatenate(
            [
                jnp.where(first, a, 0.0),
                jnp.where(first, b, 0.0),
                jnp.where(first, 0.0, a),
                jnp.where(first, 0.0, b),
            ],
            axis=0,
        ).astype(BF16)
        sums = lax.dot_general(lhs, leg_ref[k], NT, preferred_element_type=F32)
        sign = (1 - 2 * (wave % 2)).astype(F32)
        sums = jnp.where(row >= 24, sums * sign, sums)
        by_pair[pl.ds(pair, 32, stride=PAIRS), :] = jnp.concatenate(
            [sums, jnp.zeros((32, 96), F32)], axis=1
        )

    @pl.when(step == pl.num_programs(0) - 1)
    def _():
        for half in range(4):
            h, w = half % 2, half // 2
            for c in range(6):
                start = (half * 8 + c) * PAIRS
                turned = jnp.concatenate(
                    [by_pair[start : start + PAIRS, :], jnp.zeros((48, 128), F32)], axis=0
                ).T
                by_lat[w, pl.ds(h * 6 + c, 32, stride=12), :] = turned[0:32, :]
        x, core = me_ref[0] // 2, me_ref[0] % 2
        for s in range(4):
            for d in range(2):
                dest = ((x + s) % 4) * 2 + (core + d) % 2
                rows = pl.ds(pl.multiple_of(dest * 48, 8), 48)
                out_ref[s, d, :, 0:128] = by_lat[0, rows, :].astype(BF16)
                out_ref[s, d, :, 128:256] = by_lat[1, rows, :].astype(BF16)


def legendre_inverse(pair_wave, me, legendre, spec):
    slots = legendre.shape[2]
    return pl.pallas_call(
        legendre_inverse_kernel,
        grid_spec=pltpu.PrefetchScalarGridSpec(
            num_scalar_prefetch=2,
            grid=(PAIRS // PAIR_BLOCK,),
            in_specs=[
                pl.BlockSpec((PAIR_BLOCK, 32, slots), lambda i, *_: (i, 0, 0)),
                pl.BlockSpec((PAIR_BLOCK, 8, slots), lambda i, *_: (i, 0, 0)),
            ],
            out_specs=pl.BlockSpec((4, 2, 48, 256), lambda i, *_: (0, 0, 0, 0)),
            scratch_shapes=[pltpu.VMEM((32 * PAIRS, 128), F32), pltpu.VMEM((2, 384, 128), F32)],
        ),
        out_shape=jax.ShapeDtypeStruct((4, 2, 48, 256), BF16),
        compiler_params=vmem_params(32),
        cost_estimate=pl.CostEstimate(flops=2 * 80 * 32 * 32 * 1288, bytes_accessed=9_000_000, transcendentals=0),
        name="legendre_inverse",
    )(pair_wave, me, legendre, spec)


def join_pieces(pieces):
    lane = lax.broadcasted_iota(jnp.int32, pieces[0].shape, 1)
    rolled = [pltpu.roll(p, (80 * i) % 128, axis=1) if (80 * i) % 128 else p for i, p in enumerate(pieces)]
    tiles = []
    for k in range(10):
        tile = None
        for i in range(16):
            low, high = 80 * i - 128 * k, 80 * i + 80 - 128 * k
            if high <= 0 or low >= 128:
                continue
            tile = rolled[i] if tile is None else jnp.where(lane >= low, rolled[i], tile)
        tiles.append(tile)
    return tiles


def cut_piece(ref, i):
    tile, shift = (80 * i) // 128, (80 * i) % 128
    low = ref[:, tile * 128 : tile * 128 + 128]
    if shift == 0:
        return low
    low = pltpu.roll(low, 128 - shift, axis=1)
    if shift + 80 <= 128:
        return low
    high = pltpu.roll(ref[:, tile * 128 + 128 : tile * 128 + 256], 128 - shift, axis=1)
    lane = lax.broadcasted_iota(jnp.int32, low.shape, 1)
    return jnp.where(lane < 128 - shift, low, high)


def cos_sin(turn, length):
    times = jnp.floor(turn * (1.0 / length) + 0.5)
    u = (turn - times * length) * (math.pi / length)
    u2 = u * u
    s = u * (
        1.0
        + u2
        * (
            -1.0 / 6
            + u2 * (1.0 / 120 + u2 * (-1.0 / 5040 + u2 * (1.0 / 362880 + u2 * (-1.0 / 39916800))))
        )
    )
    c = 1.0 + u2 * (
        -0.5
        + u2
        * (
            1.0 / 24
            + u2
            * (-1.0 / 720 + u2 * (1.0 / 40320 + u2 * (-1.0 / 3628800 + u2 * (1.0 / 479001600))))
        )
    )
    return 1.0 - 2.0 * s * s, 2.0 * s * c


def table_kernel(me_ref, waves_ref, outer_ref, inner_ref, factor_ref, wave_row):
    lat = pl.program_id(0)
    me = me_ref[0]
    x, core = me // 2, me % 2

    @pl.when(lat == 0)
    def _():
        pieces = []
        for d in range(2):
            for s in range(4):
                source = ((x + 4 - s) % 4) * 2 + (core + d) % 2
                for w in range(2):
                    pieces.append(jnp.broadcast_to(waves_ref[source, w : w + 1, :], (8, 128)))
        for k, tile in enumerate(join_pieces(pieces)):
            wave_row[:, 128 * k : 128 * k + 128] = tile
            factor_ref[:, 128 * k : 128 * k + 128] = jnp.where(tile == 0.0, 1.0, 2.0)

    length = (5012 + 16 * me + 4 * lat).astype(F32)
    length = jnp.full((8, WAVES), length, F32)
    wave = wave_row[...]
    eight = lax.broadcasted_iota(jnp.int32, (8, WAVES), 0).astype(F32)
    low_c, low_s = cos_sin(wave * (eight * COLS), length)
    high_c, high_s = cos_sin(wave * (eight * (8 * COLS)), length)
    for k in range(4):
        hc, hs = high_c[k : k + 1, :], high_s[k : k + 1, :]
        outer_ref[0, 0, 8 * k : 8 * k + 8, :] = low_c * hc - low_s * hs
        outer_ref[0, 1, 8 * k : 8 * k + 8, :] = low_s * hc + low_c * hs
    low_c, low_s = cos_sin(wave * eight, length)
    for block in range(3):
        high_c, high_s = cos_sin(wave * (eight * 8.0 + 64.0 * block), length)
        for k in range(0, 8, 2):
            base = 64 * block + 8 * k
            if base >= BROWS:
                continue
            parts_c, parts_s = [], []
            for kk in (k, k + 1):
                hc, hs = high_c[kk : kk + 1, :], high_s[kk : kk + 1, :]
                parts_c.append(low_c * hc - low_s * hs)
                parts_s.append(low_s * hc + low_c * hs)
            inner_ref[0, base : base + 16, 0:WAVES] = jnp.concatenate(parts_c, axis=0).astype(BF16)
            inner_ref[0, base : base + 16, WAVES:] = jnp.concatenate(parts_s, axis=0).astype(BF16)


def phase_tables(me, waves):
    return pl.pallas_call(
        table_kernel,
        grid_spec=pltpu.PrefetchScalarGridSpec(
            num_scalar_prefetch=1,
            grid=(4,),
            in_specs=[pl.BlockSpec((8, 2, 128), lambda i, *_: (0, 0, 0))],
            out_specs=[
                pl.BlockSpec((1, 2, OWNERS, WAVES), lambda i, *_: (i, 0, 0, 0)),
                pl.BlockSpec((1, BROWS, 2 * WAVES), lambda i, *_: (i, 0, 0)),
                pl.BlockSpec((8, WAVES), lambda i, *_: (0, 0)),
            ],
            scratch_shapes=[pltpu.VMEM((8, WAVES), F32)],
        ),
        out_shape=[
            jax.ShapeDtypeStruct((4, 2, OWNERS, WAVES), F32),
            jax.ShapeDtypeStruct((4, BROWS, 2 * WAVES), BF16),
            jax.ShapeDtypeStruct((8, WAVES), F32),
        ],
        compiler_params=vmem_params(24),
        cost_estimate=pl.CostEstimate(flops=40_000_000, bytes_accessed=5_000_000, transcendentals=0),
        name="phase_tables",
    )(me, waves)


def inside_mask(me, lat):
    length = 5012 + 16 * me + 4 * lat
    owner = lax.broadcasted_iota(jnp.int32, (OWNERS, BROWS), 0)
    col = lax.broadcasted_iota(jnp.int32, (OWNERS, BROWS), 1)
    return (col < COLS) & (owner * COLS + col < length)


def inverse_kernel(
    me_ref, kept_ref, got_ref, outer_ref, inner_ref, factor_ref, grid_ref, send_ref, coeffs, turned, left, right
):
    lat = pl.program_id(0)

    @pl.when(lat == 0)
    def _():
        pieces = []
        for ref in (kept_ref, got_ref):
            for s in range(4):
                for w in range(2):
                    pieces.append(ref[s, :, 128 * w : 128 * w + 128].astype(F32))
        for k, tile in enumerate(join_pieces(pieces)):
            coeffs[:, 128 * k : 128 * k + 128] = tile * factor_ref[0:1, 128 * k : 128 * k + 128]

    for r in range(6):
        h, f = r // 3, r % 3
        real = coeffs[pl.ds(lat * 12 + h * 6 + f, 1), :]
        imag = coeffs[pl.ds(lat * 12 + h * 6 + 3 + f, 1), :]
        oc, os = outer_ref[0, 0], outer_ref[0, 1]
        turned[32 * r : 32 * r + 32, 0:WAVES] = (real * oc - imag * os).astype(BF16)
        turned[32 * r : 32 * r + 32, WAVES:] = (-(real * os + imag * oc)).astype(BF16)
    rows = lax.dot_general(turned[...], inner_ref[0], NT, preferred_element_type=F32)
    inside = inside_mask(me_ref[0], lat)
    for r in range(6):
        value = jnp.where(inside, rows[32 * r : 32 * r + 32, :], 0.0)
        grid_ref[0, 32 * r : 32 * r + 32, :] = value.astype(BF16)
        left[pl.ds(lat * 6 + r, 32, stride=24), :] = value[:, 0:128]
        right[pl.ds(lat * 6 + r, 32, stride=24), :] = jnp.concatenate(
            [value[:, 128:BROWS], jnp.zeros((OWNERS, 256 - BROWS), F32)], axis=1
        )

    @pl.when(lat == 3)
    def _():
        for j in range(OWNERS):
            send_ref[j, :, 0:128] = left[24 * j : 24 * j + 24, :].astype(BF16)
            send_ref[j, :, 128:COLS] = right[24 * j : 24 * j + 24, 0:36].astype(BF16)


def inverse_rows(me, kept, got, outer, inner, factor):
    return pl.pallas_call(
        inverse_kernel,
        grid_spec=pltpu.PrefetchScalarGridSpec(
            num_scalar_prefetch=1,
            grid=(4,),
            in_specs=[
                pl.BlockSpec((4, 48, 256), lambda i, *_: (0, 0, 0)),
                pl.BlockSpec((4, 48, 256), lambda i, *_: (0, 0, 0)),
                pl.BlockSpec((1, 2, OWNERS, WAVES), lambda i, *_: (i, 0, 0, 0)),
                pl.BlockSpec((1, BROWS, 2 * WAVES), lambda i, *_: (i, 0, 0)),
                pl.BlockSpec((8, WAVES), lambda i, *_: (0, 0)),
            ],
            out_specs=[
                pl.BlockSpec((1, 192, BROWS), lambda i, *_: (i, 0, 0)),
                pl.BlockSpec((OWNERS, 24, COLS), lambda i, *_: (0, 0, 0)),
            ],
            scratch_shapes=[
                pltpu.VMEM((48, WAVES), F32),
                pltpu.VMEM((192, 2 * WAVES), BF16),
                pltpu.VMEM((768, 128), F32),
                pltpu.VMEM((768, 128), F32),
            ],
        ),
        out_shape=[
            jax.ShapeDtypeStruct((4, 192, BROWS), BF16),
            jax.ShapeDtypeStruct((OWNERS, 24, COLS), BF16),
        ],
        compiler_params=vmem_params(32),
        cost_estimate=pl.CostEstimate(flops=700_000_000, bytes_accessed=6_000_000, transcendentals=0),
        name="inverse_rows",
    )(me, kept, got, outer, inner, factor)


def direct_kernel(
    me_ref, weight_ref, forcing_ref, grid_ref, outer_ref, inner_ref, out_ref, left, right, samples, sums
):
    lat = pl.program_id(0)
    me = me_ref[0]

    @pl.when(lat == 0)
    def _():
        for j in range(OWNERS):
            left[24 * j : 24 * j + 24, :] = forcing_ref[j, :, 0:128].astype(F32)
            right[24 * j : 24 * j + 24, 0:36] = forcing_ref[j, :, 128:COLS].astype(F32)

    inside = inside_mask(me, lat)
    for r in range(6):
        h, f = r // 3, r % 3
        other = h * 3 + (f + 1) % 3
        product = grid_ref[0, 32 * r : 32 * r + 32, :].astype(F32) * grid_ref[
            0, 32 * other : 32 * other + 32, :
        ].astype(F32)
        force = jnp.concatenate(
            [
                left[pl.ds(lat * 6 + r, 32, stride=24), :],
                right[pl.ds(lat * 6 + r, 32, stride=24), :][:, 0 : BROWS - 128],
            ],
            axis=1,
        )
        samples[32 * r : 32 * r + 32, :] = jnp.where(inside, product + force, 0.0).astype(BF16)
    length = jnp.full((1, 256), (5012 + 16 * me + 4 * lat).astype(F32), F32)
    scale = weight_ref[me * 4 + lat] * lax.rsqrt(length)
    data = samples[...]
    for n in range(0, WAVES, 256):
        part_c = lax.dot_general(data, inner_ref[0, :, n : n + 256], NN, preferred_element_type=F32)
        part_s = lax.dot_general(
            data, inner_ref[0, :, WAVES + n : WAVES + n + 256], NN, preferred_element_type=F32
        )
        oc, os = outer_ref[0, 0, :, n : n + 256], outer_ref[0, 1, :, n : n + 256]
        for r in range(6):
            h, f = r // 3, r % 3
            pc, ps = part_c[32 * r : 32 * r + 32, :], part_s[32 * r : 32 * r + 32, :]
            real = jnp.sum(pc * oc - ps * os, axis=0, keepdims=True)
            imag = jnp.sum(ps * oc + pc * os, axis=0, keepdims=True)
            sums[pl.ds(lat * 12 + h * 6 + f, 1), n : n + 256] = real * scale
            sums[pl.ds(lat * 12 + h * 6 + 3 + f, 1), n : n + 256] = -imag * scale

    @pl.when(lat == 3)
    def _():
        for d in range(2):
            for s in range(4):
                for w in range(2):
                    piece = cut_piece(sums, (d * 4 + s) * 2 + w)
                    out_ref[s, d, :, 128 * w : 128 * w + 128] = piece.astype(BF16)


def direct_rows(me, weight, forcing, grid, outer, inner):
    return pl.pallas_call(
        direct_kernel,
        grid_spec=pltpu.PrefetchScalarGridSpec(
            num_scalar_prefetch=2,
            grid=(4,),
            in_specs=[
                pl.BlockSpec((OWNERS, 24, COLS), lambda i, *_: (0, 0, 0)),
                pl.BlockSpec((1, 192, BROWS), lambda i, *_: (i, 0, 0)),
                pl.BlockSpec((1, 2, OWNERS, WAVES), lambda i, *_: (i, 0, 0, 0)),
                pl.BlockSpec((1, BROWS, 2 * WAVES), lambda i, *_: (i, 0, 0)),
            ],
            out_specs=pl.BlockSpec((4, 2, 48, 256), lambda i, *_: (0, 0, 0, 0)),
            scratch_shapes=[
                pltpu.VMEM((768, 128), F32),
                pltpu.VMEM((768, 128), F32),
                pltpu.VMEM((192, BROWS), BF16),
                pltpu.VMEM((48, WAVES), F32),
            ],
        ),
        out_shape=jax.ShapeDtypeStruct((4, 2, 48, 256), BF16),
        compiler_params=vmem_params(32),
        cost_estimate=pl.CostEstimate(flops=700_000_000, bytes_accessed=6_000_000, transcendentals=0),
        name="direct_rows",
    )(me, weight, forcing, grid, outer, inner)


def legendre_direct_kernel(pw_ref, me_ref, kept_ref, got_ref, leg_ref, out_ref, by_lat, by_pair):
    step = pl.program_id(0)
    slots = leg_ref.shape[2]

    @pl.when(step == 0)
    def _():
        x, core = me_ref[0] // 2, me_ref[0] % 2
        for d, ref in enumerate((kept_ref, got_ref)):
            for s in range(4):
                source = ((x + s) % 4) * 2 + (core + d) % 2
                rows = pl.ds(pl.multiple_of(source * 48, 8), 48)
                for w in range(2):
                    by_lat[w, rows, :] = ref[s, :, 128 * w : 128 * w + 128].astype(F32)
        for w in range(2):
            for c in range(6):
                north = by_lat[w, pl.ds(c, 32, stride=12), :]
                south = by_lat[w, pl.ds(6 + c, 32, stride=12), :]
                for odd, value in enumerate((north + south, north - south)):
                    turned = jnp.concatenate([value, jnp.zeros((96, 128), F32)], axis=0).T
                    by_pair[pl.ds((w * 2 + odd) * 8 + c, PAIRS, stride=32), :] = turned[0:PAIRS, :]

    slot = lax.broadcasted_iota(jnp.int32, (8, slots), 1)
    even = slot % 2 == 0
    valid = slot <= TRUNCATION + 1
    for k in range(PAIR_BLOCK):
        pair = step * PAIR_BLOCK + k
        wave = pw_ref[me_ref[0] * PAIRS + pair]
        lhs = by_pair[pl.ds(pl.multiple_of(pair * 32, 32), 32), :][:, 0:32].astype(BF16)
        sums = lax.dot_general(lhs, leg_ref[k], NN, preferred_element_type=F32)
        first = jnp.where(even, sums[0:8], sums[8:16])
        second = jnp.where((slot + wave) % 2 == 0, sums[16:24], sums[24:32])
        value = jnp.where(slot <= TRUNCATION - wave, first, second)
        out_ref[k] = jnp.where(valid, value, 0.0)[0:6].astype(BF16)


def legendre_direct(pair_wave, me, kept, got, legendre):
    slots = legendre.shape[2]
    return pl.pallas_call(
        legendre_direct_kernel,
        grid_spec=pltpu.PrefetchScalarGridSpec(
            num_scalar_prefetch=2,
            grid=(PAIRS // PAIR_BLOCK,),
            in_specs=[
                pl.BlockSpec((4, 48, 256), lambda i, *_: (0, 0, 0)),
                pl.BlockSpec((4, 48, 256), lambda i, *_: (0, 0, 0)),
                pl.BlockSpec((PAIR_BLOCK, 32, slots), lambda i, *_: (i, 0, 0)),
            ],
            out_specs=pl.BlockSpec((PAIR_BLOCK, 6, slots), lambda i, *_: (i, 0, 0)),
            scratch_shapes=[pltpu.VMEM((2, 384, 128), F32), pltpu.VMEM((32 * PAIRS, 128), F32)],
        ),
        out_shape=jax.ShapeDtypeStruct((PAIRS, 6, slots), BF16),
        compiler_params=vmem_params(32),
        cost_estimate=pl.CostEstimate(flops=2 * 80 * 32 * 32 * 1288, bytes_accessed=9_000_000, transcendentals=0),
        name="legendre_direct",
    )(pair_wave, me, kept, got, legendre)


def exchange(parts, direction):
    came = [parts[0]]
    for s in range(1, 4):
        hop = [(i, ((i // 2 + direction * s) % 4) * 2 + i % 2) for i in range(8)]
        came.append(lax.ppermute(parts[s], "aa", hop))
    kept = jnp.stack([c[0] for c in came])
    passed = jnp.stack([c[1] for c in came])
    return kept, lax.ppermute(passed, "aa", [(i, i ^ 1) for i in range(8)])


def per_device(spec_in, legendre, pair_wave, quad_weight, forcing):
    me = lax.axis_index("aa").astype(jnp.int32).reshape(1)
    forcing_send = swap_leading(forcing.reshape(24, OWNERS, COLS))
    forcing_here = lax.all_to_all(forcing_send, "ba", split_axis=0, concat_axis=0, tiled=True)
    spec = jnp.pad(spec_in.reshape(PAIRS, 6, -1), ((0, 0), (0, 2), (0, 0)))
    fourier = legendre_inverse(pair_wave, me, legendre, spec)
    kept, got = exchange(fourier, 1)
    pairs = pair_wave.astype(F32).reshape(8, PAIRS)
    waves = jnp.pad(jnp.stack([pairs, TRUNCATION - pairs], axis=1), ((0, 0), (0, 0), (0, 48)))
    outer, inner, factor = phase_tables(me, waves)
    rows, grid_send = inverse_rows(me, kept, got, outer, inner, factor)
    grid_came = lax.all_to_all(grid_send, "ba", split_axis=0, concat_axis=0, tiled=True)
    direct = direct_rows(me, quad_weight, forcing_here, rows, outer, inner)
    kept, got = exchange(direct, -1)
    spec_out = legendre_direct(pair_wave, me, kept, got, legendre)
    grid = swap_leading(grid_came)
    return (
        grid.reshape(8, FIELDS, OWNERS, COLS),
        spec_out.reshape(PAIRS, 2, FIELDS, 1, -1),
    )


def solution(mesh):
    placed = (
        P("aa", None, None, "ba", None),
        P("aa", None, None),
        P(),
        P(),
        P("aa", None, None, "ba"),
    )
    return jax.shard_map(
        per_device,
        mesh=mesh,
        in_specs=placed,
        out_specs=(P("aa", None, None, "ba"), P("aa", None, None, "ba", None)),
        check_vma=False,
    )
```

time: 443 us -> 74.1 us (0.17); the launches traced: 435 us -> 73.8 us
  matrix products: 235 us -> 0 us
  local copies, waits for them, and re-layouts: 115 us -> 13.2 us
  other arithmetic: 28.6 us -> 0.08 us
  blocking collectives: 22.3 us -> 0 us
  Pallas kernels: 0 us -> 20.7 us
  starting transfers between devices: 19.4 us -> 33.2 us
  waiting for transfers between devices: 12.7 us -> 5.71 us
    dot_general x8 -> x0, matrix products: 235 us -> none  [the longest x2 72.3 us: table_product(): jnp.einsum('thcjb,tkb->thcjk', samples, table_low, preferred_element_type...]
    unnamed x27 -> x18, local copies, waits for them, and re-layouts: 46 us -> 12.3 us
    convert_element_type x6 -> x0, local copies, waits for them, and re-layouts: 22.6 us -> none  [the longest x1 7.11 us: inverse_rows(): fourier.astype(jnp.float32).reshape(lat_rows, 2, 2, column_count, -1)]
    all_to_all x1 -> x0, blocking collectives: 22.3 us -> none  [per_device(): lax.all_to_all(grid_lat, 'ba', split_axis=3, concat_axis=2, tiled=True)]
    pallas_call x0 -> x7, Pallas kernels: none -> 20.7 us  [the longest x1 5.21 us: legendre_direct(): pl.pallas_call(legendre_direct_kernel, grid_spec=pltpu.PrefetchScalarGrid...]
    all_to_all x6 -> x0, local copies, waits for them, and re-layouts: 16.8 us -> none  [the longest x3 9.1 us: per_device(): lax.all_to_all(direct, 'aa', split_axis=4, concat_axis=0, tiled=True)]
    cos x1 -> x0, other arithmetic: 14.1 us -> none  [phase_tables(): jnp.cos(outer_angle)]
    mul x4 -> x0, local copies, waits for them, and re-layouts: 12.9 us -> none  [the longest x3 11.3 us: inverse_rows(): turned_real = real_part * turn_cos - imag_part * turn_sin]
  transfers between devices with their start and end apart: 3 -> 10, of which waited for: 1 -> 6; matrix products, arithmetic and copies ran while one was open for 6% -> 4% of each run, Pallas kernels for 0% -> 25%
where the time goes in v1:
time: 74.1 us; the launch traced here: 73.8 us
  starting transfers between devices  33.2 us (45%)
  Pallas kernels  20.7 us (28%)
  local copies, waits for them, and re-layouts  13.2 us (18%)
  waiting for transfers between devices  5.71 us (8%)
  between operations  0.86 us (1%)
    unnamed x18, local copies, waits for them, and re-layouts  12.3 us
    all_to_all x1, starting transfers between devices, per_device(): lax.all_to_all(forcing_send, 'ba', split_axis=0, concat_axis=0, tiled=True)  12 us
    all_to_all x1, starting transfers between devices, per_device(): lax.all_to_all(grid_send, 'ba', split_axis=0, concat_axis=0, tiled=True)  9.49 us
    ppermute x6, starting transfers between devices, exchange(): came.append(lax.ppermute(parts[s], 'aa', hop))  7.37 us
    pallas_call x1, Pallas kernels, legendre_direct(): pl.pallas_call(legendre_direct_kernel, grid_spec=pltpu.PrefetchScalarGrid...  5.21 us
    pallas_call x1, Pallas kernels, legendre_inverse(): pl.pallas_call(legendre_inverse_kernel, grid_spec=pltpu.PrefetchScalarGri...  4.48 us
    ppermute x2, starting transfers between devices, exchange(): return (kept, lax.ppermute(passed, 'aa', [(i, i ^ 1) for i in range(8)]))  4.29 us
    ppermute x6, waiting for transfers between devices, exchange(): came.append(lax.ppermute(parts[s], 'aa', hop))  3.85 us
  transfers between devices with their start and end apart: 10, of which 6 were waited for; matrix products, arithmetic and copies ran while one was open for 4% of the time, Pallas kernels for 25%

profile of v1, /device:TPU:1, one launch (start us, length us, event | category | flops | bytes accessed | tf_op | source)
XLA Modules:
  0.0 73.8 jit_solution(17151891508959339043)
XLA Ops:
  0.6 1.0 %copy-done.4 = bf16[8,3,32,164]{3,2,1,0:T(8,128)(2,1)S(1)} copy-done((bf16[8,3,32,164]{3,2,1,0:T(8,128)(2,1)S(1)}, bf16[8,3,32,164]{3,2,1,0:T(8,128)(2,1)}, u32[]{:S(2)}) %copy-start.4) | copy-done | bytes 251928
  1.6 1.3 %swap_leading.3 = bf16[32,24,164]{2,1,0:T(8,128)(2,1)} custom-call(bf16[24,32,164]{2,1,0:T(8,128)(2,1)S(1)} %bitcast.25), custom_call_target="tpu_custom_call" | custom-call | bytes 786432 | tf_op jit(solution)/shard_map/swap_leading/pallas_call | solution.py:41
  2.9 12.0 %all-to-all-start.1 = ((bf16[32,24,164]{2,1,0:T(8,128)(2,1)}), bf16[32,24,164]{2,1,0:T(8,128)(2,1)S(1)}, u32[]{:S(2)}, u32[]{:S(2)}) async-start(bf16[32,24,164]{2,1,0:T(8,128)(2,1)} %swap_leading.3), calls=%async_computation.1 | async-start | bytes 786432 | tf_op jit(solution)/shard_map/all_to_all | solution.py:470
  15.8 2.2 %copy-done = bf16[80,32,1288]{2,1,0:T(8,128)(2,1)S(1)} copy-done((bf16[80,32,1288]{2,1,0:T(8,128)(2,1)S(1)}, bf16[80,32,1288]{2,1,0:T(8,128)(2,1)}, u32[]{:S(2)}) %copy-start) | copy-done | bytes 6594584
  18.0 4.5 %legendre_inverse.1 = bf16[4,2,48,256]{3,2,1,0:T(8,128)(2,1)S(1)} custom-call(s32[640]{0:T(1024)S(1)} %copy-done.5, s32[1]{0:T(128)} %bitcast.me_ref, bf16[80,32,1288]{2,1,0:T(8,128)(2,1)S(1)} %copy-done, bf16[80,8,1288]{2,1,0:T(8,128)(2,1)S(1)} %pad.8.spec_ref), custom_call_target="tpu_custom_call" | custom-call | flops 211025920 | bytes 9000000 | tf_op jit(solution)/shard_map/legendre_inverse/pallas_call | solution.py:101
  22.5 1.3 %collective-permute-start = (bf16[2,48,256]{2,1,0:T(8,128)(2,1)S(1)}, bf16[2,48,256]{2,1,0:T(8,128)(2,1)S(1)}, u32[]{:S(2)}, u32[]{:S(2)}) collective-permute-start(bf16[2,48,256]{2,1,0:T(8,128)(2,1)S(1)} %get-tuple-element.23), channel_id=1, source_target_pairs={{0,64},{32,96},{64,128},{96,160},{128,192},{160,224},{192,0},{224,... | collective-permute-start | bytes 147464 | tf_op jit(solution)/shard_map/ppermute | solution.py:461
  23.8 1.5 %collective-permute-start.2 = (bf16[2,48,256]{2,1,0:T(8,128)(2,1)S(1)}, bf16[2,48,256]{2,1,0:T(8,128)(2,1)S(1)}, u32[]{:S(2)}, u32[]{:S(2)}) collective-permute-start(bf16[2,48,256]{2,1,0:T(8,128)(2,1)S(1)} %get-tuple-element.24), channel_id=1, source_target_pairs={{0,192},{32,224},{64,0},{96,32},{128,64},{160,96},{192,128},{224,1... | collective-permute-start | bytes 147464 | tf_op jit(solution)/shard_map/ppermute | solution.py:461
  25.3 1.5 %collective-permute-start.1 = (bf16[2,48,256]{2,1,0:T(8,128)(2,1)S(1)}, bf16[2,48,256]{2,1,0:T(8,128)(2,1)S(1)}, u32[]{:S(2)}, u32[]{:S(2)}) collective-permute-start(bf16[2,48,256]{2,1,0:T(8,128)(2,1)S(1)} %get-tuple-element.25), channel_id=1, source_target_pairs={{0,128},{32,160},{64,192},{96,224},{128,0},{160,32},{192,64},{224,... | collective-permute-start | bytes 147464 | tf_op jit(solution)/shard_map/ppermute | solution.py:461
  26.9 2.8 %phase_tables.1 = (f32[4,2,32,1280]{3,2,1,0:T(8,128)S(1)}, bf16[4,176,2560]{2,1,0:T(8,128)(2,1)S(1)}, f32[8,1280]{1,0:T(8,128)S(1)}) custom-call(s32[1]{0:T(128)} %bitcast.me_ref, f32[8,2,128]{2,1,0:T(2,128)S(1)} %select_maximum_fusion.waves_ref), custom_call_target="tpu_custom_call" | custom-call | flops 40000000 | bytes 5000000 | tf_op jit(solution)/shard_map/phase_tables/pallas_call | solution.py:216
  30.0 2.5 %collective-permute-start.3 = (bf16[4,48,256]{2,1,0:T(8,128)(2,1)S(1)}, bf16[4,48,256]{2,1,0:T(8,128)(2,1)S(1)}, u32[]{:S(2)}, u32[]{:S(2)}) collective-permute-start(bf16[4,48,256]{2,1,0:T(8,128)(2,1)S(1)} %pad_maximum_fusion.1), channel_id=1, source_target_pairs={{0,32},{32,0},{64,96},{96,64},{128,160},{160,128},{192,224},{224,1... | collective-permute-start | bytes 294920 | tf_op jit(solution)/shard_map/ppermute | solution.py:464
  33.4 2.9 %inverse_rows.1 = (bf16[4,192,176]{2,1,0:T(8,128)(2,1)S(1)}, bf16[32,24,164]{2,1,0:T(8,128)(2,1)}) custom-call(s32[1]{0:T(128)} %bitcast.me_ref, bf16[4,48,256]{2,1,0:T(8,128)(2,1)S(1)} %pad_maximum_fusion.kept_ref, bf16[4,48,256]{2,1,0:T(8,128)(2,1)S(1)} %collective-permute-done.3.got_ref, f32[4,2,32,1280]{3,2,1,0:T(8,128)S(1)} %get-tuple-element.7.outer_ref, ...), custom_call_target="tpu_custom_call" | custom-call | flops 700000000 | bytes 6000000 | tf_op jit(solution)/shard_map/inverse_rows/pallas_call | solution.py:287
  36.3 1.8 %copy-done.2 = bf16[4,176,2560]{2,1,0:T(8,128)(2,1)} copy-done((bf16[4,176,2560]{2,1,0:T(8,128)(2,1)}, bf16[4,176,2560]{2,1,0:T(8,128)(2,1)S(1)}, u32[]{:S(2)}) %copy-start.2) | copy-done | bytes 3604504
  38.0 9.5 %all-to-all-start = ((bf16[32,24,164]{2,1,0:T(8,128)(2,1)}), bf16[32,24,164]{2,1,0:T(8,128)(2,1)S(1)}, u32[]{:S(2)}, u32[]{:S(2)}) async-start(bf16[32,24,164]{2,1,0:T(8,128)(2,1)} %get-tuple-element.10), calls=%async_computation | async-start | bytes 786432 | tf_op jit(solution)/shard_map/all_to_all | solution.py:478
  47.6 2.0 %copy-done.3 = bf16[4,176,2560]{2,1,0:T(8,128)(2,1)S(1)} copy-done((bf16[4,176,2560]{2,1,0:T(8,128)(2,1)S(1)}, bf16[4,176,2560]{2,1,0:T(8,128)(2,1)}, u32[]{:S(2)}) %copy-start.3) | copy-done | bytes 3604504
  49.6 3.1 %direct_rows.1 = bf16[4,2,48,256]{3,2,1,0:T(8,128)(2,1)S(1)} custom-call(s32[1]{0:T(128)} %bitcast.me_ref, f32[32]{0:T(128)S(1)} %copy-done.6, bf16[32,24,164]{2,1,0:T(8,128)(2,1)S(1)} %all-to-all-done.1.forcing_ref, bf16[4,192,176]{2,1,0:T(8,128)(2,1)S(1)} %get-tuple-element.11.grid_ref, f32[4,2,32,1280]{3,2,1,0:T(8,128)S(1)} %get-tuple-element.7.outer_ref, ...), custom_call_target="tpu_custom_call" | custom-call | flops 700000000 | bytes 6000000 | tf_op jit(solution)/shard_map/direct_rows/pallas_call | solution.py:374
  52.7 1.3 %collective-permute-start.4 = (bf16[2,48,256]{2,1,0:T(8,128)(2,1)S(1)}, bf16[2,48,256]{2,1,0:T(8,128)(2,1)S(1)}, u32[]{:S(2)}, u32[]{:S(2)}) collective-permute-start(bf16[2,48,256]{2,1,0:T(8,128)(2,1)S(1)} %get-tuple-element.18), channel_id=1, source_target_pairs={{0,192},{32,224},{64,0},{96,32},{128,64},{160,96},{192,128},{224,1... | collective-permute-start | bytes 147464 | tf_op jit(solution)/shard_map/ppermute | solution.py:461
  54.3 1.6 %collective-permute-start.5 = (bf16[2,48,256]{2,1,0:T(8,128)(2,1)S(1)}, bf16[2,48,256]{2,1,0:T(8,128)(2,1)S(1)}, u32[]{:S(2)}, u32[]{:S(2)}) collective-permute-start(bf16[2,48,256]{2,1,0:T(8,128)(2,1)S(1)} %get-tuple-element.20), channel_id=1, source_target_pairs={{0,128},{32,160},{64,192},{96,224},{128,0},{160,32},{192,64},{224,... | collective-permute-start | bytes 147464 | tf_op jit(solution)/shard_map/ppermute | solution.py:461
  56.0 2.5 %collective-permute-done.6 = bf16[2,48,256]{2,1,0:T(8,128)(2,1)S(1)} collective-permute-done((bf16[2,48,256]{2,1,0:T(8,128)(2,1)S(1)}, bf16[2,48,256]{2,1,0:T(8,128)(2,1)S(1)}, u32[]{:S(2)}, u32[]{:S(2)}) %collective-permute-start.6) | collective-permute-done | bytes 49184 | tf_op jit(solution)/shard_map/ppermute | solution.py:461
  58.5 0.9 %collective-permute-done.5 = bf16[2,48,256]{2,1,0:T(8,128)(2,1)S(1)} collective-permute-done((bf16[2,48,256]{2,1,0:T(8,128)(2,1)S(1)}, bf16[2,48,256]{2,1,0:T(8,128)(2,1)S(1)}, u32[]{:S(2)}, u32[]{:S(2)}) %collective-permute-start.5) | collective-permute-done | bytes 49184 | tf_op jit(solution)/shard_map/ppermute | solution.py:461
  59.5 1.8 %collective-permute-start.7 = (bf16[4,48,256]{2,1,0:T(8,128)(2,1)S(1)}, bf16[4,48,256]{2,1,0:T(8,128)(2,1)S(1)}, u32[]{:S(2)}, u32[]{:S(2)}) collective-permute-start(bf16[4,48,256]{2,1,0:T(8,128)(2,1)S(1)} %pad_maximum_fusion.3), channel_id=1, source_target_pairs={{0,32},{32,0},{64,96},{96,64},{128,160},{160,128},{192,224},{224,1... | collective-permute-start | bytes 294920 | tf_op jit(solution)/shard_map/ppermute | solution.py:464
  62.3 3.0 %copy-done.1 = bf16[80,32,1288]{2,1,0:T(8,128)(2,1)S(1)} copy-done((bf16[80,32,1288]{2,1,0:T(8,128)(2,1)S(1)}, bf16[80,32,1288]{2,1,0:T(8,128)(2,1)}, u32[]{:S(2)}) %copy-start.1) | copy-done | bytes 6594584
  65.3 5.2 %legendre_direct.1 = bf16[80,6,1288]{2,1,0:T(8,128)(2,1)S(1)} custom-call(s32[640]{0:T(1024)S(1)} %copy-done.5, s32[1]{0:T(128)} %bitcast.me_ref, bf16[4,48,256]{2,1,0:T(8,128)(2,1)S(1)} %pad_maximum_fusion.2.kept_ref, bf16[4,48,256]{2,1,0:T(8,128)(2,1)S(1)} %collective-permute-done.7.got_ref, bf16[80,32,1288]{2,1,0:T(8,128)(2,1)S(1)} %copy-done.1), custom_call_target="tpu_custom_call" | custom-call | flops 211025920 | bytes 9000000 | tf_op jit(solution)/shard_map/legendre_direct/pallas_call | solution.py:437
  70.7 2.1 %copy.12 = bf16[80,2,3,1,1288]{4,1,3,2,0:T(2,128)(2,1)} copy(bf16[80,2,3,1,1288]{4,0,2,1,3:T(8,128)(2,1)S(1)} %bitcast.26) | data formatting | bytes 2472960
  72.8 0.9 %swap_leading.2 = bf16[24,32,164]{2,1,0:T(8,128)(2,1)} custom-call(bf16[32,24,164]{2,1,0:T(8,128)(2,1)S(1)} %all-to-all-done.x_ref), custom_call_target="tpu_custom_call" | custom-call | bytes 786432 | tf_op jit(solution)/shard_map/swap_leading/pallas_call | solution.py:41
  (42 shorter events, 3.6 us)
Async XLA Ops:
  0.6 1.0 %copy-start.4 = (bf16[8,3,32,164]{3,2,1,0:T(8,128)(2,1)S(1)}, bf16[8,3,32,164]{3,2,1,0:T(8,128)(2,1)}, u32[]{:S(2)}) copy-start(bf16[8,3,32,164]{3,2,1,0:T(8,128)(2,1)} %param.9) | copy-start | bytes 755716
  1.6 13.3 %copy-start.7 = (bf16[80,2,3,1,1288]{4,1,3,2,0:T(2,128)(2,1)S(1)}, bf16[80,2,3,1,1288]{4,1,3,2,0:T(2,128)(2,1)}, u32[]{:S(2)}) copy-start(bf16[80,2,3,1,1288]{4,1,3,2,0:T(2,128)(2,1)} %param.5) | copy-start | bytes 3709444
  2.9 35.2 %all-to-all-start.1 = ((bf16[32,24,164]{2,1,0:T(8,128)(2,1)}), bf16[32,24,164]{2,1,0:T(8,128)(2,1)S(1)}, u32[]{:S(2)}, u32[]{:S(2)}) async-start(bf16[32,24,164]{2,1,0:T(8,128)(2,1)} %swap_leading.3), calls=%async_computation.1 | async-start | bytes 786432 | tf_op jit(solution)/shard_map/all_to_all | solution.py:470
  14.9 3.0 %copy-start = (bf16[80,32,1288]{2,1,0:T(8,128)(2,1)S(1)}, bf16[80,32,1288]{2,1,0:T(8,128)(2,1)}, u32[]{:S(2)}) copy-start(bf16[80,32,1288]{2,1,0:T(8,128)(2,1)} %leg_ref.3) | copy-start | bytes 19783684
  15.4 2.6 %copy-start.5 = (s32[640]{0:T(1024)S(1)}, s32[640]{0:T(1024)}, u32[]{:S(2)}) copy-start(s32[640]{0:T(1024)} %pw_ref.3) | copy-start | bytes 7684
  22.5 7.3 %collective-permute-start = (bf16[2,48,256]{2,1,0:T(8,128)(2,1)S(1)}, bf16[2,48,256]{2,1,0:T(8,128)(2,1)S(1)}, u32[]{:S(2)}, u32[]{:S(2)}) collective-permute-start(bf16[2,48,256]{2,1,0:T(8,128)(2,1)S(1)} %get-tuple-element.23), channel_id=1, source_target_pairs={{0,64},{32,96},{64,128},{96,160},{128,192},{160,224},{192,0},{224,... | collective-permute-start | bytes 147464 | tf_op jit(solution)/shard_map/ppermute | solution.py:461
  23.8 6.0 %collective-permute-start.2 = (bf16[2,48,256]{2,1,0:T(8,128)(2,1)S(1)}, bf16[2,48,256]{2,1,0:T(8,128)(2,1)S(1)}, u32[]{:S(2)}, u32[]{:S(2)}) collective-permute-start(bf16[2,48,256]{2,1,0:T(8,128)(2,1)S(1)} %get-tuple-element.24), channel_id=1, source_target_pairs={{0,192},{32,224},{64,0},{96,32},{128,64},{160,96},{192,128},{224,1... | collective-permute-start | bytes 147464 | tf_op jit(solution)/shard_map/ppermute | solution.py:461
  25.3 4.7 %collective-permute-start.1 = (bf16[2,48,256]{2,1,0:T(8,128)(2,1)S(1)}, bf16[2,48,256]{2,1,0:T(8,128)(2,1)S(1)}, u32[]{:S(2)}, u32[]{:S(2)}) collective-permute-start(bf16[2,48,256]{2,1,0:T(8,128)(2,1)S(1)} %get-tuple-element.25), channel_id=1, source_target_pairs={{0,128},{32,160},{64,192},{96,224},{128,0},{160,32},{192,64},{224,... | collective-permute-start | bytes 147464 | tf_op jit(solution)/shard_map/ppermute | solution.py:461
  30.0 3.4 %collective-permute-start.3 = (bf16[4,48,256]{2,1,0:T(8,128)(2,1)S(1)}, bf16[4,48,256]{2,1,0:T(8,128)(2,1)S(1)}, u32[]{:S(2)}, u32[]{:S(2)}) collective-permute-start(bf16[4,48,256]{2,1,0:T(8,128)(2,1)S(1)} %pad_maximum_fusion.1), channel_id=1, source_target_pairs={{0,32},{32,0},{64,96},{96,64},{128,160},{160,128},{192,224},{224,1... | collective-permute-start | bytes 294920 | tf_op jit(solution)/shard_map/ppermute | solution.py:464
  33.4 14.1 %copy-start.6 = (f32[32]{0:T(128)S(1)}, f32[32]{0:T(128)}, u32[]{:S(2)}) copy-start(f32[32]{0:T(128)} %weight_ref.1) | copy-start | bytes 388
  36.3 1.8 %copy-start.2 = (bf16[4,176,2560]{2,1,0:T(8,128)(2,1)}, bf16[4,176,2560]{2,1,0:T(8,128)(2,1)S(1)}, u32[]{:S(2)}) copy-start(bf16[4,176,2560]{2,1,0:T(8,128)(2,1)S(1)} %get-tuple-element.8.inner_ref) | copy-start | bytes 10813444
  38.0 34.8 %all-to-all-start = ((bf16[32,24,164]{2,1,0:T(8,128)(2,1)}), bf16[32,24,164]{2,1,0:T(8,128)(2,1)S(1)}, u32[]{:S(2)}, u32[]{:S(2)}) async-start(bf16[32,24,164]{2,1,0:T(8,128)(2,1)} %get-tuple-element.10), calls=%async_computation | async-start | bytes 786432 | tf_op jit(solution)/shard_map/all_to_all | solution.py:478
  47.6 2.0 %copy-start.3 = (bf16[4,176,2560]{2,1,0:T(8,128)(2,1)S(1)}, bf16[4,176,2560]{2,1,0:T(8,128)(2,1)}, u32[]{:S(2)}) copy-start(bf16[4,176,2560]{2,1,0:T(8,128)(2,1)} %copy-done.2) | copy-start | bytes 10813444
  52.7 3.3 %collective-permute-start.4 = (bf16[2,48,256]{2,1,0:T(8,128)(2,1)S(1)}, bf16[2,48,256]{2,1,0:T(8,128)(2,1)S(1)}, u32[]{:S(2)}, u32[]{:S(2)}) collective-permute-start(bf16[2,48,256]{2,1,0:T(8,128)(2,1)S(1)} %get-tuple-element.18), channel_id=1, source_target_pairs={{0,192},{32,224},{64,0},{96,32},{128,64},{160,96},{192,128},{224,1... | collective-permute-start | bytes 147464 | tf_op jit(solution)/shard_map/ppermute | solution.py:461
  54.1 4.5 %collective-permute-start.6 = (bf16[2,48,256]{2,1,0:T(8,128)(2,1)S(1)}, bf16[2,48,256]{2,1,0:T(8,128)(2,1)S(1)}, u32[]{:S(2)}, u32[]{:S(2)}) collective-permute-start(bf16[2,48,256]{2,1,0:T(8,128)(2,1)S(1)} %get-tuple-element.19), channel_id=1, source_target_pairs={{0,64},{32,96},{64,128},{96,160},{128,192},{160,224},{192,0},{224,... | collective-permute-start | bytes 147464 | tf_op jit(solution)/shard_map/ppermute | solution.py:461
  54.3 5.2 %collective-permute-start.5 = (bf16[2,48,256]{2,1,0:T(8,128)(2,1)S(1)}, bf16[2,48,256]{2,1,0:T(8,128)(2,1)S(1)}, u32[]{:S(2)}, u32[]{:S(2)}) collective-permute-start(bf16[2,48,256]{2,1,0:T(8,128)(2,1)S(1)} %get-tuple-element.20), channel_id=1, source_target_pairs={{0,128},{32,160},{64,192},{96,224},{128,0},{160,32},{192,64},{224,... | collective-permute-start | bytes 147464 | tf_op jit(solution)/shard_map/ppermute | solution.py:461
  59.5 2.8 %collective-permute-start.7 = (bf16[4,48,256]{2,1,0:T(8,128)(2,1)S(1)}, bf16[4,48,256]{2,1,0:T(8,128)(2,1)S(1)}, u32[]{:S(2)}, u32[]{:S(2)}) collective-permute-start(bf16[4,48,256]{2,1,0:T(8,128)(2,1)S(1)} %pad_maximum_fusion.3), channel_id=1, source_target_pairs={{0,32},{32,0},{64,96},{96,64},{128,160},{160,128},{192,224},{224,1... | collective-permute-start | bytes 294920 | tf_op jit(solution)/shard_map/ppermute | solution.py:464
  62.3 3.0 %copy-start.1 = (bf16[80,32,1288]{2,1,0:T(8,128)(2,1)S(1)}, bf16[80,32,1288]{2,1,0:T(8,128)(2,1)}, u32[]{:S(2)}) copy-start(bf16[80,32,1288]{2,1,0:T(8,128)(2,1)} %leg_ref.3) | copy-start | bytes 19783684

commit v2 on v1

v2 whole, which is shorter than its diff:
```python
import functools
import math

import jax
import jax.numpy as jnp
from jax import lax
from jax.experimental import pallas as pl
from jax.experimental.pallas import tpu as pltpu
from jax.sharding import PartitionSpec as P

TRUNCATION = 1279
FIELDS = 3
PAIRS = 80
WAVES = 1280
COLS = 164
OWNERS = 32
BROWS = 176
TAIL = COLS - 128
PAIR_BLOCK = 16
F32 = jnp.float32
BF16 = jnp.bfloat16
NT = (((1,), (1,)), ((), ()))
NN = (((1,), (0,)), ((), ()))


def vmem_params(mib):
    return pltpu.CompilerParams(vmem_limit_bytes=mib << 20)


def join_tails(first, second, third):
    return first + pltpu.roll(second, TAIL, axis=1) + pltpu.roll(third, 2 * TAIL, axis=1)


def tail_of(joined, field):
    return pltpu.roll(joined, 128 - TAIL * field, axis=1) if field else joined


def pack_kernel(x_ref, spec_ref, leg_ref, o_ref, spec_out, leg_out, held, arrived, rows, fetched):
    fetches = (
        pltpu.make_async_copy(spec_ref, spec_out, fetched.at[0]),
        pltpu.make_async_copy(leg_ref.at[pl.ds(0, PAIR_BLOCK)], leg_out, fetched.at[1]),
    )

    def part(k):
        return pltpu.make_async_copy(x_ref.at[pl.ds(6 * k, 6)], held.at[pl.ds(6 * k, 6)], arrived.at[k])

    for k in range(4):
        part(k).start()
    for fetch in fetches:
        fetch.start()
    for k in range(4):
        part(k).wait()
        for pair in (2 * k, 2 * k + 1):
            tails = []
            for f in range(FIELDS):
                x = held[3 * pair + f].astype(F32)
                rows[pl.ds(3 * pair + f, OWNERS, stride=32), :] = x[:, 0:128]
                tails.append(jnp.concatenate([x[:, 128:COLS], jnp.zeros((OWNERS, 128 - TAIL), F32)], axis=1))
            rows[pl.ds(24 + pair, OWNERS, stride=32), :] = join_tails(*tails)
    for j in range(OWNERS):
        o_ref[j] = rows[32 * j : 32 * j + 32, :].astype(BF16)
    for fetch in fetches:
        fetch.wait()


def pack_rows(x, spec, legendre):
    slots = legendre.shape[2]
    return pl.pallas_call(
        pack_kernel,
        in_specs=[pl.BlockSpec(memory_space=pltpu.HBM)] * 3,
        out_specs=[pl.BlockSpec(memory_space=pltpu.VMEM)] * 3,
        out_shape=[
            jax.ShapeDtypeStruct((OWNERS, 32, 128), BF16),
            pltpu.VMEM((PAIRS, FIELDS, 2, slots), BF16),
            pltpu.VMEM((PAIR_BLOCK, 32, slots), BF16),
        ],
        scratch_shapes=[
            pltpu.VMEM((24, OWNERS, COLS), BF16),
            pltpu.SemaphoreType.DMA((4,)),
            pltpu.VMEM((1024, 128), F32),
            pltpu.SemaphoreType.DMA((2,)),
        ],
        compiler_params=vmem_params(4),
        cost_estimate=pl.CostEstimate(flops=0, bytes_accessed=800_000, transcendentals=0),
        name="pack_rows",
    )(pltpu.with_memory_space_constraint(x, pltpu.HBM), spec, legendre)


def unpack_kernel(x_ref, o_ref, rows):
    for j in range(OWNERS):
        rows[32 * j : 32 * j + 32, :] = x_ref[j].astype(F32)
    for pair in range(8):
        joined = rows[pl.ds(24 + pair, OWNERS, stride=32), :]
        for f in range(FIELDS):
            o_ref[3 * pair + f, :, 0:128] = rows[pl.ds(3 * pair + f, OWNERS, stride=32), :].astype(BF16)
            o_ref[3 * pair + f, :, 128:COLS] = tail_of(joined, f)[:, 0:TAIL].astype(BF16)


def unpack_rows(x):
    return pl.pallas_call(
        unpack_kernel,
        out_shape=jax.ShapeDtypeStruct((24, OWNERS, COLS), BF16),
        scratch_shapes=[pltpu.VMEM((1024, 128), F32)],
        compiler_params=vmem_params(4),
        cost_estimate=pl.CostEstimate(flops=0, bytes_accessed=800_000, transcendentals=0),
        name="unpack_rows",
    )(x)


def legendre_block(leg_ref, held, arrived, k):
    rows = pl.ds(pl.multiple_of(k * PAIR_BLOCK, PAIR_BLOCK), PAIR_BLOCK)
    return pltpu.make_async_copy(leg_ref.at[rows], held.at[rows], arrived.at[k])


def legendre_start(leg_ref, held, arrived):
    for k in range(1, PAIRS // PAIR_BLOCK):
        legendre_block(leg_ref, held, arrived, k).start()


def legendre_inverse_kernel(
    pw_ref, me_ref, leg_ref, block_ref, spec_ref, out_ref, held, arrived, by_pair, by_lat
):
    step = pl.program_id(0)
    slots = leg_ref.shape[2]
    slot = lax.broadcasted_iota(jnp.int32, (8, slots), 1)
    alternate = jnp.where(slot % 2 == 0, 1.0, -1.0).astype(F32)
    valid = slot <= TRUNCATION + 1
    row = lax.broadcasted_iota(jnp.int32, (32, 32), 0)

    def sum_block(table):
        for k in range(PAIR_BLOCK):
            pair = step * PAIR_BLOCK + k
            wave = pw_ref[me_ref[0] * PAIRS + pair]
            first = slot <= TRUNCATION - wave
            a = jnp.concatenate(
                [spec_ref[pair, f].astype(F32) for f in range(FIELDS)] + [jnp.zeros((2, slots), F32)], axis=0
            )
            a = jnp.where(valid, a, 0.0)
            b = a * alternate
            lhs = jnp.concatenate(
                [
                    jnp.where(first, a, 0.0),
                    jnp.where(first, b, 0.0),
                    jnp.where(first, 0.0, a),
                    jnp.where(first, 0.0, b),
                ],
                axis=0,
            ).astype(BF16)
            sums = lax.dot_general(lhs, table(k), NT, preferred_element_type=F32)
            sign = (1 - 2 * (wave % 2)).astype(F32)
            sums = jnp.where(row >= 24, sums * sign, sums)
            by_pair[pl.ds(pair, 32, stride=PAIRS), :] = jnp.concatenate(
                [sums, jnp.zeros((32, 96), F32)], axis=1
            )

    @pl.when(step == 0)
    def _():
        legendre_start(leg_ref, held, arrived)
        sum_block(lambda k: block_ref[k])

    @pl.when(step > 0)
    def _():
        legendre_block(leg_ref, held, arrived, step).wait()
        sum_block(lambda k: held[step * PAIR_BLOCK + k])

    @pl.when(step == pl.num_programs(0) - 1)
    def _():
        for half in range(4):
            h, w = half % 2, half // 2
            for c in range(6):
                start = (half * 8 + c) * PAIRS
                turned = jnp.concatenate(
                    [by_pair[start : start + PAIRS, :], jnp.zeros((48, 128), F32)], axis=0
                ).T
                by_lat[w, pl.ds(h * 6 + (c % 2) * 3 + c // 2, 32, stride=12), :] = turned[0:32, :]
        x, core = me_ref[0] // 2, me_ref[0] % 2
        for s in range(4):
            for d in range(2):
                dest = ((x + s) % 4) * 2 + (core + d) % 2
                rows = pl.ds(pl.multiple_of(dest * 48, 8), 48)
                out_ref[s, d, :, 0:128] = by_lat[0, rows, :].astype(BF16)
                out_ref[s, d, :, 128:256] = by_lat[1, rows, :].astype(BF16)


def legendre_inverse(pair_wave, me, legendre, block, spec):
    slots = legendre.shape[2]
    return pl.pallas_call(
        legendre_inverse_kernel,
        grid_spec=pltpu.PrefetchScalarGridSpec(
            num_scalar_prefetch=2,
            grid=(PAIRS // PAIR_BLOCK,),
            in_specs=[
                pl.BlockSpec(memory_space=pltpu.HBM),
                pl.BlockSpec(memory_space=pltpu.VMEM),
                pl.BlockSpec(memory_space=pltpu.VMEM),
            ],
            out_specs=pl.BlockSpec((4, 2, 48, 256), lambda i, *_: (0, 0, 0, 0)),
            scratch_shapes=[
                pltpu.VMEM((PAIRS, 32, slots), BF16),
                pltpu.SemaphoreType.DMA((PAIRS // PAIR_BLOCK,)),
                pltpu.VMEM((32 * PAIRS, 128), F32),
                pltpu.VMEM((2, 384, 128), F32),
            ],
        ),
        out_shape=jax.ShapeDtypeStruct((4, 2, 48, 256), BF16),
        compiler_params=vmem_params(16),
        cost_estimate=pl.CostEstimate(flops=2 * 80 * 32 * 32 * 1288, bytes_accessed=9_000_000, transcendentals=0),
        name="legendre_inverse",
    )(pair_wave, me, legendre, block, spec)


def join_pieces(pieces):
    lane = lax.broadcasted_iota(jnp.int32, pieces[0].shape, 1)
    rolled = [pltpu.roll(p, (80 * i) % 128, axis=1) if (80 * i) % 128 else p for i, p in enumerate(pieces)]
    tiles = []
    for k in range(10):
        tile = None
        for i in range(16):
            low, high = 80 * i - 128 * k, 80 * i + 80 - 128 * k
            if high <= 0 or low >= 128:
                continue
            tile = rolled[i] if tile is None else jnp.where(lane >= low, rolled[i], tile)
        tiles.append(tile)
    return tiles


def cut_piece(ref, i):
    tile, shift = (80 * i) // 128, (80 * i) % 128
    low = ref[:, tile * 128 : tile * 128 + 128]
    if shift == 0:
        return low
    low = pltpu.roll(low, 128 - shift, axis=1)
    if shift + 80 <= 128:
        return low
    high = pltpu.roll(ref[:, tile * 128 + 128 : tile * 128 + 256], 128 - shift, axis=1)
    lane = lax.broadcasted_iota(jnp.int32, low.shape, 1)
    return jnp.where(lane < 128 - shift, low, high)


def cos_sin(turn, length):
    times = jnp.floor(turn * (1.0 / length) + 0.5)
    u = (turn - times * length) * (math.pi / length)
    u2 = u * u
    s = u * (
        1.0
        + u2
        * (
            -1.0 / 6
            + u2 * (1.0 / 120 + u2 * (-1.0 / 5040 + u2 * (1.0 / 362880 + u2 * (-1.0 / 39916800))))
        )
    )
    c = 1.0 + u2 * (
        -0.5
        + u2
        * (
            1.0 / 24
            + u2
            * (-1.0 / 720 + u2 * (1.0 / 40320 + u2 * (-1.0 / 3628800 + u2 * (1.0 / 479001600))))
        )
    )
    return 1.0 - 2.0 * s * s, 2.0 * s * c


def table_kernel(me_ref, waves_ref, outer_ref, inner_ref, factor_ref, wave_row):
    lat = pl.program_id(0)
    me = me_ref[0]
    x, core = me // 2, me % 2

    @pl.when(lat == 0)
    def _():
        pieces = []
        for d in range(2):
            for s in range(4):
                source = ((x + 4 - s) % 4) * 2 + (core + d) % 2
                for w in range(2):
                    pieces.append(jnp.broadcast_to(waves_ref[source, w : w + 1, :], (8, 128)))
        for k, tile in enumerate(join_pieces(pieces)):
            wave_row[:, 128 * k : 128 * k + 128] = tile
            factor_ref[:, 128 * k : 128 * k + 128] = jnp.where(tile == 0.0, 1.0, 2.0)

    length = (5012 + 16 * me + 4 * lat).astype(F32)
    length = jnp.full((8, WAVES), length, F32)
    wave = wave_row[...]
    eight = lax.broadcasted_iota(jnp.int32, (8, WAVES), 0).astype(F32)
    low_c, low_s = cos_sin(wave * (eight * COLS), length)
    high_c, high_s = cos_sin(wave * (eight * (8 * COLS)), length)
    for k in range(4):
        hc, hs = high_c[k : k + 1, :], high_s[k : k + 1, :]
        outer_ref[0, 0, 8 * k : 8 * k + 8, :] = low_c * hc - low_s * hs
        outer_ref[0, 1, 8 * k : 8 * k + 8, :] = low_s * hc + low_c * hs
    low_c, low_s = cos_sin(wave * eight, length)
    for block in range(3):
        high_c, high_s = cos_sin(wave * (eight * 8.0 + 64.0 * block), length)
        for k in range(0, 8, 2):
            base = 64 * block + 8 * k
            if base >= BROWS:
                continue
            parts_c, parts_s = [], []
            for kk in (k, k + 1):
                hc, hs = high_c[kk : kk + 1, :], high_s[kk : kk + 1, :]
                parts_c.append(low_c * hc - low_s * hs)
                parts_s.append(low_s * hc + low_c * hs)
            inner_ref[0, base : base + 16, 0:WAVES] = jnp.concatenate(parts_c, axis=0).astype(BF16)
            inner_ref[0, base : base + 16, WAVES:] = jnp.concatenate(parts_s, axis=0).astype(BF16)


def phase_tables(me, waves):
    return pl.pallas_call(
        table_kernel,
        grid_spec=pltpu.PrefetchScalarGridSpec(
            num_scalar_prefetch=1,
            grid=(4,),
            in_specs=[pl.BlockSpec((8, 2, 128), lambda i, *_: (0, 0, 0))],
            out_specs=[
                pl.BlockSpec((1, 2, OWNERS, WAVES), lambda i, *_: (i, 0, 0, 0)),
                pl.BlockSpec((1, BROWS, 2 * WAVES), lambda i, *_: (i, 0, 0)),
                pl.BlockSpec((8, WAVES), lambda i, *_: (0, 0)),
            ],
            scratch_shapes=[pltpu.VMEM((8, WAVES), F32)],
        ),
        out_shape=[
            jax.ShapeDtypeStruct((4, 2, OWNERS, WAVES), F32),
            jax.ShapeDtypeStruct((4, BROWS, 2 * WAVES), BF16),
            jax.ShapeDtypeStruct((8, WAVES), F32),
        ],
        compiler_params=vmem_params(8),
        cost_estimate=pl.CostEstimate(flops=40_000_000, bytes_accessed=5_000_000, transcendentals=0),
        name="phase_tables",
    )(me, waves)


def inside_mask(me, lat):
    length = 5012 + 16 * me + 4 * lat
    owner = lax.broadcasted_iota(jnp.int32, (OWNERS, BROWS), 0)
    col = lax.broadcasted_iota(jnp.int32, (OWNERS, BROWS), 1)
    return (col < COLS) & (owner * COLS + col < length)


def row_kernel(
    me_ref,
    weight_ref,
    kept_ref,
    got_ref,
    forcing_ref,
    outer_ref,
    inner_ref,
    factor_ref,
    leg_ref,
    send_ref,
    own_ref,
    other_ref,
    block_ref,
    fetched,
    coeffs,
    turned,
    grid_rows,
    force_rows,
    values,
    samples,
    sums,
):
    lat = pl.program_id(0)
    me = me_ref[0]

    fetch = pltpu.make_async_copy(leg_ref.at[pl.ds(0, PAIR_BLOCK)], block_ref, fetched)

    @pl.when(lat == 0)
    def _():
        fetch.start()
        pieces = []
        for ref in (kept_ref, got_ref):
            for s in range(4):
                for w in range(2):
                    pieces.append(ref[s, :, 128 * w : 128 * w + 128].astype(F32))
        for k, tile in enumerate(join_pieces(pieces)):
            coeffs[:, 128 * k : 128 * k + 128] = tile * factor_ref[0:1, 128 * k : 128 * k + 128]
        for j in range(OWNERS):
            force_rows[32 * j : 32 * j + 32, :] = forcing_ref[j].astype(F32)

    for r in range(6):
        h, f = r // 3, r % 3
        real = coeffs[pl.ds(lat * 12 + h * 6 + f, 1), :]
        imag = coeffs[pl.ds(lat * 12 + h * 6 + 3 + f, 1), :]
        oc, os = outer_ref[lat, 0], outer_ref[lat, 1]
        turned[32 * r : 32 * r + 32, 0:WAVES] = (real * oc - imag * os).astype(BF16)
        turned[32 * r : 32 * r + 32, WAVES:] = (-(real * os + imag * oc)).astype(BF16)
    rows = lax.dot_general(turned[...], inner_ref[lat], NT, preferred_element_type=F32)
    inside = inside_mask(me, lat)
    for r in range(6):
        value = jnp.where(inside, rows[32 * r : 32 * r + 32, :], 0.0).astype(BF16).astype(F32)
        values[32 * r : 32 * r + 32, :] = value
        grid_rows[pl.ds(lat * 6 + r, OWNERS, stride=32), :] = value[:, 0:128]
    for h in range(2):
        tails = [
            jnp.concatenate(
                [values[32 * r : 32 * r + 32, 128:BROWS], jnp.zeros((OWNERS, 256 - BROWS), F32)], axis=1
            )
            for r in range(3 * h, 3 * h + 3)
        ]
        grid_rows[pl.ds(24 + lat * 2 + h, OWNERS, stride=32), :] = join_tails(*tails)
    for r in range(6):
        h, f = r // 3, r % 3
        other = h * 3 + (f + 1) % 3
        product = values[32 * r : 32 * r + 32, :] * values[32 * other : 32 * other + 32, :]
        tail = tail_of(force_rows[pl.ds(24 + lat * 2 + h, OWNERS, stride=32), :], f)
        force = jnp.concatenate(
            [force_rows[pl.ds(lat * 6 + r, OWNERS, stride=32), :], tail[:, 0 : BROWS - 128]], axis=1
        )
        samples[32 * r : 32 * r + 32, :] = jnp.where(inside, product + force, 0.0).astype(BF16)
    length = jnp.full((1, 256), (5012 + 16 * me + 4 * lat).astype(F32), F32)
    scale = weight_ref[me * 4 + lat] * lax.rsqrt(length)
    data = samples[...]
    for n in range(0, WAVES, 256):
        part_c = lax.dot_general(data, inner_ref[lat, :, n : n + 256], NN, preferred_element_type=F32)
        part_s = lax.dot_general(
            data, inner_ref[lat, :, WAVES + n : WAVES + n + 256], NN, preferred_element_type=F32
        )
        oc, os = outer_ref[lat, 0, :, n : n + 256], outer_ref[lat, 1, :, n : n + 256]
        for r in range(6):
            h, f = r // 3, r % 3
            pc, ps = part_c[32 * r : 32 * r + 32, :], part_s[32 * r : 32 * r + 32, :]
            real = jnp.sum(pc * oc - ps * os, axis=0, keepdims=True)
            imag = jnp.sum(ps * oc + pc * os, axis=0, keepdims=True)
            sums[pl.ds(lat * 12 + h * 6 + f, 1), n : n + 256] = real * scale
            sums[pl.ds(lat * 12 + h * 6 + 3 + f, 1), n : n + 256] = -imag * scale

    @pl.when(lat == 3)
    def _():
        for j in range(OWNERS):
            send_ref[j] = grid_rows[32 * j : 32 * j + 32, :].astype(BF16)
        for d, ref in enumerate((own_ref, other_ref)):
            for s in range(4):
                for w in range(2):
                    piece = cut_piece(sums, (d * 4 + s) * 2 + w)
                    ref[s, :, 128 * w : 128 * w + 128] = piece.astype(BF16)
        fetch.wait()


def transform_rows(me, weight, kept, got, forcing, outer, inner, factor, legendre):
    slots = legendre.shape[2]
    return pl.pallas_call(
        row_kernel,
        grid_spec=pltpu.PrefetchScalarGridSpec(
            num_scalar_prefetch=2,
            grid=(4,),
            in_specs=[
                pl.BlockSpec((4, 48, 256), lambda i, *_: (0, 0, 0)),
                pl.BlockSpec((4, 48, 256), lambda i, *_: (0, 0, 0)),
                pl.BlockSpec(memory_space=pltpu.VMEM),
                pl.BlockSpec(memory_space=pltpu.VMEM),
                pl.BlockSpec(memory_space=pltpu.VMEM),
                pl.BlockSpec(memory_space=pltpu.VMEM),
                pl.BlockSpec(memory_space=pltpu.HBM),
            ],
            out_specs=[
                pl.BlockSpec((OWNERS, 32, 128), lambda i, *_: (0, 0, 0)),
                pl.BlockSpec((4, 48, 256), lambda i, *_: (0, 0, 0)),
                pl.BlockSpec((4, 48, 256), lambda i, *_: (0, 0, 0)),
                pl.BlockSpec(memory_space=pltpu.VMEM),
            ],
            scratch_shapes=[
                pltpu.SemaphoreType.DMA,
                pltpu.VMEM((48, WAVES), F32),
                pltpu.VMEM((192, 2 * WAVES), BF16),
                pltpu.VMEM((1024, 128), F32),
                pltpu.VMEM((1024, 128), F32),
                pltpu.VMEM((192, BROWS), F32),
                pltpu.VMEM((192, BROWS), BF16),
                pltpu.VMEM((48, WAVES), F32),
            ],
        ),
        out_shape=[
            jax.ShapeDtypeStruct((OWNERS, 32, 128), BF16),
            jax.ShapeDtypeStruct((4, 48, 256), BF16),
            jax.ShapeDtypeStruct((4, 48, 256), BF16),
            pltpu.VMEM((PAIR_BLOCK, 32, slots), BF16),
        ],
        compiler_params=vmem_params(14),
        cost_estimate=pl.CostEstimate(flops=1_400_000_000, bytes_accessed=6_000_000, transcendentals=0),
        name="transform_rows",
    )(
        me,
        weight,
        kept,
        got,
        forcing,
        outer,
        inner,
        factor,
        legendre,
    )


def legendre_direct_kernel(
    pw_ref, me_ref, first_ref, second_ref, third_ref, fourth_ref, leg_ref, block_ref, out_ref, held, arrived, by_lat, by_pair
):
    step = pl.program_id(0)
    slots = leg_ref.shape[2]

    @pl.when(step == 0)
    def _():
        legendre_start(leg_ref, held, arrived)
        x, core = me_ref[0] // 2, me_ref[0] % 2
        for s, ref in enumerate((first_ref, second_ref, third_ref, fourth_ref)):
            for d in range(2):
                source = ((x + s) % 4) * 2 + (core + d) % 2
                rows = pl.ds(pl.multiple_of(source * 48, 8), 48)
                for w in range(2):
                    by_lat[w, rows, :] = ref[d, :, 128 * w : 128 * w + 128].astype(F32)
        for w in range(2):
            for c in range(6):
                north = by_lat[w, pl.ds(c, 32, stride=12), :]
                south = by_lat[w, pl.ds(6 + c, 32, stride=12), :]
                for odd, value in enumerate((north + south, north - south)):
                    turned = jnp.concatenate([value, jnp.zeros((96, 128), F32)], axis=0).T
                    row = (w * 2 + odd) * 8 + (c % 3) * 2 + c // 3
                    by_pair[pl.ds(row, PAIRS, stride=32), :] = turned[0:PAIRS, :]

    slot = lax.broadcasted_iota(jnp.int32, (8, slots), 1)
    even = slot % 2 == 0
    valid = slot <= TRUNCATION + 1

    def sum_block(table):
        for k in range(PAIR_BLOCK):
            pair = step * PAIR_BLOCK + k
            wave = pw_ref[me_ref[0] * PAIRS + pair]
            lhs = by_pair[pl.ds(pl.multiple_of(pair * 32, 32), 32), :][:, 0:32].astype(BF16)
            sums = lax.dot_general(lhs, table(k), NN, preferred_element_type=F32)
            first = jnp.where(even, sums[0:8], sums[8:16])
            second = jnp.where((slot + wave) % 2 == 0, sums[16:24], sums[24:32])
            value = jnp.where(slot <= TRUNCATION - wave, first, second)
            value = jnp.where(valid, value, 0.0).astype(BF16)
            for f in range(FIELDS):
                out_ref[k, f] = value[2 * f : 2 * f + 2]

    @pl.when(step == 0)
    def _():
        sum_block(lambda k: block_ref[k])

    @pl.when(step > 0)
    def _():
        legendre_block(leg_ref, held, arrived, step).wait()
        sum_block(lambda k: held[step * PAIR_BLOCK + k])


def legendre_direct(pair_wave, me, came, legendre, block):
    slots = legendre.shape[2]
    return pl.pallas_call(
        legendre_direct_kernel,
        grid_spec=pltpu.PrefetchScalarGridSpec(
            num_scalar_prefetch=2,
            grid=(PAIRS // PAIR_BLOCK,),
            in_specs=[pl.BlockSpec((2, 48, 256), lambda i, *_: (0, 0, 0))] * 4
            + [pl.BlockSpec(memory_space=pltpu.HBM), pl.BlockSpec(memory_space=pltpu.VMEM)],
            out_specs=pl.BlockSpec((PAIR_BLOCK, FIELDS, 2, slots), lambda i, *_: (i, 0, 0, 0)),
            scratch_shapes=[
                pltpu.VMEM((PAIRS, 32, slots), BF16),
                pltpu.SemaphoreType.DMA((PAIRS // PAIR_BLOCK,)),
                pltpu.VMEM((2, 384, 128), F32),
                pltpu.VMEM((32 * PAIRS, 128), F32),
            ],
        ),
        out_shape=jax.ShapeDtypeStruct((PAIRS, FIELDS, 2, slots), BF16),
        compiler_params=vmem_params(16),
        cost_estimate=pl.CostEstimate(flops=2 * 80 * 32 * 32 * 1288, bytes_accessed=9_000_000, transcendentals=0),
        name="legendre_direct",
    )(pair_wave, me, *came, legendre, block)


def to_chip(value, distance):
    return lax.ppermute(value, "aa", [(i, ((i // 2 + distance) % 4) * 2 + i % 2) for i in range(8)])


def to_other_core(value):
    return lax.ppermute(value, "aa", [(i, i ^ 1) for i in range(8)])


def per_device(spec_in, legendre, pair_wave, quad_weight, forcing):
    me = lax.axis_index("aa").astype(jnp.int32).reshape(1)
    legendre = pltpu.with_memory_space_constraint(legendre, pltpu.HBM)
    wave_table = pltpu.with_memory_space_constraint(pair_wave, pltpu.HBM)
    spec = jnp.swapaxes(spec_in.reshape(PAIRS, 2, FIELDS, -1), 1, 2)
    spec = pltpu.with_memory_space_constraint(spec, pltpu.HBM)
    forcing_send, spec, block = pack_rows(forcing.reshape(24, OWNERS, COLS), spec, legendre)
    forcing_here = lax.all_to_all(forcing_send, "ba", split_axis=0, concat_axis=0, tiled=True)
    fourier = legendre_inverse(wave_table, me, legendre, block, spec)
    pairs = pair_wave.astype(F32).reshape(8, PAIRS)
    waves = jnp.pad(jnp.stack([pairs, TRUNCATION - pairs], axis=1), ((0, 0), (0, 0), (0, 48)))
    waves, forcing_here = lax.optimization_barrier((waves, forcing_here))
    outer, inner, factor = phase_tables(me, waves)
    came = [fourier[0]] + [to_chip(fourier[s], s) for s in range(1, 4)]
    *came, factor = lax.optimization_barrier((*came, factor))
    kept = jnp.stack([c[0] for c in came])
    got = to_other_core(jnp.stack([c[1] for c in came]))
    grid_send, own, other, block = transform_rows(
        me, quad_weight, kept, got, forcing_here, outer, inner, factor, legendre
    )
    grid_came = lax.all_to_all(grid_send, "ba", split_axis=0, concat_axis=0, tiled=True)
    passed = to_other_core(other)
    parts = [jnp.stack([own[s], passed[s]]) for s in range(4)]
    came = [parts[0]] + [to_chip(parts[s], -s) for s in range(1, 4)]
    spec_out = legendre_direct(wave_table, me, came, legendre, block)
    grid = unpack_rows(grid_came)
    return (
        grid.reshape(8, FIELDS, OWNERS, COLS),
        jnp.swapaxes(spec_out, 1, 2).reshape(PAIRS, 2, FIELDS, 1, -1),
    )


def solution(mesh):
    placed = (
        P("aa", None, None, "ba", None),
        P("aa", None, None),
        P(),
        P(),
        P("aa", None, None, "ba"),
    )
    return jax.shard_map(
        per_device,
        mesh=mesh,
        in_specs=placed,
        out_specs=(P("aa", None, None, "ba"), P("aa", None, None, "ba", None)),
        check_vma=False,
    )
```

time: 74.1 us -> 64.6 us (0.87)
  local copies, waits for them, and re-layouts: 13.2 us -> 0.15 us
  Pallas kernels: 20.7 us -> 25.1 us
  starting transfers between devices: 33.2 us -> 29.5 us
  waiting for transfers between devices: 5.71 us -> 8.64 us
    unnamed x18 -> x4, local copies, waits for them, and re-layouts: 12.3 us -> 0.01 us
    pallas_call x4 -> x3, Pallas kernels: 8.16 us -> 11.2 us  [the longest x1 7.39 us: transform_rows(): pl.pallas_call(row_kernel, grid_spec=pltpu.PrefetchScalarGridSpec(num_sca...]
    ppermute x8, starting transfers between devices: 11.7 us -> 9.11 us  [the longest x6 5.84 us: to_chip(): lax.ppermute(value, 'aa', [(i, (i // 2 + distance) % 4 * 2 + i % 2) for i...]
    all_to_all x1, waiting for transfers between devices: 0.01 us -> 1.98 us  [per_device(): lax.all_to_all(forcing_send, 'ba', split_axis=0, concat_axis=0, tiled=True)]
    all_to_all x1, starting transfers between devices: 9.49 us -> 8.32 us  [per_device(): lax.all_to_all(grid_send, 'ba', split_axis=0, concat_axis=0, tiled=True)]
    ppermute x8, waiting for transfers between devices: 5.71 us -> 6.66 us  [the longest x6 4.8 us: to_chip(): lax.ppermute(value, 'aa', [(i, (i // 2 + distance) % 4 * 2 + i % 2) for i...]
    pallas_call x1, Pallas kernels: 4.48 us -> 5.33 us  [legendre_inverse(): pl.pallas_call(legendre_inverse_kernel, grid_spec=pltpu.PrefetchScalarGri...]
  transfers between devices with their start and end apart: 10 -> 10, of which waited for: 6 -> 6; matrix products, arithmetic and copies ran while one was open for 4% -> 0% of each run, Pallas kernels for 25% -> 22%
where the time goes in v2:
time: 64.6 us; the launch traced here: 64.3 us
  starting transfers between devices  29.5 us (46%)
  Pallas kernels  25.1 us (39%)
  waiting for transfers between devices  8.64 us (13%)
  between operations  0.8 us (1%)
    all_to_all x1, starting transfers between devices, per_device(): lax.all_to_all(forcing_send, 'ba', split_axis=0, concat_axis=0, tiled=True)  12 us
    all_to_all x1, starting transfers between devices, per_device(): lax.all_to_all(grid_send, 'ba', split_axis=0, concat_axis=0, tiled=True)  8.32 us
    pallas_call x1, Pallas kernels, transform_rows(): pl.pallas_call(row_kernel, grid_spec=pltpu.PrefetchScalarGridSpec(num_sca...  7.39 us
    ppermute x6, starting transfers between devices, to_chip(): lax.ppermute(value, 'aa', [(i, (i // 2 + distance) % 4 * 2 + i % 2) for i...  5.84 us
    pallas_call x1, Pallas kernels, legendre_direct(): pl.pallas_call(legendre_direct_kernel, grid_spec=pltpu.PrefetchScalarGrid...  5.77 us
    pallas_call x1, Pallas kernels, legendre_inverse(): pl.pallas_call(legendre_inverse_kernel, grid_spec=pltpu.PrefetchScalarGri...  5.33 us
    ppermute x6, waiting for transfers between devices, to_chip(): lax.ppermute(value, 'aa', [(i, (i // 2 + distance) % 4 * 2 + i % 2) for i...  4.8 us
    ppermute x2, starting transfers between devices, to_other_core(): return lax.ppermute(value, 'aa', [(i, i ^ 1) for i in range(8)])  3.26 us
  transfers between devices with their start and end apart: 10, of which 6 were waited for; matrix products, arithmetic and copies ran while one was open for 0% of the time, Pallas kernels for 22%

profile of v2, /device:TPU:1, one launch (start us, length us, event | category | flops | bytes accessed | tf_op | source)
XLA Modules:
  0.0 64.3 jit_solution(10171590004285418810)
XLA Ops:
  0.6 2.7 %pack_rows.1 = (bf16[32,32,128]{2,1,0:T(8,128)(2,1)}, bf16[80,3,2,1288]{3,2,1,0:T(2,128)(2,1)S(1)}, bf16[16,32,1288]{2,1,0:T(8,128)(2,1)S(1)}) custom-call(bf16[24,32,164]{2,1,0:T(8,128)(2,1)} %bitcast.21, bf16[80,3,2,1288]{3,2,1,0:T(2,128)(2,1)} %bitcast.19, bf16[80,32,1288]{2,1,0:T(8,128)(2,1)} %leg_ref.7), custom_call_target="tpu_custom_call" | custom-call | bytes 800000 | tf_op jit(solution)/shard_map/pack_rows/pallas_call | solution.py:68
  3.4 12.0 %all-to-all-start = ((bf16[32,32,128]{2,1,0:T(8,128)(2,1)}), bf16[32,32,128]{2,1,0:T(8,128)(2,1)S(1)}, u32[]{:S(2)}, u32[]{:S(2)}) async-start(bf16[32,32,128]{2,1,0:T(8,128)(2,1)} %get-tuple-element.21), calls=%async_computation | async-start | bytes 524288 | tf_op jit(solution)/shard_map/all_to_all | solution.py:585
  15.4 0.0 copy-start
  15.4 5.3 %legendre_inverse.1 = bf16[4,2,48,256]{3,2,1,0:T(8,128)(2,1)S(1)} custom-call(s32[640]{0:T(1024)} %pw_ref.3, s32[1]{0:T(128)} %bitcast.me_ref, bf16[80,32,1288]{2,1,0:T(8,128)(2,1)} %leg_ref.7, bf16[16,32,1288]{2,1,0:T(8,128)(2,1)S(1)} %get-tuple-element.19.block_ref, bf16[80,3,2,1288]{3,2,1,0:T(2,128)(2,1)S(1)} %get-tuple-element.20.spec_ref), custom_call_target="tpu_custom_call" | custom-call | flops 211025920 | bytes 9000000 | tf_op jit(solution)/shard_map/legendre_inverse/pallas_call | solution.py:187
  20.8 2.6 %collective-permute-start.2 = (bf16[2,48,256]{2,1,0:T(8,128)(2,1)S(1)}, bf16[2,48,256]{2,1,0:T(8,128)(2,1)S(1)}, u32[]{:S(2)}, u32[]{:S(2)}) collective-permute-start(bf16[2,48,256]{2,1,0:T(8,128)(2,1)S(1)} %get-tuple-element.38), channel_id=1, source_target_pairs={{0,192},{32,224},{64,0},{96,32},{128,64},{160,96},{192,128},{224,1... | collective-permute-start | bytes 147464 | tf_op jit(solution)/shard_map/ppermute | solution.py:571
  23.4 0.5 collective-permute-start.1
  23.9 0.6 collective-permute-start
  24.5 0.1 stack_reshape.3
  24.6 2.0 %all-to-all-done.forcing_ref = bf16[32,32,128]{2,1,0:T(8,128)(2,1)S(1)} async-done(((bf16[32,32,128]{2,1,0:T(8,128)(2,1)}), bf16[32,32,128]{2,1,0:T(8,128)(2,1)S(1)}, u32[]{:S(2)}, u32[]{:S(2)}) %all-to-all-start) | async-done | bytes 262176 | tf_op jit(solution)/shard_map/all_to_all | solution.py:585
  26.6 2.8 %phase_tables.1 = (f32[4,2,32,1280]{3,2,1,0:T(8,128)S(1)}, bf16[4,176,2560]{2,1,0:T(8,128)(2,1)S(1)}, f32[8,1280]{1,0:T(8,128)S(1)}) custom-call(s32[1]{0:T(128)} %bitcast.me_ref, f32[8,2,128]{2,1,0:T(2,128)S(1)} %select_maximum_fusion.waves_ref), custom_call_target="tpu_custom_call" | custom-call | flops 40000000 | bytes 5000000 | tf_op jit(solution)/shard_map/phase_tables/pallas_call | solution.py:308
  29.5 2.5 %collective-permute-start.3 = (bf16[4,48,256]{2,1,0:T(8,128)(2,1)S(1)}, bf16[4,48,256]{2,1,0:T(8,128)(2,1)S(1)}, u32[]{:S(2)}, u32[]{:S(2)}) collective-permute-start(bf16[4,48,256]{2,1,0:T(8,128)(2,1)S(1)} %pad_maximum_fusion.1), channel_id=1, source_target_pairs={{0,32},{32,0},{64,96},{96,64},{128,160},{160,128},{192,224},{224,1... | collective-permute-start | bytes 294920 | tf_op jit(solution)/shard_map/ppermute | solution.py:575
  32.1 0.9 %collective-permute-done.3.got_ref = bf16[4,48,256]{2,1,0:T(8,128)(2,1)S(1)} collective-permute-done((bf16[4,48,256]{2,1,0:T(8,128)(2,1)S(1)}, bf16[4,48,256]{2,1,0:T(8,128)(2,1)S(1)}, u32[]{:S(2)}, u32[]{:S(2)}) %collective-permute-start.3) | collective-permute-done | bytes 98336 | tf_op jit(solution)/shard_map/ppermute | solution.py:575
  33.0 7.4 %transform_rows.1 = (bf16[32,32,128]{2,1,0:T(8,128)(2,1)}, bf16[4,48,256]{2,1,0:T(8,128)(2,1)S(1)}, bf16[4,48,256]{2,1,0:T(8,128)(2,1)S(1)}, bf16[16,32,1288]{2,1,0:T(8,128)(2,1)S(1)}) custom-call(s32[1]{0:T(128)} %bitcast.me_ref, f32[32]{0:T(128)S(1)} %copy-done, bf16[4,48,256]{2,1,0:T(8,128)(2,1)S(1)} %pad_maximum_fusion.kept_ref, ...), custom_call_target="tpu_custom_call" | custom-call | flops 1400000000 | bytes 6000000 | tf_op jit(solution)/shard_map/transform_rows/pallas_call | solution.py:441
  40.4 8.3 %all-to-all-start.1 = ((bf16[32,32,128]{2,1,0:T(8,128)(2,1)}), bf16[32,32,128]{2,1,0:T(8,128)(2,1)S(1)}, u32[]{:S(2)}, u32[]{:S(2)}) async-start(bf16[32,32,128]{2,1,0:T(8,128)(2,1)} %get-tuple-element.32), calls=%async_computation.1 | async-start | bytes 524288 | tf_op jit(solution)/shard_map/all_to_all | solution.py:598
  48.7 0.7 %collective-permute-start.4 = (bf16[4,48,256]{2,1,0:T(8,128)(2,1)S(1)}, bf16[4,48,256]{2,1,0:T(8,128)(2,1)S(1)}, u32[]{:S(2)}, u32[]{:S(2)}) collective-permute-start(bf16[4,48,256]{2,1,0:T(8,128)(2,1)S(1)} %get-tuple-element.34), channel_id=1, source_target_pairs={{0,32},{32,0},{64,96},{96,64},{128,160},{160,128},{192,224},{224,1... | collective-permute-start | bytes 294920 | tf_op jit(solution)/shard_map/ppermute | solution.py:575
  49.5 0.9 %collective-permute-done.4 = bf16[4,48,256]{2,1,0:T(8,128)(2,1)S(1)} collective-permute-done((bf16[4,48,256]{2,1,0:T(8,128)(2,1)S(1)}, bf16[4,48,256]{2,1,0:T(8,128)(2,1)S(1)}, u32[]{:S(2)}, u32[]{:S(2)}) %collective-permute-start.4) | collective-permute-done | bytes 98336 | tf_op jit(solution)/shard_map/ppermute | solution.py:575
  50.4 0.7 %collective-permute-start.5 = (bf16[2,48,256]{2,1,0:T(8,128)(2,1)S(1)}, bf16[2,48,256]{2,1,0:T(8,128)(2,1)S(1)}, u32[]{:S(2)}, u32[]{:S(2)}) collective-permute-start(bf16[2,48,256]{2,1,0:T(8,128)(2,1)S(1)} %pad_maximum_fusion.3), channel_id=1, source_target_pairs={{0,192},{32,224},{64,0},{96,32},{128,64},{160,96},{192,128},{224,1... | collective-permute-start | bytes 147464 | tf_op jit(solution)/shard_map/ppermute | solution.py:571
  51.2 1.2 %collective-permute-start.6 = (bf16[2,48,256]{2,1,0:T(8,128)(2,1)S(1)}, bf16[2,48,256]{2,1,0:T(8,128)(2,1)S(1)}, u32[]{:S(2)}, u32[]{:S(2)}) collective-permute-start(bf16[2,48,256]{2,1,0:T(8,128)(2,1)S(1)} %pad_maximum_fusion.4), channel_id=1, source_target_pairs={{0,128},{32,160},{64,192},{96,224},{128,0},{160,32},{192,64},{224,... | collective-permute-start | bytes 147464 | tf_op jit(solution)/shard_map/ppermute | solution.py:571
  52.4 0.2 collective-permute-start.7
  52.6 1.1 %collective-permute-done.5.second_ref = bf16[2,48,256]{2,1,0:T(8,128)(2,1)S(1)} collective-permute-done((bf16[2,48,256]{2,1,0:T(8,128)(2,1)S(1)}, bf16[2,48,256]{2,1,0:T(8,128)(2,1)S(1)}, u32[]{:S(2)}, u32[]{:S(2)}) %collective-permute-start.5) | collective-permute-done | bytes 49184 | tf_op jit(solution)/shard_map/ppermute | solution.py:571
  53.7 2.2 %collective-permute-done.6.third_ref = bf16[2,48,256]{2,1,0:T(8,128)(2,1)S(1)} collective-permute-done((bf16[2,48,256]{2,1,0:T(8,128)(2,1)S(1)}, bf16[2,48,256]{2,1,0:T(8,128)(2,1)S(1)}, u32[]{:S(2)}, u32[]{:S(2)}) %collective-permute-start.6) | collective-permute-done | bytes 49184 | tf_op jit(solution)/shard_map/ppermute | solution.py:571
  55.9 1.5 %collective-permute-done.7.fourth_ref = bf16[2,48,256]{2,1,0:T(8,128)(2,1)S(1)} collective-permute-done((bf16[2,48,256]{2,1,0:T(8,128)(2,1)S(1)}, bf16[2,48,256]{2,1,0:T(8,128)(2,1)S(1)}, u32[]{:S(2)}, u32[]{:S(2)}) %collective-permute-start.7) | collective-permute-done | bytes 49184 | tf_op jit(solution)/shard_map/ppermute | solution.py:571
  57.4 5.8 %legendre_direct.1 = bf16[80,3,2,1288]{3,2,1,0:T(2,128)(2,1)} custom-call(s32[640]{0:T(1024)} %pw_ref.3, s32[1]{0:T(128)} %bitcast.me_ref, bf16[2,48,256]{2,1,0:T(8,128)(2,1)S(1)} %pad_maximum_fusion.2.first_ref, bf16[2,48,256]{2,1,0:T(8,128)(2,1)S(1)} %collective-permute-done.5.second_ref, bf16[2,48,256]{2,1,0:T(8,128)(2,1)S(1)} %collective-permute-done.6.third_ref, ...), custom_call_target="tpu_custom_call" | custom-call | flops 211025920 | bytes 9000000 | tf_op jit(solution)/shard_map/legendre_direct/pallas_call | solution.py:548
  63.2 1.1 %unpack_rows.1 = bf16[24,32,164]{2,1,0:T(8,128)(2,1)} custom-call(bf16[32,32,128]{2,1,0:T(8,128)(2,1)S(1)} %all-to-all-done.1.x_ref), custom_call_target="tpu_custom_call" | custom-call | bytes 800000 | tf_op jit(solution)/shard_map/unpack_rows/pallas_call | solution.py:100
  (21 shorter events, 0.2 us)
Async XLA Ops:
  3.4 23.2 %all-to-all-start = ((bf16[32,32,128]{2,1,0:T(8,128)(2,1)}), bf16[32,32,128]{2,1,0:T(8,128)(2,1)S(1)}, u32[]{:S(2)}, u32[]{:S(2)}) async-start(bf16[32,32,128]{2,1,0:T(8,128)(2,1)} %get-tuple-element.21), calls=%async_computation | async-start | bytes 524288 | tf_op jit(solution)/shard_map/all_to_all | solution.py:585
  15.4 9.1 %copy-start.1 = (s32[640]{0:T(1024)S(1)}, s32[640]{0:T(1024)}, u32[]{:S(2)}) copy-start(s32[640]{0:T(1024)} %pw_ref.3) | copy-start | bytes 7684
  15.4 17.6 %copy-start = (f32[32]{0:T(128)S(1)}, f32[32]{0:T(128)}, u32[]{:S(2)}) copy-start(f32[32]{0:T(128)} %weight_ref.1) | copy-start | bytes 388
  20.8 8.6 %collective-permute-start.2 = (bf16[2,48,256]{2,1,0:T(8,128)(2,1)S(1)}, bf16[2,48,256]{2,1,0:T(8,128)(2,1)S(1)}, u32[]{:S(2)}, u32[]{:S(2)}) collective-permute-start(bf16[2,48,256]{2,1,0:T(8,128)(2,1)S(1)} %get-tuple-element.38), channel_id=1, source_target_pairs={{0,192},{32,224},{64,0},{96,32},{128,64},{160,96},{192,128},{224,1... | collective-permute-start | bytes 147464 | tf_op jit(solution)/shard_map/ppermute | solution.py:571
  23.4 6.1 %collective-permute-start.1 = (bf16[2,48,256]{2,1,0:T(8,128)(2,1)S(1)}, bf16[2,48,256]{2,1,0:T(8,128)(2,1)S(1)}, u32[]{:S(2)}, u32[]{:S(2)}) collective-permute-start(bf16[2,48,256]{2,1,0:T(8,128)(2,1)S(1)} %get-tuple-element.39), channel_id=1, source_target_pairs={{0,128},{32,160},{64,192},{96,224},{128,0},{160,32},{192,64},{224,... | collective-permute-start | bytes 147464 | tf_op jit(solution)/shard_map/ppermute | solution.py:571
  23.9 5.6 %collective-permute-start = (bf16[2,48,256]{2,1,0:T(8,128)(2,1)S(1)}, bf16[2,48,256]{2,1,0:T(8,128)(2,1)S(1)}, u32[]{:S(2)}, u32[]{:S(2)}) collective-permute-start(bf16[2,48,256]{2,1,0:T(8,128)(2,1)S(1)} %get-tuple-element.40), channel_id=1, source_target_pairs={{0,64},{32,96},{64,128},{96,160},{128,192},{160,224},{192,0},{224,... | collective-permute-start | bytes 147464 | tf_op jit(solution)/shard_map/ppermute | solution.py:571
  29.5 3.5 %collective-permute-start.3 = (bf16[4,48,256]{2,1,0:T(8,128)(2,1)S(1)}, bf16[4,48,256]{2,1,0:T(8,128)(2,1)S(1)}, u32[]{:S(2)}, u32[]{:S(2)}) collective-permute-start(bf16[4,48,256]{2,1,0:T(8,128)(2,1)S(1)} %pad_maximum_fusion.1), channel_id=1, source_target_pairs={{0,32},{32,0},{64,96},{96,64},{128,160},{160,128},{192,224},{224,1... | collective-permute-start | bytes 294920 | tf_op jit(solution)/shard_map/ppermute | solution.py:575
  40.4 22.8 %all-to-all-start.1 = ((bf16[32,32,128]{2,1,0:T(8,128)(2,1)}), bf16[32,32,128]{2,1,0:T(8,128)(2,1)S(1)}, u32[]{:S(2)}, u32[]{:S(2)}) async-start(bf16[32,32,128]{2,1,0:T(8,128)(2,1)} %get-tuple-element.32), calls=%async_computation.1 | async-start | bytes 524288 | tf_op jit(solution)/shard_map/all_to_all | solution.py:598
  48.7 1.7 %collective-permute-start.4 = (bf16[4,48,256]{2,1,0:T(8,128)(2,1)S(1)}, bf16[4,48,256]{2,1,0:T(8,128)(2,1)S(1)}, u32[]{:S(2)}, u32[]{:S(2)}) collective-permute-start(bf16[4,48,256]{2,1,0:T(8,128)(2,1)S(1)} %get-tuple-element.34), channel_id=1, source_target_pairs={{0,32},{32,0},{64,96},{96,64},{128,160},{160,128},{192,224},{224,1... | collective-permute-start | bytes 294920 | tf_op jit(solution)/shard_map/ppermute | solution.py:575
  50.4 3.3 %collective-permute-start.5 = (bf16[2,48,256]{2,1,0:T(8,128)(2,1)S(1)}, bf16[2,48,256]{2,1,0:T(8,128)(2,1)S(1)}, u32[]{:S(2)}, u32[]{:S(2)}) collective-permute-start(bf16[2,48,256]{2,1,0:T(8,128)(2,1)S(1)} %pad_maximum_fusion.3), channel_id=1, source_target_pairs={{0,192},{32,224},{64,0},{96,32},{128,64},{160,96},{192,128},{224,1... | collective-permute-start | bytes 147464 | tf_op jit(solution)/shard_map/ppermute | solution.py:571
  51.2 4.7 %collective-permute-start.6 = (bf16[2,48,256]{2,1,0:T(8,128)(2,1)S(1)}, bf16[2,48,256]{2,1,0:T(8,128)(2,1)S(1)}, u32[]{:S(2)}, u32[]{:S(2)}) collective-permute-start(bf16[2,48,256]{2,1,0:T(8,128)(2,1)S(1)} %pad_maximum_fusion.4), channel_id=1, source_target_pairs={{0,128},{32,160},{64,192},{96,224},{128,0},{160,32},{192,64},{224,... | collective-permute-start | bytes 147464 | tf_op jit(solution)/shard_map/ppermute | solution.py:571
  52.4 5.0 %collective-permute-start.7 = (bf16[2,48,256]{2,1,0:T(8,128)(2,1)S(1)}, bf16[2,48,256]{2,1,0:T(8,128)(2,1)S(1)}, u32[]{:S(2)}, u32[]{:S(2)}) collective-permute-start(bf16[2,48,256]{2,1,0:T(8,128)(2,1)S(1)} %pad_maximum_fusion.5), channel_id=1, source_target_pairs={{0,64},{32,96},{64,128},{96,160},{128,192},{160,224},{192,0},{224,... | collective-permute-start | bytes 147464 | tf_op jit(solution)/shard_map/ppermute | solution.py:571

commit v3 on v2

--- a/solution.py
+++ b/solution.py
@@ -470,7 +470,7 @@
             ],
         ),
         out_shape=[
-            jax.ShapeDtypeStruct((OWNERS, 32, 128), BF16),
+            pltpu.HBM((OWNERS, 32, 128), BF16),
             jax.ShapeDtypeStruct((4, 48, 256), BF16),
             jax.ShapeDtypeStruct((4, 48, 256), BF16),
             pltpu.VMEM((PAIR_BLOCK, 32, slots), BF16),
@@ -595,9 +595,10 @@
     grid_send, own, other, block = transform_rows(
         me, quad_weight, kept, got, forcing_here, outer, inner, factor, legendre
     )
+    staying, grid_send = lax.optimization_barrier((own[0], grid_send))
     grid_came = lax.all_to_all(grid_send, "ba", split_axis=0, concat_axis=0, tiled=True)
     passed = to_other_core(other)
-    parts = [jnp.stack([own[s], passed[s]]) for s in range(4)]
+    parts = [jnp.stack([own[s] if s else staying, passed[s]]) for s in range(4)]
     came = [parts[0]] + [to_chip(parts[s], -s) for s in range(1, 4)]
     spec_out = legendre_direct(wave_table, me, came, legendre, block)
     grid = unpack_rows(grid_came)

time: 64.6 us -> 63.4 us (0.981)
  waiting for transfers between devices: 8.64 us -> 7.71 us
    ppermute x2, waiting for transfers between devices: 1.86 us -> 0.93 us  [to_other_core(): return lax.ppermute(value, 'aa', [(i, i ^ 1) for i in range(8)])]
  transfers between devices with their start and end apart: 10 -> 10, of which waited for: 6 -> 5; matrix products, arithmetic and copies ran while one was open for 0% -> 0% of each run, Pallas kernels for 22% -> 22%
where the time goes in v3:
time: 63.4 us; the launch traced here: 63 us
  starting transfers between devices  29.2 us (46%)
  Pallas kernels  25 us (39%)
  waiting for transfers between devices  7.71 us (12%)
  between operations  0.82 us (1%)
    all_to_all x1, starting transfers between devices, per_device(): lax.all_to_all(forcing_send, 'ba', split_axis=0, concat_axis=0, tiled=True)  12 us
    all_to_all x1, starting transfers between devices, per_device(): lax.all_to_all(grid_send, 'ba', split_axis=0, concat_axis=0, tiled=True)  8.32 us
    pallas_call x1, Pallas kernels, transform_rows(): pl.pallas_call(row_kernel, grid_spec=pltpu.PrefetchScalarGridSpec(num_sca...  7.29 us
    ppermute x6, starting transfers between devices, to_chip(): lax.ppermute(value, 'aa', [(i, (i // 2 + distance) % 4 * 2 + i % 2) for i...  5.84 us
    pallas_call x1, Pallas kernels, legendre_direct(): pl.pallas_call(legendre_direct_kernel, grid_spec=pltpu.PrefetchScalarGrid...  5.78 us
    pallas_call x1, Pallas kernels, legendre_inverse(): pl.pallas_call(legendre_inverse_kernel, grid_spec=pltpu.PrefetchScalarGri...  5.33 us
    ppermute x6, waiting for transfers between devices, to_chip(): lax.ppermute(value, 'aa', [(i, (i // 2 + distance) % 4 * 2 + i % 2) for i...  4.8 us
    ppermute x2, starting transfers between devices, to_other_core(): return lax.ppermute(value, 'aa', [(i, i ^ 1) for i in range(8)])  2.98 us
  transfers between devices with their start and end apart: 10, of which 5 were waited for; matrix products, arithmetic and copies ran while one was open for 0% of the time, Pallas kernels for 22%

profile of v3, /device:TPU:1, one launch (start us, length us, event | category | flops | bytes accessed | tf_op | source)
XLA Modules:
  0.0 63.0 jit_solution(4585814374389128107)
XLA Ops:
  0.6 2.7 %pack_rows.1 = (bf16[32,32,128]{2,1,0:T(8,128)(2,1)}, bf16[80,3,2,1288]{3,2,1,0:T(2,128)(2,1)S(1)}, bf16[16,32,1288]{2,1,0:T(8,128)(2,1)S(1)}) custom-call(bf16[24,32,164]{2,1,0:T(8,128)(2,1)} %bitcast.24, bf16[80,3,2,1288]{3,2,1,0:T(2,128)(2,1)} %bitcast.22, bf16[80,32,1288]{2,1,0:T(8,128)(2,1)} %leg_ref.7), custom_call_target="tpu_custom_call" | custom-call | bytes 800000 | tf_op jit(solution)/shard_map/pack_rows/pallas_call | solution.py:68
  3.4 12.0 %all-to-all-start = ((bf16[32,32,128]{2,1,0:T(8,128)(2,1)}), bf16[32,32,128]{2,1,0:T(8,128)(2,1)S(1)}, u32[]{:S(2)}, u32[]{:S(2)}) async-start(bf16[32,32,128]{2,1,0:T(8,128)(2,1)} %get-tuple-element.23), calls=%async_computation | async-start | bytes 524288 | tf_op jit(solution)/shard_map/all_to_all | solution.py:585
  15.4 0.0 copy-start.1
  15.4 0.0 copy-start
  15.4 5.3 %legendre_inverse.1 = bf16[4,2,48,256]{3,2,1,0:T(8,128)(2,1)S(1)} custom-call(s32[640]{0:T(1024)} %pw_ref.3, s32[1]{0:T(128)} %bitcast.me_ref, bf16[80,32,1288]{2,1,0:T(8,128)(2,1)} %leg_ref.7, bf16[16,32,1288]{2,1,0:T(8,128)(2,1)S(1)} %get-tuple-element.21.block_ref, bf16[80,3,2,1288]{3,2,1,0:T(2,128)(2,1)S(1)} %get-tuple-element.22.spec_ref), custom_call_target="tpu_custom_call" | custom-call | flops 211025920 | bytes 9000000 | tf_op jit(solution)/shard_map/legendre_inverse/pallas_call | solution.py:187
  20.8 2.6 %collective-permute-start.2 = (bf16[2,48,256]{2,1,0:T(8,128)(2,1)S(1)}, bf16[2,48,256]{2,1,0:T(8,128)(2,1)S(1)}, u32[]{:S(2)}, u32[]{:S(2)}) collective-permute-start(bf16[2,48,256]{2,1,0:T(8,128)(2,1)S(1)} %get-tuple-element.42), channel_id=1, source_target_pairs={{0,192},{32,224},{64,0},{96,32},{128,64},{160,96},{192,128},{224,1... | collective-permute-start | bytes 147464 | tf_op jit(solution)/shard_map/ppermute | solution.py:571
  23.4 0.5 collective-permute-start.1
  23.9 0.6 collective-permute-start
  24.5 0.1 stack_reshape.3
  24.6 2.0 %all-to-all-done.forcing_ref = bf16[32,32,128]{2,1,0:T(8,128)(2,1)S(1)} async-done(((bf16[32,32,128]{2,1,0:T(8,128)(2,1)}), bf16[32,32,128]{2,1,0:T(8,128)(2,1)S(1)}, u32[]{:S(2)}, u32[]{:S(2)}) %all-to-all-start) | async-done | bytes 262176 | tf_op jit(solution)/shard_map/all_to_all | solution.py:585
  26.6 2.8 %phase_tables.1 = (f32[4,2,32,1280]{3,2,1,0:T(8,128)S(1)}, bf16[4,176,2560]{2,1,0:T(8,128)(2,1)S(1)}, f32[8,1280]{1,0:T(8,128)S(1)}) custom-call(s32[1]{0:T(128)} %bitcast.me_ref, f32[8,2,128]{2,1,0:T(2,128)S(1)} %select_maximum_fusion.waves_ref), custom_call_target="tpu_custom_call" | custom-call | flops 40000000 | bytes 5000000 | tf_op jit(solution)/shard_map/phase_tables/pallas_call | solution.py:308
  29.5 2.5 %collective-permute-start.3 = (bf16[4,48,256]{2,1,0:T(8,128)(2,1)S(1)}, bf16[4,48,256]{2,1,0:T(8,128)(2,1)S(1)}, u32[]{:S(2)}, u32[]{:S(2)}) collective-permute-start(bf16[4,48,256]{2,1,0:T(8,128)(2,1)S(1)} %pad_maximum_fusion.1), channel_id=1, source_target_pairs={{0,32},{32,0},{64,96},{96,64},{128,160},{160,128},{192,224},{224,1... | collective-permute-start | bytes 294920 | tf_op jit(solution)/shard_map/ppermute | solution.py:575
  32.1 0.9 %collective-permute-done.3.got_ref = bf16[4,48,256]{2,1,0:T(8,128)(2,1)S(1)} collective-permute-done((bf16[4,48,256]{2,1,0:T(8,128)(2,1)S(1)}, bf16[4,48,256]{2,1,0:T(8,128)(2,1)S(1)}, u32[]{:S(2)}, u32[]{:S(2)}) %collective-permute-start.3) | collective-permute-done | bytes 98336 | tf_op jit(solution)/shard_map/ppermute | solution.py:575
  33.0 7.3 %transform_rows.1 = (bf16[32,32,128]{2,1,0:T(8,128)(2,1)}, bf16[4,48,256]{2,1,0:T(8,128)(2,1)S(1)}, bf16[4,48,256]{2,1,0:T(8,128)(2,1)S(1)}, bf16[16,32,1288]{2,1,0:T(8,128)(2,1)S(1)}) custom-call(s32[1]{0:T(128)} %bitcast.me_ref, f32[32]{0:T(128)S(1)} %copy-done, bf16[4,48,256]{2,1,0:T(8,128)(2,1)S(1)} %pad_maximum_fusion.kept_ref, ...), custom_call_target="tpu_custom_call" | custom-call | flops 1400000000 | bytes 6000000 | tf_op jit(solution)/shard_map/transform_rows/pallas_call | solution.py:441
  40.3 0.4 collective-permute-start.4
  40.7 8.3 %all-to-all-start.1 = ((bf16[32,32,128]{2,1,0:T(8,128)(2,1)}), bf16[32,32,128]{2,1,0:T(8,128)(2,1)S(1)}, u32[]{:S(2)}, u32[]{:S(2)}) async-start(bf16[32,32,128]{2,1,0:T(8,128)(2,1)} %get-tuple-element.36), calls=%async_computation.1 | async-start | bytes 524288 | tf_op jit(solution)/shard_map/all_to_all | solution.py:599
  49.1 0.7 %collective-permute-start.5 = (bf16[2,48,256]{2,1,0:T(8,128)(2,1)S(1)}, bf16[2,48,256]{2,1,0:T(8,128)(2,1)S(1)}, u32[]{:S(2)}, u32[]{:S(2)}) collective-permute-start(bf16[2,48,256]{2,1,0:T(8,128)(2,1)S(1)} %pad_maximum_fusion.3), channel_id=1, source_target_pairs={{0,192},{32,224},{64,0},{96,32},{128,64},{160,96},{192,128},{224,1... | collective-permute-start | bytes 147464 | tf_op jit(solution)/shard_map/ppermute | solution.py:571
  49.9 1.2 %collective-permute-start.6 = (bf16[2,48,256]{2,1,0:T(8,128)(2,1)S(1)}, bf16[2,48,256]{2,1,0:T(8,128)(2,1)S(1)}, u32[]{:S(2)}, u32[]{:S(2)}) collective-permute-start(bf16[2,48,256]{2,1,0:T(8,128)(2,1)S(1)} %pad_maximum_fusion.4), channel_id=1, source_target_pairs={{0,128},{32,160},{64,192},{96,224},{128,0},{160,32},{192,64},{224,... | collective-permute-start | bytes 147464 | tf_op jit(solution)/shard_map/ppermute | solution.py:571
  51.1 0.2 collective-permute-start.7
  51.3 0.8 %collective-permute-done.5.second_ref = bf16[2,48,256]{2,1,0:T(8,128)(2,1)S(1)} collective-permute-done((bf16[2,48,256]{2,1,0:T(8,128)(2,1)S(1)}, bf16[2,48,256]{2,1,0:T(8,128)(2,1)S(1)}, u32[]{:S(2)}, u32[]{:S(2)}) %collective-permute-start.5) | collective-permute-done | bytes 49184 | tf_op jit(solution)/shard_map/ppermute | solution.py:571
  52.1 2.2 %collective-permute-done.6.third_ref = bf16[2,48,256]{2,1,0:T(8,128)(2,1)S(1)} collective-permute-done((bf16[2,48,256]{2,1,0:T(8,128)(2,1)S(1)}, bf16[2,48,256]{2,1,0:T(8,128)(2,1)S(1)}, u32[]{:S(2)}, u32[]{:S(2)}) %collective-permute-start.6) | collective-permute-done | bytes 49184 | tf_op jit(solution)/shard_map/ppermute | solution.py:571
  54.3 1.8 %collective-permute-done.7.fourth_ref = bf16[2,48,256]{2,1,0:T(8,128)(2,1)S(1)} collective-permute-done((bf16[2,48,256]{2,1,0:T(8,128)(2,1)S(1)}, bf16[2,48,256]{2,1,0:T(8,128)(2,1)S(1)}, u32[]{:S(2)}, u32[]{:S(2)}) %collective-permute-start.7) | collective-permute-done | bytes 49184 | tf_op jit(solution)/shard_map/ppermute | solution.py:571
  56.1 5.8 %legendre_direct.1 = bf16[80,3,2,1288]{3,2,1,0:T(2,128)(2,1)} custom-call(s32[640]{0:T(1024)} %pw_ref.3, s32[1]{0:T(128)} %bitcast.me_ref, bf16[2,48,256]{2,1,0:T(8,128)(2,1)S(1)} %pad_maximum_fusion.2.first_ref, bf16[2,48,256]{2,1,0:T(8,128)(2,1)S(1)} %collective-permute-done.5.second_ref, bf16[2,48,256]{2,1,0:T(8,128)(2,1)S(1)} %collective-permute-done.6.third_ref, ...), custom_call_target="tpu_custom_call" | custom-call | flops 211025920 | bytes 9000000 | tf_op jit(solution)/shard_map/legendre_direct/pallas_call | solution.py:548
  61.9 1.1 %unpack_rows.1 = bf16[24,32,164]{2,1,0:T(8,128)(2,1)} custom-call(bf16[32,32,128]{2,1,0:T(8,128)(2,1)S(1)} %all-to-all-done.1.x_ref), custom_call_target="tpu_custom_call" | custom-call | bytes 800000 | tf_op jit(solution)/shard_map/unpack_rows/pallas_call | solution.py:100
  (21 shorter events, 0.2 us)
Async XLA Ops:
  3.4 23.2 %all-to-all-start = ((bf16[32,32,128]{2,1,0:T(8,128)(2,1)}), bf16[32,32,128]{2,1,0:T(8,128)(2,1)S(1)}, u32[]{:S(2)}, u32[]{:S(2)}) async-start(bf16[32,32,128]{2,1,0:T(8,128)(2,1)} %get-tuple-element.23), calls=%async_computation | async-start | bytes 524288 | tf_op jit(solution)/shard_map/all_to_all | solution.py:585
  15.4 9.1 %copy-start.1 = (s32[640]{0:T(1024)S(1)}, s32[640]{0:T(1024)}, u32[]{:S(2)}) copy-start(s32[640]{0:T(1024)} %pw_ref.3) | copy-start | bytes 7684
  15.4 17.6 %copy-start = (f32[32]{0:T(128)S(1)}, f32[32]{0:T(128)}, u32[]{:S(2)}) copy-start(f32[32]{0:T(128)} %weight_ref.1) | copy-start | bytes 388
  20.8 8.6 %collective-permute-start.2 = (bf16[2,48,256]{2,1,0:T(8,128)(2,1)S(1)}, bf16[2,48,256]{2,1,0:T(8,128)(2,1)S(1)}, u32[]{:S(2)}, u32[]{:S(2)}) collective-permute-start(bf16[2,48,256]{2,1,0:T(8,128)(2,1)S(1)} %get-tuple-element.42), channel_id=1, source_target_pairs={{0,192},{32,224},{64,0},{96,32},{128,64},{160,96},{192,128},{224,1... | collective-permute-start | bytes 147464 | tf_op jit(solution)/shard_map/ppermute | solution.py:571
  23.4 6.1 %collective-permute-start.1 = (bf16[2,48,256]{2,1,0:T(8,128)(2,1)S(1)}, bf16[2,48,256]{2,1,0:T(8,128)(2,1)S(1)}, u32[]{:S(2)}, u32[]{:S(2)}) collective-permute-start(bf16[2,48,256]{2,1,0:T(8,128)(2,1)S(1)} %get-tuple-element.43), channel_id=1, source_target_pairs={{0,128},{32,160},{64,192},{96,224},{128,0},{160,32},{192,64},{224,... | collective-permute-start | bytes 147464 | tf_op jit(solution)/shard_map/ppermute | solution.py:571
  23.9 5.6 %collective-permute-start = (bf16[2,48,256]{2,1,0:T(8,128)(2,1)S(1)}, bf16[2,48,256]{2,1,0:T(8,128)(2,1)S(1)}, u32[]{:S(2)}, u32[]{:S(2)}) collective-permute-start(bf16[2,48,256]{2,1,0:T(8,128)(2,1)S(1)} %get-tuple-element.44), channel_id=1, source_target_pairs={{0,64},{32,96},{64,128},{96,160},{128,192},{160,224},{192,0},{224,... | collective-permute-start | bytes 147464 | tf_op jit(solution)/shard_map/ppermute | solution.py:571
  29.5 3.5 %collective-permute-start.3 = (bf16[4,48,256]{2,1,0:T(8,128)(2,1)S(1)}, bf16[4,48,256]{2,1,0:T(8,128)(2,1)S(1)}, u32[]{:S(2)}, u32[]{:S(2)}) collective-permute-start(bf16[4,48,256]{2,1,0:T(8,128)(2,1)S(1)} %pad_maximum_fusion.1), channel_id=1, source_target_pairs={{0,32},{32,0},{64,96},{96,64},{128,160},{160,128},{192,224},{224,1... | collective-permute-start | bytes 294920 | tf_op jit(solution)/shard_map/ppermute | solution.py:575
  40.3 8.8 %collective-permute-start.4 = (bf16[4,48,256]{2,1,0:T(8,128)(2,1)S(1)}, bf16[4,48,256]{2,1,0:T(8,128)(2,1)S(1)}, u32[]{:S(2)}, u32[]{:S(2)}) collective-permute-start(bf16[4,48,256]{2,1,0:T(8,128)(2,1)S(1)} %get-tuple-element.38), channel_id=1, source_target_pairs={{0,32},{32,0},{64,96},{96,64},{128,160},{160,128},{192,224},{224,1... | collective-permute-start | bytes 294920 | tf_op jit(solution)/shard_map/ppermute | solution.py:575
  40.7 21.1 %all-to-all-start.1 = ((bf16[32,32,128]{2,1,0:T(8,128)(2,1)}), bf16[32,32,128]{2,1,0:T(8,128)(2,1)S(1)}, u32[]{:S(2)}, u32[]{:S(2)}) async-start(bf16[32,32,128]{2,1,0:T(8,128)(2,1)} %get-tuple-element.36), calls=%async_computation.1 | async-start | bytes 524288 | tf_op jit(solution)/shard_map/all_to_all | solution.py:599
  49.1 3.0 %collective-permute-start.5 = (bf16[2,48,256]{2,1,0:T(8,128)(2,1)S(1)}, bf16[2,48,256]{2,1,0:T(8,128)(2,1)S(1)}, u32[]{:S(2)}, u32[]{:S(2)}) collective-permute-start(bf16[2,48,256]{2,1,0:T(8,128)(2,1)S(1)} %pad_maximum_fusion.3), channel_id=1, source_target_pairs={{0,192},{32,224},{64,0},{96,32},{128,64},{160,96},{192,128},{224,1... | collective-permute-start | bytes 147464 | tf_op jit(solution)/shard_map/ppermute | solution.py:571
  49.9 4.4 %collective-permute-start.6 = (bf16[2,48,256]{2,1,0:T(8,128)(2,1)S(1)}, bf16[2,48,256]{2,1,0:T(8,128)(2,1)S(1)}, u32[]{:S(2)}, u32[]{:S(2)}) collective-permute-start(bf16[2,48,256]{2,1,0:T(8,128)(2,1)S(1)} %pad_maximum_fusion.4), channel_id=1, source_target_pairs={{0,128},{32,160},{64,192},{96,224},{128,0},{160,32},{192,64},{224,... | collective-permute-start | bytes 147464 | tf_op jit(solution)/shard_map/ppermute | solution.py:571
  51.1 5.0 %collective-permute-start.7 = (bf16[2,48,256]{2,1,0:T(8,128)(2,1)S(1)}, bf16[2,48,256]{2,1,0:T(8,128)(2,1)S(1)}, u32[]{:S(2)}, u32[]{:S(2)}) collective-permute-start(bf16[2,48,256]{2,1,0:T(8,128)(2,1)S(1)} %pad_maximum_fusion.5), channel_id=1, source_target_pairs={{0,64},{32,96},{64,128},{96,160},{128,192},{160,224},{192,0},{224,... | collective-permute-start | bytes 147464 | tf_op jit(solution)/shard_map/ppermute | solution.py:571

commit v4 on v3

--- a/solution.py
+++ b/solution.py
@@ -54,11 +54,10 @@
             tails = []
             for f in range(FIELDS):
                 x = held[3 * pair + f].astype(F32)
-                rows[pl.ds(3 * pair + f, OWNERS, stride=32), :] = x[:, 0:128]
+                rows[k, pl.ds(pair % 2 * 3 + f, OWNERS, stride=8), :] = x[:, 0:128]
                 tails.append(jnp.concatenate([x[:, 128:COLS], jnp.zeros((OWNERS, 128 - TAIL), F32)], axis=1))
-            rows[pl.ds(24 + pair, OWNERS, stride=32), :] = join_tails(*tails)
-    for j in range(OWNERS):
-        o_ref[j] = rows[32 * j : 32 * j + 32, :].astype(BF16)
+            rows[k, pl.ds(6 + pair % 2, OWNERS, stride=8), :] = join_tails(*tails)
+        o_ref[:, 8 * k : 8 * k + 8, :] = rows[k].reshape(OWNERS, 8, 128).astype(BF16)
     for fetch in fetches:
         fetch.wait()
 
@@ -77,7 +76,7 @@
         scratch_shapes=[
             pltpu.VMEM((24, OWNERS, COLS), BF16),
             pltpu.SemaphoreType.DMA((4,)),
-            pltpu.VMEM((1024, 128), F32),
+            pltpu.VMEM((4, OWNERS * 8, 128), F32),
             pltpu.SemaphoreType.DMA((2,)),
         ],
         compiler_params=vmem_params(4),
@@ -86,21 +85,34 @@
     )(pltpu.with_memory_space_constraint(x, pltpu.HBM), spec, legendre)
 
 
-def unpack_kernel(x_ref, o_ref, rows):
-    for j in range(OWNERS):
-        rows[32 * j : 32 * j + 32, :] = x_ref[j].astype(F32)
-    for pair in range(8):
-        joined = rows[pl.ds(24 + pair, OWNERS, stride=32), :]
-        for f in range(FIELDS):
-            o_ref[3 * pair + f, :, 0:128] = rows[pl.ds(3 * pair + f, OWNERS, stride=32), :].astype(BF16)
-            o_ref[3 * pair + f, :, 128:COLS] = tail_of(joined, f)[:, 0:TAIL].astype(BF16)
+def unpack_kernel(x_ref, o_ref, rows, held, written):
+    copies = []
+    for lat in range(4):
+        rows[lat] = x_ref[:, 8 * lat : 8 * lat + 8, :].astype(F32).reshape(OWNERS * 8, 128)
+        for h in range(2):
+            joined = rows[lat, pl.ds(6 + h, OWNERS, stride=8), :]
+            for f in range(FIELDS):
+                own = rows[lat, pl.ds(3 * h + f, OWNERS, stride=8), :]
+                held[6 * lat + 3 * h + f, :, 0:128] = own.astype(BF16)
+                held[6 * lat + 3 * h + f, :, 128:COLS] = tail_of(joined, f)[:, 0:TAIL].astype(BF16)
+        part = pl.ds(6 * lat, 6)
+        copies.append(pltpu.make_async_copy(held.at[part], o_ref.at[part], written.at[lat]))
+        copies[lat].start()
+    for copy in copies:
+        copy.wait()
 
 
 def unpack_rows(x):
     return pl.pallas_call(
         unpack_kernel,
-        out_shape=jax.ShapeDtypeStruct((24, OWNERS, COLS), BF16),
-        scratch_shapes=[pltpu.VMEM((1024, 128), F32)],
+        in_specs=[pl.BlockSpec(memory_space=pltpu.VMEM)],
+        out_specs=pl.BlockSpec(memory_space=pltpu.HBM),
+        out_shape=pltpu.HBM((24, OWNERS, COLS), BF16),
+        scratch_shapes=[
+            pltpu.VMEM((4, OWNERS * 8, 128), F32),
+            pltpu.VMEM((24, OWNERS, COLS), BF16),
+            pltpu.SemaphoreType.DMA((4,)),
+        ],
         compiler_params=vmem_params(4),
         cost_estimate=pl.CostEstimate(flops=0, bytes_accessed=800_000, transcendentals=0),
         name="unpack_rows",
@@ -278,19 +290,25 @@
             wave_row[:, 128 * k : 128 * k + 128] = tile
             factor_ref[:, 128 * k : 128 * k + 128] = jnp.where(tile == 0.0, 1.0, 2.0)
 
-    length = (5012 + 16 * me + 4 * lat).astype(F32)
-    length = jnp.full((8, WAVES), length, F32)
+    length = jnp.full((1, 1), (5012 + 16 * me + 4 * lat).astype(F32), F32)
     wave = wave_row[...]
     eight = lax.broadcasted_iota(jnp.int32, (8, WAVES), 0).astype(F32)
     low_c, low_s = cos_sin(wave * (eight * COLS), length)
-    high_c, high_s = cos_sin(wave * (eight * (8 * COLS)), length)
+    single = lax.broadcasted_iota(jnp.int32, (8, WAVES), 0)
+    steps = jnp.where(single < 4, single * (8 * COLS), (single - 4) * 64).astype(F32)
+    step_c, step_s = cos_sin(wave * steps, length)
+    high_c, high_s = step_c, step_s
     for k in range(4):
         hc, hs = high_c[k : k + 1, :], high_s[k : k + 1, :]
         outer_ref[0, 0, 8 * k : 8 * k + 8, :] = low_c * hc - low_s * hs
         outer_ref[0, 1, 8 * k : 8 * k + 8, :] = low_s * hc + low_c * hs
     low_c, low_s = cos_sin(wave * eight, length)
+    first_c, first_s = cos_sin(wave * (eight * 8.0), length)
     for block in range(3):
-        high_c, high_s = cos_sin(wave * (eight * 8.0 + 64.0 * block), length)
+        high_c, high_s = first_c, first_s
+        if block:
+            sc, ss = step_c[4 + block : 5 + block, :], step_s[4 + block : 5 + block, :]
+            high_c, high_s = first_c * sc - first_s * ss, first_s * sc + first_c * ss
         for k in range(0, 8, 2):
             base = 64 * block + 8 * k
             if base >= BROWS:
@@ -389,7 +407,7 @@
     for r in range(6):
         value = jnp.where(inside, rows[32 * r : 32 * r + 32, :], 0.0).astype(BF16).astype(F32)
         values[32 * r : 32 * r + 32, :] = value
-        grid_rows[pl.ds(lat * 6 + r, OWNERS, stride=32), :] = value[:, 0:128]
+        grid_rows[pl.ds(r, OWNERS, stride=8), :] = value[:, 0:128]
     for h in range(2):
         tails = [
             jnp.concatenate(
@@ -397,14 +415,15 @@
             )
             for r in range(3 * h, 3 * h + 3)
         ]
-        grid_rows[pl.ds(24 + lat * 2 + h, OWNERS, stride=32), :] = join_tails(*tails)
+        grid_rows[pl.ds(6 + h, OWNERS, stride=8), :] = join_tails(*tails)
+    send_ref[...] = grid_rows[...].reshape(OWNERS, 8, 128).astype(BF16)
     for r in range(6):
         h, f = r // 3, r % 3
         other = h * 3 + (f + 1) % 3
         product = values[32 * r : 32 * r + 32, :] * values[32 * other : 32 * other + 32, :]
-        tail = tail_of(force_rows[pl.ds(24 + lat * 2 + h, OWNERS, stride=32), :], f)
+        tail = tail_of(force_rows[pl.ds(lat * 8 + 6 + h, OWNERS, stride=32), :], f)
         force = jnp.concatenate(
-            [force_rows[pl.ds(lat * 6 + r, OWNERS, stride=32), :], tail[:, 0 : BROWS - 128]], axis=1
+            [force_rows[pl.ds(lat * 8 + r, OWNERS, stride=32), :], tail[:, 0 : BROWS - 128]], axis=1
         )
         samples[32 * r : 32 * r + 32, :] = jnp.where(inside, product + force, 0.0).astype(BF16)
     length = jnp.full((1, 256), (5012 + 16 * me + 4 * lat).astype(F32), F32)
@@ -426,8 +445,6 @@
 
     @pl.when(lat == 3)
     def _():
-        for j in range(OWNERS):
-            send_ref[j] = grid_rows[32 * j : 32 * j + 32, :].astype(BF16)
         for d, ref in enumerate((own_ref, other_ref)):
             for s in range(4):
                 for w in range(2):
@@ -453,7 +470,7 @@
                 pl.BlockSpec(memory_space=pltpu.HBM),
             ],
             out_specs=[
-                pl.BlockSpec((OWNERS, 32, 128), lambda i, *_: (0, 0, 0)),
+                pl.BlockSpec((OWNERS, 8, 128), lambda i, *_: (0, i, 0)),
                 pl.BlockSpec((4, 48, 256), lambda i, *_: (0, 0, 0)),
                 pl.BlockSpec((4, 48, 256), lambda i, *_: (0, 0, 0)),
                 pl.BlockSpec(memory_space=pltpu.VMEM),
@@ -462,7 +479,7 @@
                 pltpu.SemaphoreType.DMA,
                 pltpu.VMEM((48, WAVES), F32),
                 pltpu.VMEM((192, 2 * WAVES), BF16),
-                pltpu.VMEM((1024, 128), F32),
+                pltpu.VMEM((OWNERS * 8, 128), F32),
                 pltpu.VMEM((1024, 128), F32),
                 pltpu.VMEM((192, BROWS), F32),
                 pltpu.VMEM((192, BROWS), BF16),

time: 63.4 us -> 62.5 us (0.986)
  Pallas kernels: 25 us -> 24.2 us
where the time goes in v4:
time: 62.5 us; the launch traced here: 62.2 us
  starting transfers between devices  29.5 us (47%)
  Pallas kernels  24.2 us (39%)
  waiting for transfers between devices  7.42 us (12%)
  between operations  0.82 us (1%)
    all_to_all x1, starting transfers between devices, per_device(): lax.all_to_all(forcing_send, 'ba', split_axis=0, concat_axis=0, tiled=True)  12 us
    all_to_all x1, starting transfers between devices, per_device(): lax.all_to_all(grid_send, 'ba', split_axis=0, concat_axis=0, tiled=True)  8.61 us
    pallas_call x1, Pallas kernels, transform_rows(): pl.pallas_call(row_kernel, grid_spec=pltpu.PrefetchScalarGridSpec(num_sca...  6.97 us
    ppermute x6, starting transfers between devices, to_chip(): lax.ppermute(value, 'aa', [(i, (i // 2 + distance) % 4 * 2 + i % 2) for i...  5.84 us
    pallas_call x1, Pallas kernels, legendre_direct(): pl.pallas_call(legendre_direct_kernel, grid_spec=pltpu.PrefetchScalarGrid...  5.78 us
    pallas_call x1, Pallas kernels, legendre_inverse(): pl.pallas_call(legendre_inverse_kernel, grid_spec=pltpu.PrefetchScalarGri...  5.33 us
    ppermute x6, waiting for transfers between devices, to_chip(): lax.ppermute(value, 'aa', [(i, (i // 2 + distance) % 4 * 2 + i % 2) for i...  4.5 us
    ppermute x2, starting transfers between devices, to_other_core(): return lax.ppermute(value, 'aa', [(i, i ^ 1) for i in range(8)])  2.98 us
  transfers between devices with their start and end apart: 10, of which 5 were waited for; matrix products, arithmetic and copies ran while one was open for 0% of the time, Pallas kernels for 22%

profile of v4, /device:TPU:1, one launch (start us, length us, event | category | flops | bytes accessed | tf_op | source)
XLA Modules:
  0.0 62.2 jit_solution(7754174374764520433)
XLA Ops:
  0.6 2.7 %pack_rows.1 = (bf16[32,32,128]{2,1,0:T(8,128)(2,1)}, bf16[80,3,2,1288]{3,2,1,0:T(2,128)(2,1)S(1)}, bf16[16,32,1288]{2,1,0:T(8,128)(2,1)S(1)}) custom-call(bf16[24,32,164]{2,1,0:T(8,128)(2,1)} %bitcast.24, bf16[80,3,2,1288]{3,2,1,0:T(2,128)(2,1)} %bitcast.22, bf16[80,32,1288]{2,1,0:T(8,128)(2,1)} %leg_ref.7), custom_call_target="tpu_custom_call" | custom-call | bytes 800000 | tf_op jit(solution)/shard_map/pack_rows/pallas_call | solution.py:67
  3.4 12.0 %all-to-all-start = ((bf16[32,32,128]{2,1,0:T(8,128)(2,1)}), bf16[32,32,128]{2,1,0:T(8,128)(2,1)S(1)}, u32[]{:S(2)}, u32[]{:S(2)}) async-start(bf16[32,32,128]{2,1,0:T(8,128)(2,1)} %get-tuple-element.23), calls=%async_computation | async-start | bytes 524288 | tf_op jit(solution)/shard_map/all_to_all | solution.py:602
  15.4 0.0 copy-start.1
  15.4 0.0 copy-start
  15.4 5.3 %legendre_inverse.1 = bf16[4,2,48,256]{3,2,1,0:T(8,128)(2,1)S(1)} custom-call(s32[640]{0:T(1024)} %pw_ref.3, s32[1]{0:T(128)} %bitcast.me_ref, bf16[80,32,1288]{2,1,0:T(8,128)(2,1)} %leg_ref.7, bf16[16,32,1288]{2,1,0:T(8,128)(2,1)S(1)} %get-tuple-element.21.block_ref, bf16[80,3,2,1288]{3,2,1,0:T(2,128)(2,1)S(1)} %get-tuple-element.22.spec_ref), custom_call_target="tpu_custom_call" | custom-call | flops 211025920 | bytes 9000000 | tf_op jit(solution)/shard_map/legendre_inverse/pallas_call | solution.py:199
  20.8 2.6 %collective-permute-start.2 = (bf16[2,48,256]{2,1,0:T(8,128)(2,1)S(1)}, bf16[2,48,256]{2,1,0:T(8,128)(2,1)S(1)}, u32[]{:S(2)}, u32[]{:S(2)}) collective-permute-start(bf16[2,48,256]{2,1,0:T(8,128)(2,1)S(1)} %get-tuple-element.42), channel_id=1, source_target_pairs={{0,192},{32,224},{64,0},{96,32},{128,64},{160,96},{192,128},{224,1... | collective-permute-start | bytes 147464 | tf_op jit(solution)/shard_map/ppermute | solution.py:588
  23.4 0.5 collective-permute-start.1
  23.9 0.6 collective-permute-start
  24.5 0.1 stack_reshape.3
  24.6 2.0 %all-to-all-done.forcing_ref = bf16[32,32,128]{2,1,0:T(8,128)(2,1)S(1)} async-done(((bf16[32,32,128]{2,1,0:T(8,128)(2,1)}), bf16[32,32,128]{2,1,0:T(8,128)(2,1)S(1)}, u32[]{:S(2)}, u32[]{:S(2)}) %all-to-all-start) | async-done | bytes 262176 | tf_op jit(solution)/shard_map/all_to_all | solution.py:602
  26.6 2.5 %phase_tables.1 = (f32[4,2,32,1280]{3,2,1,0:T(8,128)S(1)}, bf16[4,176,2560]{2,1,0:T(8,128)(2,1)S(1)}, f32[8,1280]{1,0:T(8,128)S(1)}) custom-call(s32[1]{0:T(128)} %bitcast.me_ref, f32[8,2,128]{2,1,0:T(2,128)S(1)} %select_maximum_fusion.waves_ref), custom_call_target="tpu_custom_call" | custom-call | flops 40000000 | bytes 5000000 | tf_op jit(solution)/shard_map/phase_tables/pallas_call | solution.py:326
  29.2 2.5 %collective-permute-start.3 = (bf16[4,48,256]{2,1,0:T(8,128)(2,1)S(1)}, bf16[4,48,256]{2,1,0:T(8,128)(2,1)S(1)}, u32[]{:S(2)}, u32[]{:S(2)}) collective-permute-start(bf16[4,48,256]{2,1,0:T(8,128)(2,1)S(1)} %pad_maximum_fusion.1), channel_id=1, source_target_pairs={{0,32},{32,0},{64,96},{96,64},{128,160},{160,128},{192,224},{224,1... | collective-permute-start | bytes 294920 | tf_op jit(solution)/shard_map/ppermute | solution.py:592
  31.8 0.9 %collective-permute-done.3.got_ref = bf16[4,48,256]{2,1,0:T(8,128)(2,1)S(1)} collective-permute-done((bf16[4,48,256]{2,1,0:T(8,128)(2,1)S(1)}, bf16[4,48,256]{2,1,0:T(8,128)(2,1)S(1)}, u32[]{:S(2)}, u32[]{:S(2)}) %collective-permute-start.3) | collective-permute-done | bytes 98336 | tf_op jit(solution)/shard_map/ppermute | solution.py:592
  32.7 7.0 %transform_rows.1 = (bf16[32,32,128]{2,1,0:T(8,128)(2,1)}, bf16[4,48,256]{2,1,0:T(8,128)(2,1)S(1)}, bf16[4,48,256]{2,1,0:T(8,128)(2,1)S(1)}, bf16[16,32,1288]{2,1,0:T(8,128)(2,1)S(1)}) custom-call(s32[1]{0:T(128)} %bitcast.me_ref, f32[32]{0:T(128)S(1)} %copy-done, bf16[4,48,256]{2,1,0:T(8,128)(2,1)S(1)} %pad_maximum_fusion.kept_ref, ...), custom_call_target="tpu_custom_call" | custom-call | flops 1400000000 | bytes 6000000 | tf_op jit(solution)/shard_map/transform_rows/pallas_call | solution.py:458
  39.7 0.4 collective-permute-start.4
  40.1 8.6 %all-to-all-start.1 = ((bf16[32,32,128]{2,1,0:T(8,128)(2,1)}), bf16[32,32,128]{2,1,0:T(8,128)(2,1)S(1)}, u32[]{:S(2)}, u32[]{:S(2)}) async-start(bf16[32,32,128]{2,1,0:T(8,128)(2,1)} %get-tuple-element.36), calls=%async_computation.1 | async-start | bytes 524288 | tf_op jit(solution)/shard_map/all_to_all | solution.py:616
  48.8 0.4 collective-permute-start.5
  49.2 1.2 %collective-permute-start.6 = (bf16[2,48,256]{2,1,0:T(8,128)(2,1)S(1)}, bf16[2,48,256]{2,1,0:T(8,128)(2,1)S(1)}, u32[]{:S(2)}, u32[]{:S(2)}) collective-permute-start(bf16[2,48,256]{2,1,0:T(8,128)(2,1)S(1)} %pad_maximum_fusion.4), channel_id=1, source_target_pairs={{0,128},{32,160},{64,192},{96,224},{128,0},{160,32},{192,64},{224,... | collective-permute-start | bytes 147464 | tf_op jit(solution)/shard_map/ppermute | solution.py:588
  50.5 0.5 collective-permute-start.7
  51.0 0.8 %collective-permute-done.5.second_ref = bf16[2,48,256]{2,1,0:T(8,128)(2,1)S(1)} collective-permute-done((bf16[2,48,256]{2,1,0:T(8,128)(2,1)S(1)}, bf16[2,48,256]{2,1,0:T(8,128)(2,1)S(1)}, u32[]{:S(2)}, u32[]{:S(2)}) %collective-permute-start.5) | collective-permute-done | bytes 49184 | tf_op jit(solution)/shard_map/ppermute | solution.py:588
  51.8 2.2 %collective-permute-done.6.third_ref = bf16[2,48,256]{2,1,0:T(8,128)(2,1)S(1)} collective-permute-done((bf16[2,48,256]{2,1,0:T(8,128)(2,1)S(1)}, bf16[2,48,256]{2,1,0:T(8,128)(2,1)S(1)}, u32[]{:S(2)}, u32[]{:S(2)}) %collective-permute-start.6) | collective-permute-done | bytes 49184 | tf_op jit(solution)/shard_map/ppermute | solution.py:588
  54.0 1.5 %collective-permute-done.7.fourth_ref = bf16[2,48,256]{2,1,0:T(8,128)(2,1)S(1)} collective-permute-done((bf16[2,48,256]{2,1,0:T(8,128)(2,1)S(1)}, bf16[2,48,256]{2,1,0:T(8,128)(2,1)S(1)}, u32[]{:S(2)}, u32[]{:S(2)}) %collective-permute-start.7) | collective-permute-done | bytes 49184 | tf_op jit(solution)/shard_map/ppermute | solution.py:588
  55.5 5.8 %legendre_direct.1 = bf16[80,3,2,1288]{3,2,1,0:T(2,128)(2,1)} custom-call(s32[640]{0:T(1024)} %pw_ref.3, s32[1]{0:T(128)} %bitcast.me_ref, bf16[2,48,256]{2,1,0:T(8,128)(2,1)S(1)} %pad_maximum_fusion.2.first_ref, bf16[2,48,256]{2,1,0:T(8,128)(2,1)S(1)} %collective-permute-done.5.second_ref, bf16[2,48,256]{2,1,0:T(8,128)(2,1)S(1)} %collective-permute-done.6.third_ref, ...), custom_call_target="tpu_custom_call" | custom-call | flops 211025920 | bytes 9000000 | tf_op jit(solution)/shard_map/legendre_direct/pallas_call | solution.py:565
  61.3 0.9 %unpack_rows.1 = bf16[24,32,164]{2,1,0:T(8,128)(2,1)} custom-call(bf16[32,32,128]{2,1,0:T(8,128)(2,1)S(1)} %all-to-all-done.1.x_ref), custom_call_target="tpu_custom_call" | custom-call | bytes 800000 | tf_op jit(solution)/shard_map/unpack_rows/pallas_call | solution.py:106
  (21 shorter events, 0.2 us)
Async XLA Ops:
  3.4 23.2 %all-to-all-start = ((bf16[32,32,128]{2,1,0:T(8,128)(2,1)}), bf16[32,32,128]{2,1,0:T(8,128)(2,1)S(1)}, u32[]{:S(2)}, u32[]{:S(2)}) async-start(bf16[32,32,128]{2,1,0:T(8,128)(2,1)} %get-tuple-element.23), calls=%async_computation | async-start | bytes 524288 | tf_op jit(solution)/shard_map/all_to_all | solution.py:602
  15.4 9.1 %copy-start.1 = (s32[640]{0:T(1024)S(1)}, s32[640]{0:T(1024)}, u32[]{:S(2)}) copy-start(s32[640]{0:T(1024)} %pw_ref.3) | copy-start | bytes 7684
  15.4 17.3 %copy-start = (f32[32]{0:T(128)S(1)}, f32[32]{0:T(128)}, u32[]{:S(2)}) copy-start(f32[32]{0:T(128)} %weight_ref.1) | copy-start | bytes 388
  20.8 8.3 %collective-permute-start.2 = (bf16[2,48,256]{2,1,0:T(8,128)(2,1)S(1)}, bf16[2,48,256]{2,1,0:T(8,128)(2,1)S(1)}, u32[]{:S(2)}, u32[]{:S(2)}) collective-permute-start(bf16[2,48,256]{2,1,0:T(8,128)(2,1)S(1)} %get-tuple-element.42), channel_id=1, source_target_pairs={{0,192},{32,224},{64,0},{96,32},{128,64},{160,96},{192,128},{224,1... | collective-permute-start | bytes 147464 | tf_op jit(solution)/shard_map/ppermute | solution.py:588
  23.4 5.8 %collective-permute-start.1 = (bf16[2,48,256]{2,1,0:T(8,128)(2,1)S(1)}, bf16[2,48,256]{2,1,0:T(8,128)(2,1)S(1)}, u32[]{:S(2)}, u32[]{:S(2)}) collective-permute-start(bf16[2,48,256]{2,1,0:T(8,128)(2,1)S(1)} %get-tuple-element.43), channel_id=1, source_target_pairs={{0,128},{32,160},{64,192},{96,224},{128,0},{160,32},{192,64},{224,... | collective-permute-start | bytes 147464 | tf_op jit(solution)/shard_map/ppermute | solution.py:588
  23.9 5.3 %collective-permute-start = (bf16[2,48,256]{2,1,0:T(8,128)(2,1)S(1)}, bf16[2,48,256]{2,1,0:T(8,128)(2,1)S(1)}, u32[]{:S(2)}, u32[]{:S(2)}) collective-permute-start(bf16[2,48,256]{2,1,0:T(8,128)(2,1)S(1)} %get-tuple-element.44), channel_id=1, source_target_pairs={{0,64},{32,96},{64,128},{96,160},{128,192},{160,224},{192,0},{224,... | collective-permute-start | bytes 147464 | tf_op jit(solution)/shard_map/ppermute | solution.py:588
  29.2 3.5 %collective-permute-start.3 = (bf16[4,48,256]{2,1,0:T(8,128)(2,1)S(1)}, bf16[4,48,256]{2,1,0:T(8,128)(2,1)S(1)}, u32[]{:S(2)}, u32[]{:S(2)}) collective-permute-start(bf16[4,48,256]{2,1,0:T(8,128)(2,1)S(1)} %pad_maximum_fusion.1), channel_id=1, source_target_pairs={{0,32},{32,0},{64,96},{96,64},{128,160},{160,128},{192,224},{224,1... | collective-permute-start | bytes 294920 | tf_op jit(solution)/shard_map/ppermute | solution.py:592
  39.7 9.1 %collective-permute-start.4 = (bf16[4,48,256]{2,1,0:T(8,128)(2,1)S(1)}, bf16[4,48,256]{2,1,0:T(8,128)(2,1)S(1)}, u32[]{:S(2)}, u32[]{:S(2)}) collective-permute-start(bf16[4,48,256]{2,1,0:T(8,128)(2,1)S(1)} %get-tuple-element.38), channel_id=1, source_target_pairs={{0,32},{32,0},{64,96},{96,64},{128,160},{160,128},{192,224},{224,1... | collective-permute-start | bytes 294920 | tf_op jit(solution)/shard_map/ppermute | solution.py:592
  40.1 21.1 %all-to-all-start.1 = ((bf16[32,32,128]{2,1,0:T(8,128)(2,1)}), bf16[32,32,128]{2,1,0:T(8,128)(2,1)S(1)}, u32[]{:S(2)}, u32[]{:S(2)}) async-start(bf16[32,32,128]{2,1,0:T(8,128)(2,1)} %get-tuple-element.36), calls=%async_computation.1 | async-start | bytes 524288 | tf_op jit(solution)/shard_map/all_to_all | solution.py:616
  48.8 3.0 %collective-permute-start.5 = (bf16[2,48,256]{2,1,0:T(8,128)(2,1)S(1)}, bf16[2,48,256]{2,1,0:T(8,128)(2,1)S(1)}, u32[]{:S(2)}, u32[]{:S(2)}) collective-permute-start(bf16[2,48,256]{2,1,0:T(8,128)(2,1)S(1)} %pad_maximum_fusion.3), channel_id=1, source_target_pairs={{0,192},{32,224},{64,0},{96,32},{128,64},{160,96},{192,128},{224,1... | collective-permute-start | bytes 147464 | tf_op jit(solution)/shard_map/ppermute | solution.py:588
  49.2 4.7 %collective-permute-start.6 = (bf16[2,48,256]{2,1,0:T(8,128)(2,1)S(1)}, bf16[2,48,256]{2,1,0:T(8,128)(2,1)S(1)}, u32[]{:S(2)}, u32[]{:S(2)}) collective-permute-start(bf16[2,48,256]{2,1,0:T(8,128)(2,1)S(1)} %pad_maximum_fusion.4), channel_id=1, source_target_pairs={{0,128},{32,160},{64,192},{96,224},{128,0},{160,32},{192,64},{224,... | collective-permute-start | bytes 147464 | tf_op jit(solution)/shard_map/ppermute | solution.py:588
  50.5 5.0 %collective-permute-start.7 = (bf16[2,48,256]{2,1,0:T(8,128)(2,1)S(1)}, bf16[2,48,256]{2,1,0:T(8,128)(2,1)S(1)}, u32[]{:S(2)}, u32[]{:S(2)}) collective-permute-start(bf16[2,48,256]{2,1,0:T(8,128)(2,1)S(1)} %pad_maximum_fusion.5), channel_id=1, source_target_pairs={{0,64},{32,96},{64,128},{96,160},{128,192},{160,224},{192,0},{224,... | collective-permute-start | bytes 147464 | tf_op jit(solution)/shard_map/ppermute | solution.py:588

commit v5 on v4

--- a/solution.py
+++ b/solution.py
@@ -35,19 +35,15 @@
     return pltpu.roll(joined, 128 - TAIL * field, axis=1) if field else joined
 
 
-def pack_kernel(x_ref, spec_ref, leg_ref, o_ref, spec_out, leg_out, held, arrived, rows, fetched):
-    fetches = (
-        pltpu.make_async_copy(spec_ref, spec_out, fetched.at[0]),
-        pltpu.make_async_copy(leg_ref.at[pl.ds(0, PAIR_BLOCK)], leg_out, fetched.at[1]),
-    )
+def pack_kernel(x_ref, spec_ref, o_ref, spec_out, held, arrived, rows, fetched):
+    fetch = pltpu.make_async_copy(spec_ref, spec_out, fetched)
 
     def part(k):
         return pltpu.make_async_copy(x_ref.at[pl.ds(6 * k, 6)], held.at[pl.ds(6 * k, 6)], arrived.at[k])
 
     for k in range(4):
         part(k).start()
-    for fetch in fetches:
-        fetch.start()
+    fetch.start()
     for k in range(4):
         part(k).wait()
         for pair in (2 * k, 2 * k + 1):
@@ -58,31 +54,29 @@
                 tails.append(jnp.concatenate([x[:, 128:COLS], jnp.zeros((OWNERS, 128 - TAIL), F32)], axis=1))
             rows[k, pl.ds(6 + pair % 2, OWNERS, stride=8), :] = join_tails(*tails)
         o_ref[:, 8 * k : 8 * k + 8, :] = rows[k].reshape(OWNERS, 8, 128).astype(BF16)
-    for fetch in fetches:
-        fetch.wait()
-
-
-def pack_rows(x, spec, legendre):
-    slots = legendre.shape[2]
+    fetch.wait()
+
+
+def pack_rows(x, spec):
+    slots = spec.shape[3]
     return pl.pallas_call(
         pack_kernel,
-        in_specs=[pl.BlockSpec(memory_space=pltpu.HBM)] * 3,
-        out_specs=[pl.BlockSpec(memory_space=pltpu.VMEM)] * 3,
+        in_specs=[pl.BlockSpec(memory_space=pltpu.HBM)] * 2,
+        out_specs=[pl.BlockSpec(memory_space=pltpu.VMEM)] * 2,
         out_shape=[
             jax.ShapeDtypeStruct((OWNERS, 32, 128), BF16),
             pltpu.VMEM((PAIRS, FIELDS, 2, slots), BF16),
-            pltpu.VMEM((PAIR_BLOCK, 32, slots), BF16),
         ],
         scratch_shapes=[
             pltpu.VMEM((24, OWNERS, COLS), BF16),
             pltpu.SemaphoreType.DMA((4,)),
             pltpu.VMEM((4, OWNERS * 8, 128), F32),
-            pltpu.SemaphoreType.DMA((2,)),
+            pltpu.SemaphoreType.DMA,
         ],
         compiler_params=vmem_params(4),
         cost_estimate=pl.CostEstimate(flops=0, bytes_accessed=800_000, transcendentals=0),
         name="pack_rows",
-    )(pltpu.with_memory_space_constraint(x, pltpu.HBM), spec, legendre)
+    )(pltpu.with_memory_space_constraint(x, pltpu.HBM), spec)
 
 
 def unpack_kernel(x_ref, o_ref, rows, held, written):
@@ -124,13 +118,13 @@
     return pltpu.make_async_copy(leg_ref.at[rows], held.at[rows], arrived.at[k])
 
 
-def legendre_start(leg_ref, held, arrived):
-    for k in range(1, PAIRS // PAIR_BLOCK):
+def legendre_start(leg_ref, held, arrived, first):
+    for k in range(first, PAIRS // PAIR_BLOCK):
         legendre_block(leg_ref, held, arrived, k).start()
 
 
 def legendre_inverse_kernel(
-    pw_ref, me_ref, leg_ref, block_ref, spec_ref, out_ref, held, arrived, by_pair, by_lat
+    pw_ref, me_ref, leg_ref, spec_ref, out_ref, held, arrived, by_pair, by_lat
 ):
     step = pl.program_id(0)
     slots = leg_ref.shape[2]
@@ -167,13 +161,10 @@
 
     @pl.when(step == 0)
     def _():
-        legendre_start(leg_ref, held, arrived)
-        sum_block(lambda k: block_ref[k])
-
-    @pl.when(step > 0)
-    def _():
-        legendre_block(leg_ref, held, arrived, step).wait()
-        sum_block(lambda k: held[step * PAIR_BLOCK + k])
+        legendre_start(leg_ref, held, arrived, 0)
+
+    legendre_block(leg_ref, held, arrived, step).wait()
+    sum_block(lambda k: held[step * PAIR_BLOCK + k])
 
     @pl.when(step == pl.num_programs(0) - 1)
     def _():
@@ -194,7 +185,7 @@
                 out_ref[s, d, :, 128:256] = by_lat[1, rows, :].astype(BF16)
 
 
-def legendre_inverse(pair_wave, me, legendre, block, spec):
+def legendre_inverse(pair_wave, me, legendre, spec):
     slots = legendre.shape[2]
     return pl.pallas_call(
         legendre_inverse_kernel,
@@ -203,7 +194,6 @@
             grid=(PAIRS // PAIR_BLOCK,),
             in_specs=[
                 pl.BlockSpec(memory_space=pltpu.HBM),
-                pl.BlockSpec(memory_space=pltpu.VMEM),
                 pl.BlockSpec(memory_space=pltpu.VMEM),
             ],
             out_specs=pl.BlockSpec((4, 2, 48, 256), lambda i, *_: (0, 0, 0, 0)),
@@ -218,7 +208,7 @@
         compiler_params=vmem_params(16),
         cost_estimate=pl.CostEstimate(flops=2 * 80 * 32 * 32 * 1288, bytes_accessed=9_000_000, transcendentals=0),
         name="legendre_inverse",
-    )(pair_wave, me, legendre, block, spec)
+    )(pair_wave, me, legendre, spec)
 
 
 def join_pieces(pieces):
@@ -516,7 +506,7 @@
 
     @pl.when(step == 0)
     def _():
-        legendre_start(leg_ref, held, arrived)
+        legendre_start(leg_ref, held, arrived, 1)
         x, core = me_ref[0] // 2, me_ref[0] % 2
         for s, ref in enumerate((first_ref, second_ref, third_ref, fourth_ref)):
             for d in range(2):
@@ -598,9 +588,9 @@
     wave_table = pltpu.with_memory_space_constraint(pair_wave, pltpu.HBM)
     spec = jnp.swapaxes(spec_in.reshape(PAIRS, 2, FIELDS, -1), 1, 2)
     spec = pltpu.with_memory_space_constraint(spec, pltpu.HBM)
-    forcing_send, spec, block = pack_rows(forcing.reshape(24, OWNERS, COLS), spec, legendre)
+    forcing_send, spec = pack_rows(forcing.reshape(24, OWNERS, COLS), spec)
     forcing_here = lax.all_to_all(forcing_send, "ba", split_axis=0, concat_axis=0, tiled=True)
-    fourier = legendre_inverse(wave_table, me, legendre, block, spec)
+    fourier = legendre_inverse(wave_table, me, legendre, spec)
     pairs = pair_wave.astype(F32).reshape(8, PAIRS)
     waves = jnp.pad(jnp.stack([pairs, TRUNCATION - pairs], axis=1), ((0, 0), (0, 0), (0, 48)))
     waves, forcing_here = lax.optimization_barrier((waves, forcing_here))

time: 62.5 us -> 62.2 us (level)
  no operation moved by 1% of the time
where the time goes in v5:
time: 62.2 us; the launch traced here: 61.9 us
  starting transfers between devices  29.6 us (48%)
  Pallas kernels  23.9 us (38%)
  waiting for transfers between devices  7.28 us (12%)
  between operations  0.82 us (1%)
    all_to_all x1, starting transfers between devices, per_device(): lax.all_to_all(forcing_send, 'ba', split_axis=0, concat_axis=0, tiled=True)  12 us
    all_to_all x1, starting transfers between devices, per_device(): lax.all_to_all(grid_send, 'ba', split_axis=0, concat_axis=0, tiled=True)  8.75 us
    pallas_call x1, Pallas kernels, transform_rows(): pl.pallas_call(row_kernel, grid_spec=pltpu.PrefetchScalarGridSpec(num_sca...  6.97 us
    ppermute x6, starting transfers between devices, to_chip(): lax.ppermute(value, 'aa', [(i, (i // 2 + distance) % 4 * 2 + i % 2) for i...  5.84 us
    pallas_call x1, Pallas kernels, legendre_direct(): pl.pallas_call(legendre_direct_kernel, grid_spec=pltpu.PrefetchScalarGrid...  5.78 us
    pallas_call x1, Pallas kernels, legendre_inverse(): pl.pallas_call(legendre_inverse_kernel, grid_spec=pltpu.PrefetchScalarGri...  5.47 us
    ppermute x6, waiting for transfers between devices, to_chip(): lax.ppermute(value, 'aa', [(i, (i // 2 + distance) % 4 * 2 + i % 2) for i...  4.5 us
    ppermute x2, starting transfers between devices, to_other_core(): return lax.ppermute(value, 'aa', [(i, i ^ 1) for i in range(8)])  2.98 us
  transfers between devices with their start and end apart: 10, of which 5 were waited for; matrix products, arithmetic and copies ran while one was open for 0% of the time, Pallas kernels for 22%

profile of v5, /device:TPU:1, one launch (start us, length us, event | category | flops | bytes accessed | tf_op | source)
XLA Modules:
  0.0 61.9 jit_solution(6115494214974686798)
XLA Ops:
  0.6 2.3 %pack_rows.1 = (bf16[32,32,128]{2,1,0:T(8,128)(2,1)}, bf16[80,3,2,1288]{3,2,1,0:T(2,128)(2,1)S(1)}) custom-call(bf16[24,32,164]{2,1,0:T(8,128)(2,1)} %bitcast.25, bf16[80,3,2,1288]{3,2,1,0:T(2,128)(2,1)} %bitcast.23), custom_call_target="tpu_custom_call" | custom-call | bytes 800000 | tf_op jit(solution)/shard_map/pack_rows/pallas_call | solution.py:62
  2.9 12.0 %all-to-all-start = ((bf16[32,32,128]{2,1,0:T(8,128)(2,1)}), bf16[32,32,128]{2,1,0:T(8,128)(2,1)S(1)}, u32[]{:S(2)}, u32[]{:S(2)}) async-start(bf16[32,32,128]{2,1,0:T(8,128)(2,1)} %get-tuple-element.21), calls=%async_computation | async-start | bytes 524288 | tf_op jit(solution)/shard_map/all_to_all | solution.py:592
  15.0 0.0 copy-start.1
  15.0 5.5 %legendre_inverse.1 = bf16[4,2,48,256]{3,2,1,0:T(8,128)(2,1)S(1)} custom-call(s32[640]{0:T(1024)} %pw_ref.3, s32[1]{0:T(128)} %bitcast.me_ref, bf16[80,32,1288]{2,1,0:T(8,128)(2,1)} %leg_ref.5, bf16[80,3,2,1288]{3,2,1,0:T(2,128)(2,1)S(1)} %get-tuple-element.20.spec_ref), custom_call_target="tpu_custom_call" | custom-call | flops 211025920 | bytes 9000000 | tf_op jit(solution)/shard_map/legendre_inverse/pallas_call | solution.py:190
  20.5 0.0 copy-start
  20.5 2.6 %collective-permute-start.2 = (bf16[2,48,256]{2,1,0:T(8,128)(2,1)S(1)}, bf16[2,48,256]{2,1,0:T(8,128)(2,1)S(1)}, u32[]{:S(2)}, u32[]{:S(2)}) collective-permute-start(bf16[2,48,256]{2,1,0:T(8,128)(2,1)S(1)} %get-tuple-element.40), channel_id=1, source_target_pairs={{0,192},{32,224},{64,0},{96,32},{128,64},{160,96},{192,128},{224,1... | collective-permute-start | bytes 147464 | tf_op jit(solution)/shard_map/ppermute | solution.py:578
  23.1 0.5 collective-permute-start.1
  23.6 0.6 collective-permute-start
  24.2 0.1 stack_reshape.3
  24.3 1.8 %all-to-all-done.forcing_ref = bf16[32,32,128]{2,1,0:T(8,128)(2,1)S(1)} async-done(((bf16[32,32,128]{2,1,0:T(8,128)(2,1)}), bf16[32,32,128]{2,1,0:T(8,128)(2,1)S(1)}, u32[]{:S(2)}, u32[]{:S(2)}) %all-to-all-start) | async-done | bytes 262176 | tf_op jit(solution)/shard_map/all_to_all | solution.py:592
  26.2 2.5 %phase_tables.1 = (f32[4,2,32,1280]{3,2,1,0:T(8,128)S(1)}, bf16[4,176,2560]{2,1,0:T(8,128)(2,1)S(1)}, f32[8,1280]{1,0:T(8,128)S(1)}) custom-call(s32[1]{0:T(128)} %bitcast.me_ref, f32[8,2,128]{2,1,0:T(2,128)S(1)} %select_maximum_fusion.waves_ref), custom_call_target="tpu_custom_call" | custom-call | flops 40000000 | bytes 5000000 | tf_op jit(solution)/shard_map/phase_tables/pallas_call | solution.py:316
  28.8 2.5 %collective-permute-start.3 = (bf16[4,48,256]{2,1,0:T(8,128)(2,1)S(1)}, bf16[4,48,256]{2,1,0:T(8,128)(2,1)S(1)}, u32[]{:S(2)}, u32[]{:S(2)}) collective-permute-start(bf16[4,48,256]{2,1,0:T(8,128)(2,1)S(1)} %pad_maximum_fusion.1), channel_id=1, source_target_pairs={{0,32},{32,0},{64,96},{96,64},{128,160},{160,128},{192,224},{224,1... | collective-permute-start | bytes 294920 | tf_op jit(solution)/shard_map/ppermute | solution.py:582
  31.3 0.9 %collective-permute-done.3.got_ref = bf16[4,48,256]{2,1,0:T(8,128)(2,1)S(1)} collective-permute-done((bf16[4,48,256]{2,1,0:T(8,128)(2,1)S(1)}, bf16[4,48,256]{2,1,0:T(8,128)(2,1)S(1)}, u32[]{:S(2)}, u32[]{:S(2)}) %collective-permute-start.3) | collective-permute-done | bytes 98336 | tf_op jit(solution)/shard_map/ppermute | solution.py:582
  32.3 7.0 %transform_rows.1 = (bf16[32,32,128]{2,1,0:T(8,128)(2,1)}, bf16[4,48,256]{2,1,0:T(8,128)(2,1)S(1)}, bf16[4,48,256]{2,1,0:T(8,128)(2,1)S(1)}, bf16[16,32,1288]{2,1,0:T(8,128)(2,1)S(1)}) custom-call(s32[1]{0:T(128)} %bitcast.me_ref, f32[32]{0:T(128)S(1)} %copy-done, bf16[4,48,256]{2,1,0:T(8,128)(2,1)S(1)} %pad_maximum_fusion.kept_ref, ...), custom_call_target="tpu_custom_call" | custom-call | flops 1400000000 | bytes 6000000 | tf_op jit(solution)/shard_map/transform_rows/pallas_call | solution.py:448
  39.2 0.4 collective-permute-start.4
  39.7 8.7 %all-to-all-start.1 = ((bf16[32,32,128]{2,1,0:T(8,128)(2,1)}), bf16[32,32,128]{2,1,0:T(8,128)(2,1)S(1)}, u32[]{:S(2)}, u32[]{:S(2)}) async-start(bf16[32,32,128]{2,1,0:T(8,128)(2,1)} %get-tuple-element.34), calls=%async_computation.1 | async-start | bytes 524288 | tf_op jit(solution)/shard_map/all_to_all | solution.py:606
  48.5 0.4 collective-permute-start.5
  48.9 1.2 %collective-permute-start.6 = (bf16[2,48,256]{2,1,0:T(8,128)(2,1)S(1)}, bf16[2,48,256]{2,1,0:T(8,128)(2,1)S(1)}, u32[]{:S(2)}, u32[]{:S(2)}) collective-permute-start(bf16[2,48,256]{2,1,0:T(8,128)(2,1)S(1)} %pad_maximum_fusion.4), channel_id=1, source_target_pairs={{0,128},{32,160},{64,192},{96,224},{128,0},{160,32},{192,64},{224,... | collective-permute-start | bytes 147464 | tf_op jit(solution)/shard_map/ppermute | solution.py:578
  50.2 0.5 collective-permute-start.7
  50.7 0.8 %collective-permute-done.5.second_ref = bf16[2,48,256]{2,1,0:T(8,128)(2,1)S(1)} collective-permute-done((bf16[2,48,256]{2,1,0:T(8,128)(2,1)S(1)}, bf16[2,48,256]{2,1,0:T(8,128)(2,1)S(1)}, u32[]{:S(2)}, u32[]{:S(2)}) %collective-permute-start.5) | collective-permute-done | bytes 49184 | tf_op jit(solution)/shard_map/ppermute | solution.py:578
  51.5 2.2 %collective-permute-done.6.third_ref = bf16[2,48,256]{2,1,0:T(8,128)(2,1)S(1)} collective-permute-done((bf16[2,48,256]{2,1,0:T(8,128)(2,1)S(1)}, bf16[2,48,256]{2,1,0:T(8,128)(2,1)S(1)}, u32[]{:S(2)}, u32[]{:S(2)}) %collective-permute-start.6) | collective-permute-done | bytes 49184 | tf_op jit(solution)/shard_map/ppermute | solution.py:578
  53.7 1.5 %collective-permute-done.7.fourth_ref = bf16[2,48,256]{2,1,0:T(8,128)(2,1)S(1)} collective-permute-done((bf16[2,48,256]{2,1,0:T(8,128)(2,1)S(1)}, bf16[2,48,256]{2,1,0:T(8,128)(2,1)S(1)}, u32[]{:S(2)}, u32[]{:S(2)}) %collective-permute-start.7) | collective-permute-done | bytes 49184 | tf_op jit(solution)/shard_map/ppermute | solution.py:578
  55.2 5.8 %legendre_direct.1 = bf16[80,3,2,1288]{3,2,1,0:T(2,128)(2,1)} custom-call(s32[640]{0:T(1024)} %pw_ref.3, s32[1]{0:T(128)} %bitcast.me_ref, bf16[2,48,256]{2,1,0:T(8,128)(2,1)S(1)} %pad_maximum_fusion.2.first_ref, bf16[2,48,256]{2,1,0:T(8,128)(2,1)S(1)} %collective-permute-done.5.second_ref, bf16[2,48,256]{2,1,0:T(8,128)(2,1)S(1)} %collective-permute-done.6.third_ref, ...), custom_call_target="tpu_custom_call" | custom-call | flops 211025920 | bytes 9000000 | tf_op jit(solution)/shard_map/legendre_direct/pallas_call | solution.py:555
  61.0 0.9 %unpack_rows.1 = bf16[24,32,164]{2,1,0:T(8,128)(2,1)} custom-call(bf16[32,32,128]{2,1,0:T(8,128)(2,1)S(1)} %all-to-all-done.1.x_ref), custom_call_target="tpu_custom_call" | custom-call | bytes 800000 | tf_op jit(solution)/shard_map/unpack_rows/pallas_call | solution.py:100
  (21 shorter events, 0.2 us)
Async XLA Ops:
  2.9 23.2 %all-to-all-start = ((bf16[32,32,128]{2,1,0:T(8,128)(2,1)}), bf16[32,32,128]{2,1,0:T(8,128)(2,1)S(1)}, u32[]{:S(2)}, u32[]{:S(2)}) async-start(bf16[32,32,128]{2,1,0:T(8,128)(2,1)} %get-tuple-element.21), calls=%async_computation | async-start | bytes 524288 | tf_op jit(solution)/shard_map/all_to_all | solution.py:592
  15.0 9.2 %copy-start.1 = (s32[640]{0:T(1024)S(1)}, s32[640]{0:T(1024)}, u32[]{:S(2)}) copy-start(s32[640]{0:T(1024)} %pw_ref.3) | copy-start | bytes 7684
  20.5 11.8 %copy-start = (f32[32]{0:T(128)S(1)}, f32[32]{0:T(128)}, u32[]{:S(2)}) copy-start(f32[32]{0:T(128)} %weight_ref.1) | copy-start | bytes 388
  20.5 8.2 %collective-permute-start.2 = (bf16[2,48,256]{2,1,0:T(8,128)(2,1)S(1)}, bf16[2,48,256]{2,1,0:T(8,128)(2,1)S(1)}, u32[]{:S(2)}, u32[]{:S(2)}) collective-permute-start(bf16[2,48,256]{2,1,0:T(8,128)(2,1)S(1)} %get-tuple-element.40), channel_id=1, source_target_pairs={{0,192},{32,224},{64,0},{96,32},{128,64},{160,96},{192,128},{224,1... | collective-permute-start | bytes 147464 | tf_op jit(solution)/shard_map/ppermute | solution.py:578
  23.1 5.6 %collective-permute-start.1 = (bf16[2,48,256]{2,1,0:T(8,128)(2,1)S(1)}, bf16[2,48,256]{2,1,0:T(8,128)(2,1)S(1)}, u32[]{:S(2)}, u32[]{:S(2)}) collective-permute-start(bf16[2,48,256]{2,1,0:T(8,128)(2,1)S(1)} %get-tuple-element.41), channel_id=1, source_target_pairs={{0,128},{32,160},{64,192},{96,224},{128,0},{160,32},{192,64},{224,... | collective-permute-start | bytes 147464 | tf_op jit(solution)/shard_map/ppermute | solution.py:578
  23.6 5.1 %collective-permute-start = (bf16[2,48,256]{2,1,0:T(8,128)(2,1)S(1)}, bf16[2,48,256]{2,1,0:T(8,128)(2,1)S(1)}, u32[]{:S(2)}, u32[]{:S(2)}) collective-permute-start(bf16[2,48,256]{2,1,0:T(8,128)(2,1)S(1)} %get-tuple-element.42), channel_id=1, source_target_pairs={{0,64},{32,96},{64,128},{96,160},{128,192},{160,224},{192,0},{224,... | collective-permute-start | bytes 147464 | tf_op jit(solution)/shard_map/ppermute | solution.py:578
  28.8 3.5 %collective-permute-start.3 = (bf16[4,48,256]{2,1,0:T(8,128)(2,1)S(1)}, bf16[4,48,256]{2,1,0:T(8,128)(2,1)S(1)}, u32[]{:S(2)}, u32[]{:S(2)}) collective-permute-start(bf16[4,48,256]{2,1,0:T(8,128)(2,1)S(1)} %pad_maximum_fusion.1), channel_id=1, source_target_pairs={{0,32},{32,0},{64,96},{96,64},{128,160},{160,128},{192,224},{224,1... | collective-permute-start | bytes 294920 | tf_op jit(solution)/shard_map/ppermute | solution.py:582
  39.2 9.2 %collective-permute-start.4 = (bf16[4,48,256]{2,1,0:T(8,128)(2,1)S(1)}, bf16[4,48,256]{2,1,0:T(8,128)(2,1)S(1)}, u32[]{:S(2)}, u32[]{:S(2)}) collective-permute-start(bf16[4,48,256]{2,1,0:T(8,128)(2,1)S(1)} %get-tuple-element.36), channel_id=1, source_target_pairs={{0,32},{32,0},{64,96},{96,64},{128,160},{160,128},{192,224},{224,1... | collective-permute-start | bytes 294920 | tf_op jit(solution)/shard_map/ppermute | solution.py:582
  39.7 21.3 %all-to-all-start.1 = ((bf16[32,32,128]{2,1,0:T(8,128)(2,1)}), bf16[32,32,128]{2,1,0:T(8,128)(2,1)S(1)}, u32[]{:S(2)}, u32[]{:S(2)}) async-start(bf16[32,32,128]{2,1,0:T(8,128)(2,1)} %get-tuple-element.34), calls=%async_computation.1 | async-start | bytes 524288 | tf_op jit(solution)/shard_map/all_to_all | solution.py:606
  48.5 3.0 %collective-permute-start.5 = (bf16[2,48,256]{2,1,0:T(8,128)(2,1)S(1)}, bf16[2,48,256]{2,1,0:T(8,128)(2,1)S(1)}, u32[]{:S(2)}, u32[]{:S(2)}) collective-permute-start(bf16[2,48,256]{2,1,0:T(8,128)(2,1)S(1)} %pad_maximum_fusion.3), channel_id=1, source_target_pairs={{0,192},{32,224},{64,0},{96,32},{128,64},{160,96},{192,128},{224,1... | collective-permute-start | bytes 147464 | tf_op jit(solution)/shard_map/ppermute | solution.py:578
  48.9 4.7 %collective-permute-start.6 = (bf16[2,48,256]{2,1,0:T(8,128)(2,1)S(1)}, bf16[2,48,256]{2,1,0:T(8,128)(2,1)S(1)}, u32[]{:S(2)}, u32[]{:S(2)}) collective-permute-start(bf16[2,48,256]{2,1,0:T(8,128)(2,1)S(1)} %pad_maximum_fusion.4), channel_id=1, source_target_pairs={{0,128},{32,160},{64,192},{96,224},{128,0},{160,32},{192,64},{224,... | collective-permute-start | bytes 147464 | tf_op jit(solution)/shard_map/ppermute | solution.py:578
  50.2 5.0 %collective-permute-start.7 = (bf16[2,48,256]{2,1,0:T(8,128)(2,1)S(1)}, bf16[2,48,256]{2,1,0:T(8,128)(2,1)S(1)}, u32[]{:S(2)}, u32[]{:S(2)}) collective-permute-start(bf16[2,48,256]{2,1,0:T(8,128)(2,1)S(1)} %pad_maximum_fusion.5), channel_id=1, source_target_pairs={{0,64},{32,96},{64,128},{96,160},{128,192},{160,224},{192,0},{224,... | collective-permute-start | bytes 147464 | tf_op jit(solution)/shard_map/ppermute | solution.py:578

commit v6 on v5

--- a/solution.py
+++ b/solution.py
@@ -16,7 +16,7 @@
 OWNERS = 32
 BROWS = 176
 TAIL = COLS - 128
-PAIR_BLOCK = 16
+PAIR_BLOCK = 20
 F32 = jnp.float32
 BF16 = jnp.bfloat16
 NT = (((1,), (1,)), ((), ()))

time: 62.2 us -> 62.2 us (level)
  no operation moved by 1% of the time
where the time goes in v6:
time: 62.2 us; the launch traced here: 61.8 us
  starting transfers between devices  29.6 us (48%)
  Pallas kernels  23.8 us (38%)
  waiting for transfers between devices  7.31 us (12%)
  between operations  0.82 us (1%)
    all_to_all x1, starting transfers between devices, per_device(): lax.all_to_all(forcing_send, 'ba', split_axis=0, concat_axis=0, tiled=True)  12 us
    all_to_all x1, starting transfers between devices, per_device(): lax.all_to_all(grid_send, 'ba', split_axis=0, concat_axis=0, tiled=True)  8.71 us
    pallas_call x1, Pallas kernels, transform_rows(): pl.pallas_call(row_kernel, grid_spec=pltpu.PrefetchScalarGridSpec(num_sca...  6.97 us
    ppermute x6, starting transfers between devices, to_chip(): lax.ppermute(value, 'aa', [(i, (i // 2 + distance) % 4 * 2 + i % 2) for i...  5.84 us
    pallas_call x1, Pallas kernels, legendre_direct(): pl.pallas_call(legendre_direct_kernel, grid_spec=pltpu.PrefetchScalarGrid...  5.73 us
    pallas_call x1, Pallas kernels, legendre_inverse(): pl.pallas_call(legendre_inverse_kernel, grid_spec=pltpu.PrefetchScalarGri...  5.43 us
    ppermute x6, waiting for transfers between devices, to_chip(): lax.ppermute(value, 'aa', [(i, (i // 2 + distance) % 4 * 2 + i % 2) for i...  4.5 us
    ppermute x2, starting transfers between devices, to_other_core(): return lax.ppermute(value, 'aa', [(i, i ^ 1) for i in range(8)])  2.98 us
  transfers between devices with their start and end apart: 10, of which 5 were waited for; matrix products, arithmetic and copies ran while one was open for 0% of the time, Pallas kernels for 22%

profile of v6, /device:TPU:1, one launch (start us, length us, event | category | flops | bytes accessed | tf_op | source)
XLA Modules:
  0.0 61.8 jit_solution(7748135761088925172)
XLA Ops:
  0.6 2.3 %pack_rows.1 = (bf16[32,32,128]{2,1,0:T(8,128)(2,1)}, bf16[80,3,2,1288]{3,2,1,0:T(2,128)(2,1)S(1)}) custom-call(bf16[24,32,164]{2,1,0:T(8,128)(2,1)} %bitcast.25, bf16[80,3,2,1288]{3,2,1,0:T(2,128)(2,1)} %bitcast.23), custom_call_target="tpu_custom_call" | custom-call | bytes 800000 | tf_op jit(solution)/shard_map/pack_rows/pallas_call | solution.py:62
  2.9 12.0 %all-to-all-start = ((bf16[32,32,128]{2,1,0:T(8,128)(2,1)}), bf16[32,32,128]{2,1,0:T(8,128)(2,1)S(1)}, u32[]{:S(2)}, u32[]{:S(2)}) async-start(bf16[32,32,128]{2,1,0:T(8,128)(2,1)} %get-tuple-element.21), calls=%async_computation | async-start | bytes 524288 | tf_op jit(solution)/shard_map/all_to_all | solution.py:592
  15.0 0.0 copy-start.1
  15.0 5.4 %legendre_inverse.1 = bf16[4,2,48,256]{3,2,1,0:T(8,128)(2,1)S(1)} custom-call(s32[640]{0:T(1024)} %pw_ref.3, s32[1]{0:T(128)} %bitcast.me_ref, bf16[80,32,1288]{2,1,0:T(8,128)(2,1)} %leg_ref.5, bf16[80,3,2,1288]{3,2,1,0:T(2,128)(2,1)S(1)} %get-tuple-element.20.spec_ref), custom_call_target="tpu_custom_call" | custom-call | flops 211025920 | bytes 9000000 | tf_op jit(solution)/shard_map/legendre_inverse/pallas_call | solution.py:190
  20.4 0.0 copy-start
  20.5 2.6 %collective-permute-start.2 = (bf16[2,48,256]{2,1,0:T(8,128)(2,1)S(1)}, bf16[2,48,256]{2,1,0:T(8,128)(2,1)S(1)}, u32[]{:S(2)}, u32[]{:S(2)}) collective-permute-start(bf16[2,48,256]{2,1,0:T(8,128)(2,1)S(1)} %get-tuple-element.40), channel_id=1, source_target_pairs={{0,192},{32,224},{64,0},{96,32},{128,64},{160,96},{192,128},{224,1... | collective-permute-start | bytes 147464 | tf_op jit(solution)/shard_map/ppermute | solution.py:578
  23.0 0.5 collective-permute-start.1
  23.6 0.6 collective-permute-start
  24.2 0.1 stack_reshape.3
  24.3 1.9 %all-to-all-done.forcing_ref = bf16[32,32,128]{2,1,0:T(8,128)(2,1)S(1)} async-done(((bf16[32,32,128]{2,1,0:T(8,128)(2,1)}), bf16[32,32,128]{2,1,0:T(8,128)(2,1)S(1)}, u32[]{:S(2)}, u32[]{:S(2)}) %all-to-all-start) | async-done | bytes 262176 | tf_op jit(solution)/shard_map/all_to_all | solution.py:592
  26.2 2.5 %phase_tables.1 = (f32[4,2,32,1280]{3,2,1,0:T(8,128)S(1)}, bf16[4,176,2560]{2,1,0:T(8,128)(2,1)S(1)}, f32[8,1280]{1,0:T(8,128)S(1)}) custom-call(s32[1]{0:T(128)} %bitcast.me_ref, f32[8,2,128]{2,1,0:T(2,128)S(1)} %select_maximum_fusion.waves_ref), custom_call_target="tpu_custom_call" | custom-call | flops 40000000 | bytes 5000000 | tf_op jit(solution)/shard_map/phase_tables/pallas_call | solution.py:316
  28.8 2.5 %collective-permute-start.3 = (bf16[4,48,256]{2,1,0:T(8,128)(2,1)S(1)}, bf16[4,48,256]{2,1,0:T(8,128)(2,1)S(1)}, u32[]{:S(2)}, u32[]{:S(2)}) collective-permute-start(bf16[4,48,256]{2,1,0:T(8,128)(2,1)S(1)} %pad_maximum_fusion.1), channel_id=1, source_target_pairs={{0,32},{32,0},{64,96},{96,64},{128,160},{160,128},{192,224},{224,1... | collective-permute-start | bytes 294920 | tf_op jit(solution)/shard_map/ppermute | solution.py:582
  31.3 0.9 %collective-permute-done.3.got_ref = bf16[4,48,256]{2,1,0:T(8,128)(2,1)S(1)} collective-permute-done((bf16[4,48,256]{2,1,0:T(8,128)(2,1)S(1)}, bf16[4,48,256]{2,1,0:T(8,128)(2,1)S(1)}, u32[]{:S(2)}, u32[]{:S(2)}) %collective-permute-start.3) | collective-permute-done | bytes 98336 | tf_op jit(solution)/shard_map/ppermute | solution.py:582
  32.3 7.0 %transform_rows.1 = (bf16[32,32,128]{2,1,0:T(8,128)(2,1)}, bf16[4,48,256]{2,1,0:T(8,128)(2,1)S(1)}, bf16[4,48,256]{2,1,0:T(8,128)(2,1)S(1)}, bf16[20,32,1288]{2,1,0:T(8,128)(2,1)S(1)}) custom-call(s32[1]{0:T(128)} %bitcast.me_ref, f32[32]{0:T(128)S(1)} %copy-done, bf16[4,48,256]{2,1,0:T(8,128)(2,1)S(1)} %pad_maximum_fusion.kept_ref, ...), custom_call_target="tpu_custom_call" | custom-call | flops 1400000000 | bytes 6000000 | tf_op jit(solution)/shard_map/transform_rows/pallas_call | solution.py:448
  39.2 0.4 collective-permute-start.4
  39.7 8.7 %all-to-all-start.1 = ((bf16[32,32,128]{2,1,0:T(8,128)(2,1)}), bf16[32,32,128]{2,1,0:T(8,128)(2,1)S(1)}, u32[]{:S(2)}, u32[]{:S(2)}) async-start(bf16[32,32,128]{2,1,0:T(8,128)(2,1)} %get-tuple-element.34), calls=%async_computation.1 | async-start | bytes 524288 | tf_op jit(solution)/shard_map/all_to_all | solution.py:606
  48.5 0.4 collective-permute-start.5
  48.9 1.2 %collective-permute-start.6 = (bf16[2,48,256]{2,1,0:T(8,128)(2,1)S(1)}, bf16[2,48,256]{2,1,0:T(8,128)(2,1)S(1)}, u32[]{:S(2)}, u32[]{:S(2)}) collective-permute-start(bf16[2,48,256]{2,1,0:T(8,128)(2,1)S(1)} %pad_maximum_fusion.4), channel_id=1, source_target_pairs={{0,128},{32,160},{64,192},{96,224},{128,0},{160,32},{192,64},{224,... | collective-permute-start | bytes 147464 | tf_op jit(solution)/shard_map/ppermute | solution.py:578
  50.2 0.5 collective-permute-start.7
  50.6 0.8 %collective-permute-done.5.second_ref = bf16[2,48,256]{2,1,0:T(8,128)(2,1)S(1)} collective-permute-done((bf16[2,48,256]{2,1,0:T(8,128)(2,1)S(1)}, bf16[2,48,256]{2,1,0:T(8,128)(2,1)S(1)}, u32[]{:S(2)}, u32[]{:S(2)}) %collective-permute-start.5) | collective-permute-done | bytes 49184 | tf_op jit(solution)/shard_map/ppermute | solution.py:578
  51.5 2.2 %collective-permute-done.6.third_ref = bf16[2,48,256]{2,1,0:T(8,128)(2,1)S(1)} collective-permute-done((bf16[2,48,256]{2,1,0:T(8,128)(2,1)S(1)}, bf16[2,48,256]{2,1,0:T(8,128)(2,1)S(1)}, u32[]{:S(2)}, u32[]{:S(2)}) %collective-permute-start.6) | collective-permute-done | bytes 49184 | tf_op jit(solution)/shard_map/ppermute | solution.py:578
  53.7 1.5 %collective-permute-done.7.fourth_ref = bf16[2,48,256]{2,1,0:T(8,128)(2,1)S(1)} collective-permute-done((bf16[2,48,256]{2,1,0:T(8,128)(2,1)S(1)}, bf16[2,48,256]{2,1,0:T(8,128)(2,1)S(1)}, u32[]{:S(2)}, u32[]{:S(2)}) %collective-permute-start.7) | collective-permute-done | bytes 49184 | tf_op jit(solution)/shard_map/ppermute | solution.py:578
  55.1 5.7 %legendre_direct.1 = bf16[80,3,2,1288]{3,2,1,0:T(2,128)(2,1)} custom-call(s32[640]{0:T(1024)} %pw_ref.3, s32[1]{0:T(128)} %bitcast.me_ref, bf16[2,48,256]{2,1,0:T(8,128)(2,1)S(1)} %pad_maximum_fusion.2.first_ref, bf16[2,48,256]{2,1,0:T(8,128)(2,1)S(1)} %collective-permute-done.5.second_ref, bf16[2,48,256]{2,1,0:T(8,128)(2,1)S(1)} %collective-permute-done.6.third_ref, ...), custom_call_target="tpu_custom_call" | custom-call | flops 211025920 | bytes 9000000 | tf_op jit(solution)/shard_map/legendre_direct/pallas_call | solution.py:555
  60.9 0.9 %unpack_rows.1 = bf16[24,32,164]{2,1,0:T(8,128)(2,1)} custom-call(bf16[32,32,128]{2,1,0:T(8,128)(2,1)S(1)} %all-to-all-done.1.x_ref), custom_call_target="tpu_custom_call" | custom-call | bytes 800000 | tf_op jit(solution)/shard_map/unpack_rows/pallas_call | solution.py:100
  (21 shorter events, 0.2 us)
Async XLA Ops:
  2.9 23.2 %all-to-all-start = ((bf16[32,32,128]{2,1,0:T(8,128)(2,1)}), bf16[32,32,128]{2,1,0:T(8,128)(2,1)S(1)}, u32[]{:S(2)}, u32[]{:S(2)}) async-start(bf16[32,32,128]{2,1,0:T(8,128)(2,1)} %get-tuple-element.21), calls=%async_computation | async-start | bytes 524288 | tf_op jit(solution)/shard_map/all_to_all | solution.py:592
  15.0 9.2 %copy-start.1 = (s32[640]{0:T(1024)S(1)}, s32[640]{0:T(1024)}, u32[]{:S(2)}) copy-start(s32[640]{0:T(1024)} %pw_ref.3) | copy-start | bytes 7684
  20.4 11.8 %copy-start = (f32[32]{0:T(128)S(1)}, f32[32]{0:T(128)}, u32[]{:S(2)}) copy-start(f32[32]{0:T(128)} %weight_ref.1) | copy-start | bytes 388
  20.5 8.2 %collective-permute-start.2 = (bf16[2,48,256]{2,1,0:T(8,128)(2,1)S(1)}, bf16[2,48,256]{2,1,0:T(8,128)(2,1)S(1)}, u32[]{:S(2)}, u32[]{:S(2)}) collective-permute-start(bf16[2,48,256]{2,1,0:T(8,128)(2,1)S(1)} %get-tuple-element.40), channel_id=1, source_target_pairs={{0,192},{32,224},{64,0},{96,32},{128,64},{160,96},{192,128},{224,1... | collective-permute-start | bytes 147464 | tf_op jit(solution)/shard_map/ppermute | solution.py:578
  23.0 5.7 %collective-permute-start.1 = (bf16[2,48,256]{2,1,0:T(8,128)(2,1)S(1)}, bf16[2,48,256]{2,1,0:T(8,128)(2,1)S(1)}, u32[]{:S(2)}, u32[]{:S(2)}) collective-permute-start(bf16[2,48,256]{2,1,0:T(8,128)(2,1)S(1)} %get-tuple-element.41), channel_id=1, source_target_pairs={{0,128},{32,160},{64,192},{96,224},{128,0},{160,32},{192,64},{224,... | collective-permute-start | bytes 147464 | tf_op jit(solution)/shard_map/ppermute | solution.py:578
  23.6 5.2 %collective-permute-start = (bf16[2,48,256]{2,1,0:T(8,128)(2,1)S(1)}, bf16[2,48,256]{2,1,0:T(8,128)(2,1)S(1)}, u32[]{:S(2)}, u32[]{:S(2)}) collective-permute-start(bf16[2,48,256]{2,1,0:T(8,128)(2,1)S(1)} %get-tuple-element.42), channel_id=1, source_target_pairs={{0,64},{32,96},{64,128},{96,160},{128,192},{160,224},{192,0},{224,... | collective-permute-start | bytes 147464 | tf_op jit(solution)/shard_map/ppermute | solution.py:578
  28.8 3.5 %collective-permute-start.3 = (bf16[4,48,256]{2,1,0:T(8,128)(2,1)S(1)}, bf16[4,48,256]{2,1,0:T(8,128)(2,1)S(1)}, u32[]{:S(2)}, u32[]{:S(2)}) collective-permute-start(bf16[4,48,256]{2,1,0:T(8,128)(2,1)S(1)} %pad_maximum_fusion.1), channel_id=1, source_target_pairs={{0,32},{32,0},{64,96},{96,64},{128,160},{160,128},{192,224},{224,1... | collective-permute-start | bytes 294920 | tf_op jit(solution)/shard_map/ppermute | solution.py:582
  39.2 9.2 %collective-permute-start.4 = (bf16[4,48,256]{2,1,0:T(8,128)(2,1)S(1)}, bf16[4,48,256]{2,1,0:T(8,128)(2,1)S(1)}, u32[]{:S(2)}, u32[]{:S(2)}) collective-permute-start(bf16[4,48,256]{2,1,0:T(8,128)(2,1)S(1)} %get-tuple-element.36), channel_id=1, source_target_pairs={{0,32},{32,0},{64,96},{96,64},{128,160},{160,128},{192,224},{224,1... | collective-permute-start | bytes 294920 | tf_op jit(solution)/shard_map/ppermute | solution.py:582
  39.7 21.2 %all-to-all-start.1 = ((bf16[32,32,128]{2,1,0:T(8,128)(2,1)}), bf16[32,32,128]{2,1,0:T(8,128)(2,1)S(1)}, u32[]{:S(2)}, u32[]{:S(2)}) async-start(bf16[32,32,128]{2,1,0:T(8,128)(2,1)} %get-tuple-element.34), calls=%async_computation.1 | async-start | bytes 524288 | tf_op jit(solution)/shard_map/all_to_all | solution.py:606
  48.5 3.0 %collective-permute-start.5 = (bf16[2,48,256]{2,1,0:T(8,128)(2,1)S(1)}, bf16[2,48,256]{2,1,0:T(8,128)(2,1)S(1)}, u32[]{:S(2)}, u32[]{:S(2)}) collective-permute-start(bf16[2,48,256]{2,1,0:T(8,128)(2,1)S(1)} %pad_maximum_fusion.3), channel_id=1, source_target_pairs={{0,192},{32,224},{64,0},{96,32},{128,64},{160,96},{192,128},{224,1... | collective-permute-start | bytes 147464 | tf_op jit(solution)/shard_map/ppermute | solution.py:578
  48.9 4.7 %collective-permute-start.6 = (bf16[2,48,256]{2,1,0:T(8,128)(2,1)S(1)}, bf16[2,48,256]{2,1,0:T(8,128)(2,1)S(1)}, u32[]{:S(2)}, u32[]{:S(2)}) collective-permute-start(bf16[2,48,256]{2,1,0:T(8,128)(2,1)S(1)} %pad_maximum_fusion.4), channel_id=1, source_target_pairs={{0,128},{32,160},{64,192},{96,224},{128,0},{160,32},{192,64},{224,... | collective-permute-start | bytes 147464 | tf_op jit(solution)/shard_map/ppermute | solution.py:578
  50.2 5.0 %collective-permute-start.7 = (bf16[2,48,256]{2,1,0:T(8,128)(2,1)S(1)}, bf16[2,48,256]{2,1,0:T(8,128)(2,1)S(1)}, u32[]{:S(2)}, u32[]{:S(2)}) collective-permute-start(bf16[2,48,256]{2,1,0:T(8,128)(2,1)S(1)} %pad_maximum_fusion.5), channel_id=1, source_target_pairs={{0,64},{32,96},{64,128},{96,160},{128,192},{160,224},{192,0},{224,... | collective-permute-start | bytes 147464 | tf_op jit(solution)/shard_map/ppermute | solution.py:578
